TPU v7x, 512 devices: a whole 4x4x16 slice. The times are simulated.
512 devices in a mesh: grp: 16 (over y, x), tok: 32 (over z, core).
Axes of the slice: x: 4, y: 4, z: 16, core: 2. Of those that a mesh axis runs over, the one named last changes fastest.
Arguments:
- hidden_in: bfloat16 [16, 4096, 1024], P('grp', 'tok'), may hold values from -6 to 6
- lengths: int32 [16, 3], P('grp'), may hold values from 1 to 3072, 4096 in all within a row
- prefix_cache: bfloat16 [16, 512, 512], P('grp', 'tok'), may hold values from -2600 to 2600
- routes: int32 [16, 4096, 8], P('grp', 'tok'), may hold values from 0 to 31, all different within a row; in each aligned block of 128 rows (0 to 127, 128 to 255, ..., all dimensions but the last counted through in order) at most 40 rows name the same one
- gates: float32 [16, 4096, 8], P('grp', 'tok'), may hold values from 0.05 to 0.4
- attn_gain: float32 [1024], replicated, may hold values from 0.1 to 1.9
- w_qkv: bfloat16 [1024, 1024], P('grp', 'tok'), may hold values from -0.75 to 0.75
- w_out: bfloat16 [512, 1024], P('grp', 'tok'), may hold values from -0.25 to 0.25
- moe_gain: float32 [1024], replicated, may hold values from 0.1 to 1.9
- expert_gate_up: bfloat16 [32, 1024, 1024], P('tok', 'grp'), may hold values from -0.1875 to 0.1875
- expert_down: bfloat16 [32, 512, 1024], P('tok', 'grp'), may hold values from -0.25 to 0.25
Outputs:
- hidden_out: bfloat16 [16, 4096, 1024], P('grp', 'tok')
- suffix_cache: bfloat16 [16, 4096, 512], P('grp', 'tok')
Inputs may be any that keep to these rules, and one draw needn't show every extreme that they name: Each group's 3 lengths sum to 4096; no request is longer than 3072 tokens, and some request of every draw has exactly 3072. `routes`: each token names 8 different experts. Among the 128 tokens of one device no expert is named more than 40 times, a bound that some block reaches.
All inputs are finite; a program needn't handle non-finite values.
Results may differ from a plain program's by a relative error of at most 0.02.
Values may be sent and summed in bfloat16 or wider, within the bound.
A program may use at most 128 MiB of HBM per device.

v0:
```python
import jax
import jax.numpy as jnp
from jax import lax
from jax.sharding import PartitionSpec as P

HEADS = 8
KV_HEADS = 4
HEAD_DIM = 64
FF = 512
EXPERTS = 32
TOP = 8
CAP = 40


epsilon = 1e-05
score_scale = 0.015625
rope_base = 10000.0
big_negative = -1e30


def rms_scale(values, gain):
    values = values.astype(jnp.float32)
    mean_square = jnp.mean(values * values, axis=-1, keepdims=True)
    return values * lax.rsqrt(mean_square + epsilon) * gain


def request_layout(group_lengths, token_index):
    ends = jnp.cumsum(group_lengths)
    starts = ends - group_lengths
    segment = jnp.sum((token_index[:, None] >= ends[None, :]).astype(jnp.int32), axis=1)
    match = segment[:, None] == jnp.arange(group_lengths.shape[0], dtype=jnp.int32)[None, :]
    offset = token_index - jnp.sum(jnp.where(match, starts[None, :], 0), axis=1)
    return (segment, offset)


def rotate(values, position):
    half_width = values.shape[-1] // 2
    frequency = rope_base ** (-jnp.arange(half_width, dtype=jnp.float32) * 2.0 / values.shape[-1])
    angle = position.astype(jnp.float32)[:, None] * frequency[None, :]
    cosine = jnp.cos(angle)[:, None, :]
    sine = jnp.sin(angle)[:, None, :]
    first = values[..., :half_width]
    second = values[..., half_width:]
    return jnp.concatenate(
        [first * cosine - second * sine, second * cosine + first * sine], axis=-1
    )


def attend(carry, grouped, keys_values, allowed):
    best, total, mixed = carry
    key_count = keys_values.shape[0]
    key_width = KV_HEADS * HEAD_DIM
    key_heads = keys_values[:, :key_width].reshape(key_count, KV_HEADS, HEAD_DIM).transpose(1, 0, 2)
    value_heads = (
        keys_values[:, key_width:].reshape(key_count, KV_HEADS, HEAD_DIM).transpose(1, 0, 2)
    )
    scores = (
        jnp.einsum("kqd,knd->kqn", grouped, key_heads, preferred_element_type=jnp.float32)
        * score_scale
    )
    if allowed is not None:
        row_count = grouped.shape[1]
        share = row_count // allowed.shape[0]
        mask = jnp.broadcast_to(allowed[:, None, :], (allowed.shape[0], share, key_count)).reshape(
            row_count, key_count
        )
        scores = jnp.where(mask[None], scores, big_negative)
    new_best = jnp.maximum(best, jnp.max(scores, axis=-1))
    factor = jnp.exp(best - new_best)
    probs = jnp.exp(scores - new_best[..., None])
    total = total * factor + jnp.sum(probs, axis=-1)
    mixed = mixed * factor[..., None] + jnp.einsum(
        "kqn,knd->kqd", probs.astype(jnp.bfloat16), value_heads, preferred_element_type=jnp.float32
    )
    return (new_best, total, mixed)


def local(
    hidden_in,
    lengths,
    prefix_cache,
    routes,
    gates,
    attn_gain,
    w_qkv,
    w_out,
    moe_gain,
    expert_gate_up,
    expert_down,
):
    tokens_here = hidden_in[0]
    tok_count = tokens_here.shape[0]
    axis_count = lax.axis_size("tok")
    device_place = lax.axis_index("tok")
    group_lengths = lengths[0]
    token_index = device_place * tok_count + jnp.arange(tok_count, dtype=jnp.int32)
    segment, offset = request_layout(group_lengths, token_index)
    position = prefix_cache.shape[1] * axis_count + offset
    query_width = HEADS * HEAD_DIM
    key_width = KV_HEADS * HEAD_DIM
    group_share = HEADS // KV_HEADS
    normed = rms_scale(tokens_here, attn_gain).astype(jnp.bfloat16)
    columns = lax.all_gather(w_qkv, "tok", axis=1, tiled=True)
    sliced = normed
    projected = jnp.dot(
        sliced,
        lax.all_gather(columns, "grp", axis=0, tiled=True),
        preferred_element_type=jnp.float32,
    )
    query = rotate(projected[:, :query_width].reshape(tok_count, HEADS, HEAD_DIM), position).astype(
        jnp.bfloat16
    )
    keys_new = rotate(
        projected[:, query_width : query_width + key_width].reshape(tok_count, KV_HEADS, HEAD_DIM),
        position,
    ).astype(jnp.bfloat16)
    values_new = projected[:, query_width + key_width :].astype(jnp.bfloat16)
    suffix_cache = jnp.concatenate([keys_new.reshape(tok_count, key_width), values_new], axis=1)
    row_count = tok_count * group_share
    grouped = (
        query.reshape(tok_count, KV_HEADS, group_share, HEAD_DIM)
        .transpose(1, 0, 2, 3)
        .reshape(KV_HEADS, row_count, HEAD_DIM)
    )
    start_carry = (
        jnp.full((KV_HEADS, row_count), big_negative, jnp.float32),
        jnp.zeros((KV_HEADS, row_count), jnp.float32),
        jnp.zeros((KV_HEADS, row_count, HEAD_DIM), jnp.float32),
    )
    carry = attend(
        start_carry, grouped, lax.all_gather(prefix_cache[0], "tok", axis=0, tiled=True), None
    )
    piece = lax.all_gather(suffix_cache, "tok", axis=0, tiled=True)
    key_index = jnp.arange(piece.shape[0], dtype=jnp.int32)
    key_segment, key_offset = request_layout(group_lengths, key_index)
    earlier = key_index[None, :] <= token_index[:, None]
    same_request = key_segment[None, :] == segment[:, None]
    carry = attend(carry, grouped, piece, earlier & same_request & (key_index[None, :] >= 0))
    best, total, mixed = carry
    attended = (mixed / total[..., None]).reshape(KV_HEADS, tok_count, group_share, HEAD_DIM)
    attended = attended.transpose(1, 0, 2, 3).reshape(tok_count, query_width).astype(jnp.bfloat16)
    out_columns = lax.all_gather(w_out, "tok", axis=1, tiled=True)
    sliced = attended
    projected_out = jnp.dot(
        sliced,
        lax.all_gather(out_columns, "grp", axis=0, tiled=True),
        preferred_element_type=jnp.float32,
    )
    after_attention = tokens_here.astype(jnp.float32) + projected_out
    moe_in = rms_scale(after_attention, moe_gain).astype(jnp.bfloat16)
    model_width = moe_in.shape[1]
    flat_routes = routes[0].reshape(-1)
    onehot = (flat_routes[:, None] == jnp.arange(EXPERTS, dtype=jnp.int32)[None, :]).astype(
        jnp.int32
    )
    slot_rank = jnp.sum(jnp.cumsum(onehot, axis=0) * onehot, axis=1) - 1
    slot_index = flat_routes * CAP + slot_rank
    source_token = jnp.arange(flat_routes.shape[0], dtype=jnp.int32) // TOP
    outgoing = (
        jnp.zeros((EXPERTS * CAP, model_width), jnp.bfloat16)
        .at[slot_index]
        .set(moe_in[source_token])
    )
    arrived = lax.all_to_all(
        outgoing.reshape(EXPERTS, CAP, model_width), "tok", split_axis=0, concat_axis=1, tiled=True
    )
    sliced = arrived
    hidden_pair = jnp.einsum(
        "erd,edf->erf",
        sliced,
        lax.all_gather(expert_gate_up, "grp", axis=1, tiled=True),
        preferred_element_type=jnp.float32,
    )
    activated = (jax.nn.silu(hidden_pair[..., :FF]) * hidden_pair[..., FF:]).astype(jnp.bfloat16)
    sliced = activated
    expert_result = jnp.einsum(
        "erf,efd->erd",
        sliced,
        lax.all_gather(expert_down, "grp", axis=1, tiled=True),
        preferred_element_type=jnp.float32,
    ).astype(jnp.bfloat16)
    returned = lax.all_to_all(
        expert_result, "tok", split_axis=1, concat_axis=0, tiled=True
    ).reshape(EXPERTS * CAP, -1)
    weighted = returned[slot_index].astype(jnp.float32) * gates[0].reshape(-1)[:, None]
    moe_out = jnp.sum(weighted.reshape(tok_count, TOP, -1), axis=1)
    hidden_out = (after_attention + moe_out).astype(jnp.bfloat16)
    return (hidden_out[None], suffix_cache[None])


def solution(mesh):
    return jax.shard_map(
        local,
        mesh=mesh,
        in_specs=(
            P("grp", "tok", None),
            P("grp", None),
            P("grp", "tok", None),
            P("grp", "tok", None),
            P("grp", "tok", None),
            P(),
            P("grp", "tok"),
            P("grp", "tok"),
            P(),
            P("tok", "grp", None),
            P("tok", "grp", None),
        ),
        out_specs=(P("grp", "tok", None), P("grp", "tok", None)),
        check_vma=False,
    )
```

profile of v0, /device:TPU:1, one launch (start us, length us, event | category | flops | bytes accessed | tf_op | source)
XLA Modules:
  0.0 591.6 jit_solution(6562197188762396571)
XLA Ops:
  7.2 38.5 %all_gather.24 = bf16[64,1024]{0,1:T(8,128)(2,1)S(1)} all-gather(bf16[64,32]{0,1:T(8,128)(2,1)} %param.17), channel_id=1, replica_groups=mesh['grp'=16,'tok'=32] {'tok'}, dimensions={1}, use_global_device_ids=true | all-gather | bytes 135168 | tf_op jit(solution)/shard_map/all_gather | solution.py:103
  45.8 0.8 copy.106
  46.6 0.8 reduce-window.10
  47.6 0.7 fusion.38
  48.3 1.1 fusion.26
  49.6 52.1 %all-gather.7.cloned.1.call-done = bf16[1024,1024]{1,0:T(8,128)(2,1)} async-done(((bf16[64,1024]{1,0:T(8,128)(2,1)}), bf16[1024,1024]{1,0:T(8,128)(2,1)}) %all-gather.7.cloned.1.call-update) | async-done | bytes 2097168 | tf_op jit(solution)/shard_map/all_gather | solution.py:107
  101.6 2.2 fusion.30
  103.9 0.8 copy-done.3
  104.9 0.7 fusion.44
  105.8 33.3 %all_gather.28 = bf16[32,1024]{0,1:T(8,128)(2,1)S(1)} all-gather(bf16[32,32]{0,1:T(8,128)(2,1)S(1)} %copy.120), channel_id=1, replica_groups=mesh['grp'=16,'tok'=32] {'tok'}, dimensions={1}, use_global_device_ids=true | all-gather | bytes 67584 | tf_op jit(solution)/shard_map/all_gather | solution.py:142
  139.1 0.7 copy.121
  140.8 2.4 broadcast_in_dim.41
  143.2 2.6 broadcast_in_dim.42
  145.8 30.3 %all-gather = bf16[1,512,512]{2,1,0:T(8,128)(2,1)S(1)} all-gather(bf16[1,16,512]{2,1,0:T(8,128)(2,1)S(1)} %copy-done.5), channel_id=2, replica_groups=mesh['grp'=16,'tok'=32] {'tok'}, dimensions={1}, use_global_device_ids=true | all-gather | bytes 540672 | tf_op jit(solution)/shard_map/all_gather | solution.py:131
  176.3 0.9 copy.112
  177.3 9.2 %reduce-window.11 = s32[32,8,128]{2,1,0:T(8,128)S(1)} reduce-window(s32[32,8,128]{2,1,0:T(8,128)S(1)} %fusion.37, s32[]{:T(128)} %constant.34.clone.1), window={size=1x1x128 pad=0_0x0_0x127_0}, to_apply=%region_9.10 | reduce-window | flops 4161536 | bytes 262148 | tf_op jit(solution)/shard_map/reduce-window.1
  187.6 0.7 pad_maximum_fusion
  188.3 1.8 multiply_reduce_fusion
  190.1 3.8 fusion.45
  193.9 2.9 copy.117
  196.9 2.9 copy.115
  199.8 3.5 fusion
  203.3 4.4 fusion.1
  207.7 1.9 copy-done
  209.6 0.5 fusion.13
  210.2 11.2 %fusion.3 = f32[4,256,64]{1,2,0:T(8,128)} fusion(bf16[4,4096,64]{1,2,0:T(8,128)(2,1)} %bitcast.105, f32[4,256,4096]{2,1,0:T(8,128)} %copy-done, f32[4,256]{1,0:T(4,128)S(1)} %get-tuple-element.15, pred[256,4096]{1,0:T(8,128)(4,1)S(1)} %broadcast_in_dim.42), kind=kOutput, calls=%fused_computation.8 | convolution fusion | flops 553648128 | bytes 20189184 | tf_op jit(solution)/shard_map/kqn,knd->kqd/dot_general | solution.py:72
  221.4 1.6 fusion.21
  223.3 14.0 %all-gather.11.cloned.1.call-done = bf16[512,1024]{1,0:T(8,128)(2,1)} async-done(((bf16[32,1024]{1,0:T(8,128)(2,1)}), bf16[512,1024]{1,0:T(8,128)(2,1)}) %all-gather.11.cloned.1.call-update) | async-done | bytes 1048592 | tf_op jit(solution)/shard_map/all_gather | solution.py:146
  237.3 1.6 multiply_reduce_fusion.1
  239.1 14.7 %scatter_custom_fusion = bf16[1280,1024]{1,0:T(8,128)(2,1)} fusion(s32[1024]{0:T(1024)S(1)} %bitcast.118, bf16[128,1024]{1,0:T(8,128)(2,1)S(1)} %multiply_convert_fusion, s32[1024]{0:T(1024)S(1)} %broadcast_clamp_fusion.1, bf16[]{:T(256)} %constant.67.clone.1), kind=kCustom, calls=%fused_computation.19 | custom fusion | bytes 2621442 | tf_op jit(solution)/shard_map/scatter | solution.py:162
  253.8 14.4 %all-to-all-start = ((bf16[32,40,1024]{2,1,0:T(8,128)(2,1)}), bf16[32,40,1024]{2,1,0:T(8,128)(2,1)S(1)}, u32[]{:S(2)}, u32[]{:S(2)}) async-start(bf16[32,40,1024]{2,1,0:T(8,128)(2,1)} %bitcast.31), calls=%async_computation | async-start | bytes 5242880 | tf_op jit(solution)/shard_map/all_to_all | solution.py:164
  268.3 0.5 all-gather.13.cloned.1.call-update
  268.9 0.5 all-gather.15.cloned.1.call-update
  269.4 60.3 %all-gather.13.cloned.1.call-done = bf16[1,1024,1024]{2,1,0:T(8,128)(2,1)} async-done(((bf16[1,64,1024]{2,1,0:T(8,128)(2,1)}), bf16[1,1024,1024]{2,1,0:T(8,128)(2,1)}) %all-gather.13.cloned.1.call-update) | async-done | bytes 2097168 | tf_op jit(solution)/shard_map/all_gather | solution.py:171
  329.8 58.1 %all-to-all-done = bf16[32,40,1024]{2,1,0:T(8,128)(2,1)S(1)} async-done(((bf16[32,40,1024]{2,1,0:T(8,128)(2,1)}), bf16[32,40,1024]{2,1,0:T(8,128)(2,1)S(1)}, u32[]{:S(2)}, u32[]{:S(2)}) %all-to-all-start) | async-done | bytes 2621472 | tf_op jit(solution)/shard_map/all_to_all | solution.py:164
  387.8 6.2 %convolution_bitcast_fusion = f32[1,1280,1024]{2,1,0:T(8,128)} fusion(bf16[1280,1024]{1,0:T(8,128)(2,1)S(1)} %bitcast.104, bf16[1,1024,1024]{2,1,0:T(8,128)(2,1)} %all-gather.13.cloned.1.call-done), kind=kOutput, calls=%fused_computation.10 | convolution fusion | flops 2684354560 | bytes 9961472 | tf_op jit(solution)/shard_map/erd,edf->erf/dot_general | solution.py:168
  394.0 4.4 fusion.7
  398.4 18.2 %copy.137 = bf16[1,1280,1024]{2,0,1:T(2,128)(2,1)} copy(bf16[1,1280,1024]{2,1,0:T(8,128)(2,1)S(1)} %fusion.7) | data formatting | bytes 5242880 | tf_op jit(solution)/shard_map/convert_element_type | solution.py:181
  416.6 0.5 broadcast.297
  417.1 15.6 %reduce = bf16[1280,1024]{1,0:T(8,128)(2,1)S(1)} reduce(bf16[1280,1,1024]{2,1,0:T(2,128)(2,1)} %bitcast.99, bf16[]{:T(256)} %broadcast.297), dimensions={1}, to_apply=%bitcast.97.reduce_sub_computation | reduce | bytes 5242882
  432.7 3.0 reshape.386
  435.7 10.1 %all-to-all-start.1 = ((bf16[32,2,20480]{2,1,0:T(2,128)(2,1)}), bf16[32,2,20480]{2,1,0:T(2,128)(2,1)S(1)}, u32[]{:S(2)}, u32[]{:S(2)}) async-start(bf16[32,2,20480]{2,1,0:T(2,128)(2,1)} %reshape.386), calls=%async_computation.1 | async-start | bytes 5242880 | tf_op jit(solution)/shard_map/all_to_all | solution.py:182
  445.9 119.5 %all-to-all-done.1 = bf16[32,2,20480]{2,1,0:T(2,128)(2,1)S(1)} async-done(((bf16[32,2,20480]{2,1,0:T(2,128)(2,1)}), bf16[32,2,20480]{2,1,0:T(2,128)(2,1)S(1)}, u32[]{:S(2)}, u32[]{:S(2)}) %all-to-all-start.1) | async-done | bytes 2621472 | tf_op jit(solution)/shard_map/all_to_all | solution.py:182
  565.3 7.2 %reshape.387 = bf16[1280,1,1024]{2,1,0:T(2,128)(2,1)} reshape(bf16[32,2,20480]{2,1,0:T(2,128)(2,1)S(1)} %all-to-all-done.1) | data formatting | bytes 5242880
  572.5 3.5 copy.136
  576.0 5.4 gather_fusion
  581.4 2.9 fusion.6
  584.3 0.8 fusion.29
  (78 shorter events, 3.8 us)
Async XLA Ops:
  7.2 94.5 %all-gather.7.cloned.1.call-start = ((), (), s32[]{:S(2)}) async-start(), calls=%async_computation.2 | async-start | bytes 2228224 | tf_op jit(solution)/shard_map/all_gather | solution.py:107
  45.8 59.9 %copy-start.7 = (bf16[32,32]{1,0:T(8,128)(2,1)S(1)}, bf16[32,32]{1,0:T(8,128)(2,1)}, u32[]{:S(2)}) copy-start(bf16[32,32]{1,0:T(8,128)(2,1)} %param.18) | copy-start | bytes 6148
  46.6 143.5 %all-gather.9.cloned.1.call-start = ((), (), s32[]{:S(2)}) async-start(), calls=%async_computation.3 | async-start | bytes 4325376 | tf_op jit(solution)/shard_map/all_gather | solution.py:133
  49.5 90.4 %copy-start.6 = (s32[1,128,8]{1,2,0:T(8,128)S(1)}, s32[1,128,8]{1,2,0:T(8,128)}, u32[]{:S(2)}) copy-start(s32[1,128,8]{1,2,0:T(8,128)} %param.14) | copy-start | bytes 12292
  103.8 0.8 copy-start.3
  105.6 131.7 %all-gather.11.cloned.1.call-start = ((), (), s32[]{:S(2)}) async-start(), calls=%async_computation.4 | async-start | bytes 1114112 | tf_op jit(solution)/shard_map/all_gather | solution.py:146
  140.8 5.0 copy-start.5
  145.8 41.3 %slice-start = ((f32[128,1024]{1,0:T(8,128)}), f32[128,512]{1,0:T(8,128)S(1)}, s32[]{:S(2)}) async-start(f32[128,1024]{1,0:T(8,128)} %copy-done.3), calls=%async_computation.7 | async-start | bytes 524288 | tf_op jit(solution)/shard_map/slice | solution.py:110
  203.3 6.3 %copy-start = (f32[4,256,4096]{2,1,0:T(8,128)}, f32[4,256,4096]{2,1,0:T(8,128)S(1)}, u32[]{:S(2)}) copy-start(f32[4,256,4096]{2,1,0:T(8,128)S(1)} %get-tuple-element.22) | copy-start | bytes 50331652
  203.3 6.3 %copy-start.1 = (f32[4,256,512]{2,1,0:T(8,128)S(1)}, f32[4,256,512]{2,1,0:T(8,128)}, u32[]{:S(2)}) copy-start(f32[4,256,512]{2,1,0:T(8,128)} %get-tuple-element.20) | copy-start | bytes 6291460
  210.2 11.2 %copy-start.4 = (bf16[512,256]{0,1:T(8,128)(2,1)S(1)}, bf16[512,256]{0,1:T(8,128)(2,1)}, u32[]{:S(2)}) copy-start(bf16[512,256]{0,1:T(8,128)(2,1)} %copy.112) | copy-start | bytes 786436
  221.4 15.9 %copy-start.2 = (bf16[1,128,1024]{2,1,0:T(8,128)(2,1)S(1)}, bf16[1,128,1024]{2,1,0:T(8,128)(2,1)}, u32[]{:S(2)}) copy-start(bf16[1,128,1024]{2,1,0:T(8,128)(2,1)} %param.11) | copy-start | bytes 786436
  221.4 17.6 %copy-start.8 = (f32[1024]{0:T(1024)S(1)}, f32[1024]{0:T(1024)}, u32[]{:S(2)}) copy-start(f32[1024]{0:T(1024)} %param.19) | copy-start | bytes 12292
  253.8 134.0 %all-to-all-start = ((bf16[32,40,1024]{2,1,0:T(8,128)(2,1)}), bf16[32,40,1024]{2,1,0:T(8,128)(2,1)S(1)}, u32[]{:S(2)}, u32[]{:S(2)}) async-start(bf16[32,40,1024]{2,1,0:T(8,128)(2,1)} %bitcast.31), calls=%async_computation | async-start | bytes 5242880 | tf_op jit(solution)/shard_map/all_to_all | solution.py:164
  268.3 61.5 %all-gather.13.cloned.1.call-start = ((), (), s32[]{:S(2)}) async-start(), calls=%async_computation.5 | async-start | bytes 2228224 | tf_op jit(solution)/shard_map/all_gather | solution.py:171
  268.8 125.2 %all-gather.15.cloned.1.call-start = ((), (), s32[]{:S(2)}) async-start(), calls=%async_computation.6 | async-start | bytes 1114112 | tf_op jit(solution)/shard_map/all_gather | solution.py:179
  435.6 10.1 %copy-start.9 = (f32[1,128,8]{1,2,0:T(8,128)S(1)}, f32[1,128,8]{1,2,0:T(8,128)}, u32[]{:S(2)}) copy-start(f32[1,128,8]{1,2,0:T(8,128)} %param.15) | copy-start | bytes 12292
  435.7 129.7 %all-to-all-start.1 = ((bf16[32,2,20480]{2,1,0:T(2,128)(2,1)}), bf16[32,2,20480]{2,1,0:T(2,128)(2,1)S(1)}, u32[]{:S(2)}, u32[]{:S(2)}) async-start(bf16[32,2,20480]{2,1,0:T(2,128)(2,1)} %reshape.386), calls=%async_computation.1 | async-start | bytes 5242880 | tf_op jit(solution)/shard_map/all_to_all | solution.py:182
Sparse Core Ops, SparseCore 0:
  46.7 54.9 all-gather.6
  105.8 75.6 all-gather.8
  184.5 52.7 all-gather.10
  271.8 57.9 all-gather.12
  332.6 56.8 all-gather.14
where the time goes:
time: 594 us; the launch traced here: 592 us
  waiting for transfers between devices  305 us (51%)
  blocking collectives  102 us (17%)
  local copies, waits for them, and re-layouts  74.3 us (13%)
  other arithmetic  38.8 us (7%)
  matrix products  32.4 us (5%)
  starting transfers between devices  24.7 us (4%)
  between operations  14.2 us (2%)
    all_to_all x1, waiting for transfers between devices, local(): lax.all_to_all(expert_result, 'tok', split_axis=1, concat_axis=0, tiled=T...  119 us
    all_gather x1, waiting for transfers between devices, local(): lax.all_gather(expert_gate_up, 'grp', axis=1, tiled=True)  60.3 us
    all_to_all x1, waiting for transfers between devices, local(): lax.all_to_all(outgoing.reshape(EXPERTS, CAP, model_width), 'tok', split_...  58.1 us
    all_gather x1, waiting for transfers between devices, local(): lax.all_gather(columns, 'grp', axis=0, tiled=True)  52.1 us
    all_gather x1, blocking collectives, local(): columns = lax.all_gather(w_qkv, 'tok', axis=1, tiled=True)  38.5 us
    all_gather x1, blocking collectives, local(): out_columns = lax.all_gather(w_out, 'tok', axis=1, tiled=True)  33.3 us
    all_gather x1, blocking collectives, local(): lax.all_gather(prefix_cache[0], 'tok', axis=0, tiled=True)  30.3 us
    convert_element_type x1, local copies, waits for them, and re-layouts, local(): expert_result = jnp.einsum('erf,efd->erd', sliced, lax.all_gather(expert_...  18.2 us
  transfers between devices with their start and end apart: 7, of which 5 were waited for; matrix products, arithmetic and copies ran while one was open for 10% of the time, Pallas kernels for 0%

commit v1 on v0

--- a/solution.py
+++ b/solution.py
@@ -44,6 +44,21 @@
     return jnp.concatenate(
         [first * cosine - second * sine, second * cosine + first * sine], axis=-1
     )
+
+
+def gather_small(blocks):
+    flat = jnp.concatenate([b.reshape(-1) for b in blocks])
+    gathered = lax.all_gather(flat[None], "tok", axis=0, tiled=True)
+    pieces, start = [], 0
+    for b in blocks:
+        size = b.size
+        pieces.append(gathered[:, start : start + size].reshape((-1,) + b.shape[1:]))
+        start += size
+    return pieces
+
+
+def gather_rows(by_columns):
+    return lax.all_gather(by_columns[None], "grp", axis=0, tiled=True)
 
 
 def attend(carry, grouped, keys_values, allowed):
@@ -100,11 +115,12 @@
     key_width = KV_HEADS * HEAD_DIM
     group_share = HEADS // KV_HEADS
     normed = rms_scale(tokens_here, attn_gain).astype(jnp.bfloat16)
-    columns = lax.all_gather(w_qkv, "tok", axis=1, tiled=True)
-    sliced = normed
-    projected = jnp.dot(
-        sliced,
-        lax.all_gather(columns, "grp", axis=0, tiled=True),
+    qkv_columns, out_columns, prefix_all = gather_small([w_qkv.T, w_out.T, prefix_cache[0]])
+    qkv_weight = gather_rows(qkv_columns)
+    projected = jnp.einsum(
+        "ngr,gcr->nc",
+        normed.reshape(tok_count, qkv_weight.shape[0], qkv_weight.shape[2]),
+        qkv_weight,
         preferred_element_type=jnp.float32,
     )
     query = rotate(projected[:, :query_width].reshape(tok_count, HEADS, HEAD_DIM), position).astype(
@@ -128,7 +144,7 @@
         jnp.zeros((KV_HEADS, row_count, HEAD_DIM), jnp.float32),
     )
     carry = attend(
-        start_carry, grouped, lax.all_gather(prefix_cache[0], "tok", axis=0, tiled=True), None
+        start_carry, grouped, prefix_all, None
     )
     piece = lax.all_gather(suffix_cache, "tok", axis=0, tiled=True)
     key_index = jnp.arange(piece.shape[0], dtype=jnp.int32)
@@ -139,11 +155,11 @@
     best, total, mixed = carry
     attended = (mixed / total[..., None]).reshape(KV_HEADS, tok_count, group_share, HEAD_DIM)
     attended = attended.transpose(1, 0, 2, 3).reshape(tok_count, query_width).astype(jnp.bfloat16)
-    out_columns = lax.all_gather(w_out, "tok", axis=1, tiled=True)
-    sliced = attended
-    projected_out = jnp.dot(
-        sliced,
-        lax.all_gather(out_columns, "grp", axis=0, tiled=True),
+    out_weight = gather_rows(out_columns)
+    projected_out = jnp.einsum(
+        "ngr,gcr->nc",
+        attended.reshape(tok_count, out_weight.shape[0], out_weight.shape[2]),
+        out_weight,
         preferred_element_type=jnp.float32,
     )
     after_attention = tokens_here.astype(jnp.float32) + projected_out
@@ -162,8 +178,8 @@
         .set(moe_in[source_token])
     )
     arrived = lax.all_to_all(
-        outgoing.reshape(EXPERTS, CAP, model_width), "tok", split_axis=0, concat_axis=1, tiled=True
-    )
+        outgoing.reshape(EXPERTS, CAP, model_width), "tok", split_axis=0, concat_axis=0, tiled=True
+    ).reshape(1, EXPERTS * CAP, model_width)
     sliced = arrived
     hidden_pair = jnp.einsum(
         "erd,edf->erf",
@@ -180,7 +196,7 @@
         preferred_element_type=jnp.float32,
     ).astype(jnp.bfloat16)
     returned = lax.all_to_all(
-        expert_result, "tok", split_axis=1, concat_axis=0, tiled=True
+        expert_result.reshape(EXPERTS, CAP, model_width), "tok", split_axis=0, concat_axis=0, tiled=True
     ).reshape(EXPERTS * CAP, -1)
     weighted = returned[slot_index].astype(jnp.float32) * gates[0].reshape(-1)[:, None]
     moe_out = jnp.sum(weighted.reshape(tok_count, TOP, -1), axis=1)

time: 594 us -> 551 us (0.928)
  waiting for transfers between devices: 305 us -> 368 us
  blocking collectives: 102 us -> 39.5 us
  local copies, waits for them, and re-layouts: 74.3 us -> 47.2 us
  other arithmetic: 38.8 us -> 21 us
    all_gather x3 -> x1, blocking collectives: 102 us -> 39.5 us  [gather_small(): gathered = lax.all_gather(flat[None], 'tok', axis=0, tiled=True)]
    all_gather x1, waiting for transfers between devices: 0.01 us -> 51.5 us  [local(): piece = lax.all_gather(suffix_cache, 'tok', axis=0, tiled=True)]
    convert_element_type x1, local copies, waits for them, and re-layouts: 18.2 us -> 0.13 us  [local(): after_attention = tokens_here.astype(jnp.float32) + projected_out]
    unnamed x1 -> x0, other arithmetic: 15.6 us -> none
    unnamed x26 -> x24, local copies, waits for them, and re-layouts: 17.1 us -> 3.38 us
    all_gather x2, waiting for transfers between devices: 66.1 us -> 77.1 us  [gather_rows(): return lax.all_gather(by_columns[None], 'grp', axis=0, tiled=True)]
  transfers between devices with their start and end apart: 7 -> 7, of which waited for: 5 -> 6; matrix products, arithmetic and copies ran while one was open for 10% -> 11% of each run, Pallas kernels for 0% -> 0%
where the time goes in v1:
time: 551 us; the launch traced here: 549 us
  waiting for transfers between devices  368 us (67%)
  local copies, waits for them, and re-layouts  47.2 us (9%)
  blocking collectives  39.5 us (7%)
  matrix products  34.1 us (6%)
  starting transfers between devices  24.9 us (5%)
  other arithmetic  21 us (4%)
  between operations  14.3 us (3%)
    all_to_all x1, waiting for transfers between devices, local(): lax.all_to_all(expert_result.reshape(EXPERTS, CAP, model_width), 'tok', s...  119 us
    all_gather x2, waiting for transfers between devices, gather_rows(): return lax.all_gather(by_columns[None], 'grp', axis=0, tiled=True)  77.1 us
    all_gather x1, waiting for transfers between devices, local(): lax.all_gather(expert_gate_up, 'grp', axis=1, tiled=True)  60.3 us
    all_to_all x1, waiting for transfers between devices, local(): lax.all_to_all(outgoing.reshape(EXPERTS, CAP, model_width), 'tok', split_...  58.1 us
    all_gather x1, waiting for transfers between devices, local(): piece = lax.all_gather(suffix_cache, 'tok', axis=0, tiled=True)  51.5 us
    all_gather x1, blocking collectives, gather_small(): gathered = lax.all_gather(flat[None], 'tok', axis=0, tiled=True)  39.5 us
    scatter x1, local copies, waits for them, and re-layouts, local(): outgoing = jnp.zeros((EXPERTS * CAP, model_width), jnp.bfloat16).at[slot_...  14.7 us
    all_to_all x1, starting transfers between devices, local(): lax.all_to_all(outgoing.reshape(EXPERTS, CAP, model_width), 'tok', split_...  14.4 us
  transfers between devices with their start and end apart: 7, of which 6 were waited for; matrix products, arithmetic and copies ran while one was open for 11% of the time, Pallas kernels for 0%

profile of v1, /device:TPU:1, one launch (start us, length us, event | category | flops | bytes accessed | tf_op | source)
XLA Modules:
  0.0 548.7 jit_solution(17672893901105111063)
XLA Ops:
  7.2 0.8 copy.113
  8.0 0.8 copy.89
  8.9 0.8 reshape.360
  9.7 39.5 %all-gather = bf16[360448]{0:T(1024)(128)(2,1)S(1)} all-gather(bf16[11264]{0:T(1024)(128)(2,1)S(1)} %pad_maximum_fusion.3), channel_id=2, replica_groups=mesh['grp'=16,'tok'=32] {'tok'}, dimensions={0}, use_global_device_ids=true | all-gather | bytes 743424 | tf_op jit(solution)/shard_map/all_gather | solution.py:51
  49.2 0.3 reshape.407
  49.5 0.2 broadcast_in_dim_reshape.7
  49.7 0.8 copy.90
  51.5 54.1 %all-gather.7.cloned.1.call-done = bf16[16,1024,64]{1,2,0:T(8,128)(2,1)} async-done(((bf16[1,1024,64]{1,2,0:T(8,128)(2,1)}), bf16[16,1024,64]{1,2,0:T(8,128)(2,1)}) %all-gather.7.cloned.1.call-update) | async-done | bytes 2097168 | tf_op jit(solution)/shard_map/all_gather | solution.py:61
  105.6 2.3 convolution_bitcast_fusion.2
  108.0 0.8 copy-done.4
  109.0 0.7 fusion.39
  109.8 0.2 all-gather.11.cloned.1.call-start
  110.0 0.2 broadcast_in_dim_reshape.8
  110.2 0.7 copy.104
  111.1 0.9 slice.81
  112.3 0.5 fusion.11
  112.8 2.4 broadcast_in_dim.44
  115.2 2.6 broadcast_in_dim.49
  117.8 1.3 reshape.366
  119.3 0.9 copy.96
  120.4 9.0 %reduce-window.11 = s32[32,8,128]{2,1,0:T(8,128)S(1)} reduce-window(s32[32,8,128]{2,1,0:T(8,128)S(1)} %fusion.32, s32[]{:T(128)} %constant.34.clone.1), window={size=1x1x128 pad=0_0x0_0x127_0}, to_apply=%region_9.10 | reduce-window | flops 4161536 | bytes 262148 | tf_op jit(solution)/shard_map/reduce-window.1
  130.5 0.7 pad_maximum_fusion
  131.2 1.8 multiply_reduce_fusion
  132.9 51.5 %all-gather.9.cloned.1.call-done = bf16[4096,512]{1,0:T(8,128)(2,1)} async-done(((bf16[128,512]{1,0:T(8,128)(2,1)}), bf16[4096,512]{1,0:T(8,128)(2,1)}) %all-gather.9.cloned.1.call-update) | async-done | bytes 4194320 | tf_op jit(solution)/shard_map/all_gather | solution.py:149
  184.5 3.8 fusion.40
  188.3 2.9 copy.101
  191.2 2.9 copy.99
  194.2 3.5 fusion
  197.7 4.6 fusion.1
  202.3 1.7 copy-done
  204.1 0.6 fusion.12
  204.6 11.2 %fusion.3 = f32[4,256,64]{1,2,0:T(8,128)} fusion(bf16[4,4096,64]{1,2,0:T(8,128)(2,1)} %bitcast.104, f32[4,256,4096]{2,1,0:T(8,128)} %copy-done, f32[4,256]{1,0:T(4,128)S(1)} %get-tuple-element.15, pred[256,4096]{1,0:T(8,128)(4,1)S(1)} %broadcast_in_dim.49), kind=kOutput, calls=%fused_computation.8 | convolution fusion | flops 553648128 | bytes 20189184 | tf_op jit(solution)/shard_map/kqn,knd->kqd/dot_general | solution.py:87
  215.9 1.6 fusion.21
  217.8 23.0 %all-gather.11.cloned.1.call-done = bf16[16,1024,32]{1,2,0:T(8,128)(2,1)} async-done(((bf16[1,1024,32]{1,2,0:T(8,128)(2,1)}), bf16[16,1024,32]{1,2,0:T(8,128)(2,1)}) %all-gather.11.cloned.1.call-update) | async-done | bytes 1048592 | tf_op jit(solution)/shard_map/all_gather | solution.py:61
  240.8 1.6 multiply_reduce_fusion.1
  242.6 14.7 %scatter_custom_fusion = bf16[1280,1024]{1,0:T(8,128)(2,1)} fusion(s32[1024]{0:T(1024)S(1)} %bitcast.118, bf16[128,1024]{1,0:T(8,128)(2,1)S(1)} %multiply_convert_fusion, s32[1024]{0:T(1024)S(1)} %broadcast_clamp_fusion.1, bf16[]{:T(256)} %constant.67.clone.1), kind=kCustom, calls=%fused_computation.17 | custom fusion | bytes 2621442 | tf_op jit(solution)/shard_map/scatter | solution.py:178
  257.4 14.4 %all-to-all-start = ((bf16[32,40,1024]{2,1,0:T(8,128)(2,1)}), bf16[32,40,1024]{2,1,0:T(8,128)(2,1)S(1)}, u32[]{:S(2)}, u32[]{:S(2)}) async-start(bf16[32,40,1024]{2,1,0:T(8,128)(2,1)} %bitcast.34), calls=%async_computation | async-start | bytes 5242880 | tf_op jit(solution)/shard_map/all_to_all | solution.py:180
  271.9 0.5 all-gather.13.cloned.1.call-update
  272.4 0.5 all-gather.15.cloned.1.call-update
  273.0 60.3 %all-gather.13.cloned.1.call-done = bf16[1,1024,1024]{2,1,0:T(8,128)(2,1)} async-done(((bf16[1,64,1024]{2,1,0:T(8,128)(2,1)}), bf16[1,1024,1024]{2,1,0:T(8,128)(2,1)}) %all-gather.13.cloned.1.call-update) | async-done | bytes 2097168 | tf_op jit(solution)/shard_map/all_gather | solution.py:187
  333.3 58.1 %all-to-all-done = bf16[32,40,1024]{2,1,0:T(8,128)(2,1)S(1)} async-done(((bf16[32,40,1024]{2,1,0:T(8,128)(2,1)}), bf16[32,40,1024]{2,1,0:T(8,128)(2,1)S(1)}, u32[]{:S(2)}, u32[]{:S(2)}) %all-to-all-start) | async-done | bytes 2621472 | tf_op jit(solution)/shard_map/all_to_all | solution.py:180
  391.4 6.2 %convolution_bitcast_fusion = f32[1,1280,1024]{2,1,0:T(8,128)} fusion(bf16[1280,1024]{1,0:T(8,128)(2,1)S(1)} %bitcast.102, bf16[1,1024,1024]{2,1,0:T(8,128)(2,1)} %all-gather.13.cloned.1.call-done), kind=kOutput, calls=%fused_computation.10 | convolution fusion | flops 2684354560 | bytes 9961472 | tf_op jit(solution)/shard_map/erd,edf->erf/dot_general | solution.py:184
  397.6 5.9 %convolution_convert_fusion = bf16[1280,1024]{1,0:T(8,128)(2,1)} fusion(f32[1,1280,1024]{2,1,0:T(8,128)} %convolution_bitcast_fusion, bf16[1,512,1024]{2,1,0:T(8,128)(2,1)} %all-gather.15.cloned.1.call-done), kind=kOutput, calls=%fused_computation.13 | convolution fusion | flops 1347420160 | bytes 8912896 | tf_op jit(solution)/shard_map/erf,efd->erd/dot_general | solution.py:192
  403.4 10.1 %all-to-all-start.1 = ((bf16[32,40,1024]{2,1,0:T(8,128)(2,1)}), bf16[32,40,1024]{2,1,0:T(8,128)(2,1)S(1)}, u32[]{:S(2)}, u32[]{:S(2)}) async-start(bf16[32,40,1024]{2,1,0:T(8,128)(2,1)} %bitcast.103), calls=%async_computation.1 | async-start | bytes 5242880 | tf_op jit(solution)/shard_map/all_to_all | solution.py:198
  413.7 119.5 %all-to-all-done.1 = bf16[32,40,1024]{2,1,0:T(8,128)(2,1)S(1)} async-done(((bf16[32,40,1024]{2,1,0:T(8,128)(2,1)}), bf16[32,40,1024]{2,1,0:T(8,128)(2,1)S(1)}, u32[]{:S(2)}, u32[]{:S(2)}) %all-to-all-start.1) | async-done | bytes 2621472 | tf_op jit(solution)/shard_map/all_to_all | solution.py:198
  533.1 5.4 gather_fusion
  538.5 2.9 fusion.6
  541.4 0.8 fusion.27
  (85 shorter events, 3.8 us)
Async XLA Ops:
  7.2 43.5 %copy-start.2 = (bf16[1,128,1024]{2,1,0:T(8,128)(2,1)S(1)}, bf16[1,128,1024]{2,1,0:T(8,128)(2,1)}, u32[]{:S(2)}) copy-start(bf16[1,128,1024]{2,1,0:T(8,128)(2,1)} %param.11) | copy-start | bytes 786436
  7.2 43.6 %copy-start.8 = (f32[1024]{0:T(1024)S(1)}, f32[1024]{0:T(1024)}, u32[]{:S(2)}) copy-start(f32[1024]{0:T(1024)} %param.16) | copy-start | bytes 12292
  7.2 43.7 %copy-start.10 = (s32[1,3]{1,0:T(1,128)S(1)}, s32[1,3]{1,0:T(1,128)}, u32[]{:S(2)}) copy-start(s32[1,3]{1,0:T(1,128)} %param.12) | copy-start | bytes 40
  7.2 98.4 %all-gather.7.cloned.1.call-start = ((), (), s32[]{:S(2)}) async-start(), calls=%async_computation.2 | async-start | bytes 2228224 | tf_op jit(solution)/shard_map/all_gather | solution.py:61
  50.6 133.9 %all-gather.9.cloned.1.call-start = ((), (), s32[]{:S(2)}) async-start(), calls=%async_computation.3 | async-start | bytes 4325376 | tf_op jit(solution)/shard_map/all_gather | solution.py:149
  105.6 6.3 %copy-start.6 = (s32[1,128,8]{1,2,0:T(8,128)S(1)}, s32[1,128,8]{1,2,0:T(8,128)}, u32[]{:S(2)}) copy-start(s32[1,128,8]{1,2,0:T(8,128)} %param.14) | copy-start | bytes 12292
  108.0 0.8 copy-start.4
  109.8 131.0 %all-gather.11.cloned.1.call-start = ((), (), s32[]{:S(2)}) async-start(), calls=%async_computation.4 | async-start | bytes 1114112 | tf_op jit(solution)/shard_map/all_gather | solution.py:61
  117.8 12.2 %slice-start = ((f32[128,1024]{1,0:T(8,128)}), f32[128,512]{1,0:T(8,128)S(1)}, s32[]{:S(2)}) async-start(f32[128,1024]{1,0:T(8,128)} %copy-done.4), calls=%async_computation.7 | async-start | bytes 524288 | tf_op jit(solution)/shard_map/slice | solution.py:126
  197.7 6.4 %copy-start = (f32[4,256,4096]{2,1,0:T(8,128)}, f32[4,256,4096]{2,1,0:T(8,128)S(1)}, u32[]{:S(2)}) copy-start(f32[4,256,4096]{2,1,0:T(8,128)S(1)} %get-tuple-element.22) | copy-start | bytes 50331652
  197.7 6.4 %copy-start.1 = (f32[4,256,512]{2,1,0:T(8,128)S(1)}, f32[4,256,512]{2,1,0:T(8,128)}, u32[]{:S(2)}) copy-start(f32[4,256,512]{2,1,0:T(8,128)} %get-tuple-element.20) | copy-start | bytes 6291460
  204.6 11.3 %copy-start.5 = (bf16[512,256]{0,1:T(8,128)(2,1)S(1)}, bf16[512,256]{0,1:T(8,128)(2,1)}, u32[]{:S(2)}) copy-start(bf16[512,256]{0,1:T(8,128)(2,1)} %copy.96) | copy-start | bytes 786436
  215.9 24.9 %copy-start.3 = (bf16[1,128,1024]{2,1,0:T(8,128)(2,1)S(1)}, bf16[1,128,1024]{2,1,0:T(8,128)(2,1)}, u32[]{:S(2)}) copy-start(bf16[1,128,1024]{2,1,0:T(8,128)(2,1)} %param.11) | copy-start | bytes 786436
  215.9 26.6 %copy-start.7 = (f32[1024]{0:T(1024)S(1)}, f32[1024]{0:T(1024)}, u32[]{:S(2)}) copy-start(f32[1024]{0:T(1024)} %param.19) | copy-start | bytes 12292
  257.4 134.0 %all-to-all-start = ((bf16[32,40,1024]{2,1,0:T(8,128)(2,1)}), bf16[32,40,1024]{2,1,0:T(8,128)(2,1)S(1)}, u32[]{:S(2)}, u32[]{:S(2)}) async-start(bf16[32,40,1024]{2,1,0:T(8,128)(2,1)} %bitcast.34), calls=%async_computation | async-start | bytes 5242880 | tf_op jit(solution)/shard_map/all_to_all | solution.py:180
  271.8 61.5 %all-gather.13.cloned.1.call-start = ((), (), s32[]{:S(2)}) async-start(), calls=%async_computation.5 | async-start | bytes 2228224 | tf_op jit(solution)/shard_map/all_gather | solution.py:187
  272.4 125.2 %all-gather.15.cloned.1.call-start = ((), (), s32[]{:S(2)}) async-start(), calls=%async_computation.6 | async-start | bytes 1114112 | tf_op jit(solution)/shard_map/all_gather | solution.py:195
  403.4 10.1 %copy-start.9 = (f32[1,128,8]{1,2,0:T(8,128)S(1)}, f32[1,128,8]{1,2,0:T(8,128)}, u32[]{:S(2)}) copy-start(f32[1,128,8]{1,2,0:T(8,128)} %param.15) | copy-start | bytes 12292
  403.4 129.7 %all-to-all-start.1 = ((bf16[32,40,1024]{2,1,0:T(8,128)(2,1)}), bf16[32,40,1024]{2,1,0:T(8,128)(2,1)S(1)}, u32[]{:S(2)}, u32[]{:S(2)}) async-start(bf16[32,40,1024]{2,1,0:T(8,128)(2,1)} %bitcast.103), calls=%async_computation.1 | async-start | bytes 5242880 | tf_op jit(solution)/shard_map/all_to_all | solution.py:198
Sparse Core Ops, SparseCore 0:
  50.7 54.9 all-gather.6
  109.9 74.5 all-gather.8
  187.5 53.2 all-gather.10
  275.3 57.9 all-gather.12
  336.2 56.8 all-gather.14

commit v2 on v1

--- a/solution.py
+++ b/solution.py
@@ -59,6 +59,26 @@
 
 def gather_rows(by_columns):
     return lax.all_gather(by_columns[None], "grp", axis=0, tiled=True)
+
+
+def expert_weight_slices(gate_up, down):
+    grp_count = lax.axis_size("grp")
+    tok_count = lax.axis_size("tok")
+    per = tok_count // grp_count
+    pairs = []
+    for g in range(grp_count):
+        for e in range(tok_count):
+            pairs.append((g * tok_count + e, (e // per) * tok_count + per * g + e % per))
+    block = jnp.concatenate([gate_up[0], down[0]], axis=0)
+    return lax.ppermute(block, ("grp", "tok"), pairs)
+
+
+def expert_weights_full(block, after):
+    block, _ = lax.optimization_barrier((block, after))
+    grp_count = lax.axis_size("grp")
+    tok_count = lax.axis_size("tok")
+    gathered = lax.all_gather(block, "tok", axis=0, tiled=True)
+    return gathered.reshape(grp_count, tok_count // grp_count, block.shape[0], block.shape[1])
 
 
 def attend(carry, grouped, keys_values, allowed):
@@ -116,7 +136,11 @@
     group_share = HEADS // KV_HEADS
     normed = rms_scale(tokens_here, attn_gain).astype(jnp.bfloat16)
     qkv_columns, out_columns, prefix_all = gather_small([w_qkv.T, w_out.T, prefix_cache[0]])
-    qkv_weight = gather_rows(qkv_columns)
+    packed_rows = gather_rows(jnp.concatenate([qkv_columns, out_columns], axis=1))
+    qkv_width = qkv_columns.shape[1]
+    qkv_weight = packed_rows[:, :, :qkv_width]
+    out_weight = packed_rows[:, :, qkv_width:]
+    expert_weights = expert_weight_slices(expert_gate_up, expert_down)
     projected = jnp.einsum(
         "ngr,gcr->nc",
         normed.reshape(tok_count, qkv_weight.shape[0], qkv_weight.shape[2]),
@@ -155,7 +179,6 @@
     best, total, mixed = carry
     attended = (mixed / total[..., None]).reshape(KV_HEADS, tok_count, group_share, HEAD_DIM)
     attended = attended.transpose(1, 0, 2, 3).reshape(tok_count, query_width).astype(jnp.bfloat16)
-    out_weight = gather_rows(out_columns)
     projected_out = jnp.einsum(
         "ngr,gcr->nc",
         attended.reshape(tok_count, out_weight.shape[0], out_weight.shape[2]),
@@ -177,26 +200,33 @@
         .at[slot_index]
         .set(moe_in[source_token])
     )
+    grp_count = lax.axis_size("grp")
+    local_experts = EXPERTS // grp_count
+    full = expert_weights_full(expert_weights, piece)
+    gate_rows = expert_gate_up.shape[1]
     arrived = lax.all_to_all(
-        outgoing.reshape(EXPERTS, CAP, model_width), "tok", split_axis=0, concat_axis=0, tiled=True
-    ).reshape(1, EXPERTS * CAP, model_width)
-    sliced = arrived
-    hidden_pair = jnp.einsum(
-        "erd,edf->erf",
-        sliced,
-        lax.all_gather(expert_gate_up, "grp", axis=1, tiled=True),
-        preferred_element_type=jnp.float32,
-    )
+        outgoing.reshape(grp_count, local_experts * CAP, model_width),
+        "grp",
+        split_axis=0,
+        concat_axis=0,
+        tiled=True,
+    )
+    arrived = arrived.reshape(grp_count, local_experts, CAP, model_width).transpose(1, 0, 2, 3)
+    arrived = arrived.reshape(local_experts, grp_count * CAP, model_width)
+    gate_up_w = full[:, :, :gate_rows].transpose(1, 0, 2, 3).reshape(local_experts, -1, model_width)
+    down_w = full[:, :, gate_rows:].transpose(1, 0, 2, 3).reshape(local_experts, -1, model_width)
+    hidden_pair = jnp.einsum("erd,edf->erf", arrived, gate_up_w, preferred_element_type=jnp.float32)
     activated = (jax.nn.silu(hidden_pair[..., :FF]) * hidden_pair[..., FF:]).astype(jnp.bfloat16)
-    sliced = activated
     expert_result = jnp.einsum(
-        "erf,efd->erd",
-        sliced,
-        lax.all_gather(expert_down, "grp", axis=1, tiled=True),
-        preferred_element_type=jnp.float32,
+        "erf,efd->erd", activated, down_w, preferred_element_type=jnp.float32
     ).astype(jnp.bfloat16)
+    expert_result = expert_result.reshape(local_experts, grp_count, CAP, model_width).transpose(1, 0, 2, 3)
     returned = lax.all_to_all(
-        expert_result.reshape(EXPERTS, CAP, model_width), "tok", split_axis=0, concat_axis=0, tiled=True
+        expert_result.reshape(grp_count, local_experts * CAP, model_width),
+        "grp",
+        split_axis=0,
+        concat_axis=0,
+        tiled=True,
     ).reshape(EXPERTS * CAP, -1)
     weighted = returned[slot_index].astype(jnp.float32) * gates[0].reshape(-1)[:, None]
     moe_out = jnp.sum(weighted.reshape(tok_count, TOP, -1), axis=1)

time: 551 us -> 394 us (0.72)
  waiting for transfers between devices: 368 us -> 186 us
  blocking collectives: 39.5 us -> 83.4 us
  starting transfers between devices: 24.9 us -> 4.84 us
    all_to_all x2 -> x1, waiting for transfers between devices: 178 us -> 36.3 us  [local(): lax.all_to_all(expert_result.reshape(grp_count, local_experts * CAP, mode...]
    all_gather x2 -> x1, waiting for transfers between devices: 60.3 us -> 0.02 us  [expert_weights_full(): gathered = lax.all_gather(block, 'tok', axis=0, tiled=True)]
    all_to_all x0 -> x1, blocking collectives: none -> 43.9 us  [local(): lax.all_to_all(outgoing.reshape(grp_count, local_experts * CAP, model_wid...]
    all_gather x1, waiting for transfers between devices: 51.5 us -> 87.8 us  [local(): piece = lax.all_gather(suffix_cache, 'tok', axis=0, tiled=True)]
    all_to_all x2 -> x1, starting transfers between devices: 24.5 us -> 3.86 us  [local(): lax.all_to_all(expert_result.reshape(grp_count, local_experts * CAP, mode...]
    all_gather x2 -> x1, waiting for transfers between devices: 77.1 us -> 61.5 us  [gather_rows(): return lax.all_gather(by_columns[None], 'grp', axis=0, tiled=True)]
    dot_general x2, matrix products: 12.1 us -> 4.47 us  [the longest x1 2.91 us: local(): jnp.einsum('erd,edf->erf', arrived, gate_up_w, preferred_element_type=jnp...]
  transfers between devices with their start and end apart: 7 -> 5, of which waited for: 6 -> 3; matrix products, arithmetic and copies ran while one was open for 11% -> 19% of each run, Pallas kernels for 0% -> 0%
where the time goes in v2:
time: 394 us; the launch traced here: 393 us
  waiting for transfers between devices  186 us (47%)
  blocking collectives  83.4 us (21%)
  local copies, waits for them, and re-layouts  50.8 us (13%)
  matrix products  31.5 us (8%)
  other arithmetic  21.9 us (6%)
  between operations  14.4 us (4%)
  starting transfers between devices  4.84 us (1%)
    all_gather x1, waiting for transfers between devices, local(): piece = lax.all_gather(suffix_cache, 'tok', axis=0, tiled=True)  87.8 us
    all_gather x1, waiting for transfers between devices, gather_rows(): return lax.all_gather(by_columns[None], 'grp', axis=0, tiled=True)  61.5 us
    all_to_all x1, blocking collectives, local(): lax.all_to_all(outgoing.reshape(grp_count, local_experts * CAP, model_wid...  43.9 us
    all_gather x1, blocking collectives, gather_small(): gathered = lax.all_gather(flat[None], 'tok', axis=0, tiled=True)  39.5 us
    all_to_all x1, waiting for transfers between devices, local(): lax.all_to_all(expert_result.reshape(grp_count, local_experts * CAP, mode...  36.3 us
    scatter x1, local copies, waits for them, and re-layouts, local(): outgoing = jnp.zeros((EXPERTS * CAP, model_width), jnp.bfloat16).at[slot_...  13.8 us
    dot_general x2, matrix products, attend(): jnp.einsum('kqn,knd->kqd', probs.astype(jnp.bfloat16), value_heads, prefe...  13.2 us
    another operation x6, other arithmetic  9.38 us
  transfers between devices with their start and end apart: 5, of which 3 were waited for; matrix products, arithmetic and copies ran while one was open for 19% of the time, Pallas kernels for 0%

profile of v2, /device:TPU:1, one launch (start us, length us, event | category | flops | bytes accessed | tf_op | source)
XLA Modules:
  0.0 392.6 jit_solution(4936981358622045825)
XLA Ops:
  7.2 0.8 copy.142
  8.0 0.8 copy.106
  8.9 0.8 reshape.366
  9.7 39.5 %all-gather = bf16[360448]{0:T(1024)(128)(2,1)S(1)} all-gather(bf16[11264]{0:T(1024)(128)(2,1)S(1)} %pad_maximum_fusion.5), channel_id=2, replica_groups=mesh['grp'=16,'tok'=32] {'tok'}, dimensions={0}, use_global_device_ids=true | all-gather | bytes 743424 | tf_op jit(solution)/shard_map/all_gather | solution.py:51
  49.2 0.3 reshape.417
  49.5 0.2 reshape.369
  49.7 0.2 reshape.368
  50.0 0.9 pad_maximum_fusion
  51.8 61.5 %all-gather.10.cloned.1.call-done = bf16[16384,96]{1,0:T(8,128)(2,1)} async-done(((bf16[1024,96]{1,0:T(8,128)(2,1)}), bf16[16384,96]{1,0:T(8,128)(2,1)}) %all-gather.10.cloned.1.call-update) | async-done | bytes 3145744 | tf_op jit(solution)/shard_map/all_gather | solution.py:61
  113.4 4.1 %fusion.20 = f32[128,1024]{1,0:T(8,128)S(1)} fusion(bf16[16,1024,96]{2,1,0:T(8,128)(2,1)} %bitcast.142, f32[128,16,64]{0,2,1:T(8,128)S(1)} %bitcast.120, f32[16,64]{1,0:T(8,128)S(1)} %mul.203, f32[128]{0:T(128)S(1)} %add_rsqrt_fusion.1), kind=kOutput, calls=%fused_computation.29 | convolution fusion | flops 268828672 | bytes 4198912 | tf_op jit(solution)/shard_map/ngr,gcr->nc/dot_general | solution.py:144
  117.5 0.8 copy-done.5
  118.6 0.7 fusion.49
  119.4 0.9 collective-permute-start
  120.3 87.8 %all-gather.6.cloned.1.call-done = bf16[4096,512]{1,0:T(8,128)(2,1)} async-done(((bf16[128,512]{1,0:T(8,128)(2,1)}), bf16[4096,512]{1,0:T(8,128)(2,1)}) %all-gather.6.cloned.1.call-update) | async-done | bytes 4194320 | tf_op jit(solution)/shard_map/all_gather | solution.py:173
  208.1 0.9 slice.99
  209.4 0.5 fusion.14
  209.9 2.4 broadcast_in_dim.51
  212.3 2.6 broadcast_in_dim.52
  214.9 1.3 reshape.374
  216.4 0.9 copy.114
  217.5 9.0 %reduce-window.11 = s32[32,8,128]{2,1,0:T(8,128)S(1)} reduce-window(s32[32,8,128]{2,1,0:T(8,128)S(1)} %fusion.42, s32[]{:T(128)} %constant.34.clone.1), window={size=1x1x128 pad=0_0x0_0x127_0}, to_apply=%region_9.10 | reduce-window | flops 4161536 | bytes 262148 | tf_op jit(solution)/shard_map/reduce-window.1
  227.6 0.7 pad_maximum_fusion.1
  228.3 1.7 multiply_reduce_fusion
  230.0 3.8 fusion.50
  233.8 2.9 copy.119
  236.7 2.9 copy.117
  239.7 3.5 fusion
  243.2 0.6 fusion.15
  243.8 4.6 %fusion.1 = f32[4,256]{1,0:T(4,128)S(1)} fusion(f32[4,256,4096]{2,1,0:T(8,128)S(1)} %get-tuple-element.24, f32[4,256]{1,0:T(4,128)S(1)} %get-tuple-element.17, pred[256,4096]{1,0:T(8,128)(4,1)S(1)} %broadcast_in_dim.52), kind=kLoop, calls=%fused_computation.6 | loop fusion | flops 16776192 | bytes 17833984 | tf_op jit(solution)/shard_map/reduce_sum | solution.py:106
  248.4 0.5 copy-done
  248.9 11.6 %fusion.3 = f32[4,256,64]{1,2,0:T(8,128)} fusion(bf16[4,4096,64]{1,2,0:T(8,128)(2,1)} %bitcast.115, f32[4,256,4096]{2,1,0:T(8,128)} %copy-done, f32[4,256]{1,0:T(4,128)S(1)} %get-tuple-element.17, pred[256,4096]{1,0:T(8,128)(4,1)S(1)} %broadcast_in_dim.52), kind=kOutput, calls=%fused_computation.8 | convolution fusion | flops 553648128 | bytes 20189184 | tf_op jit(solution)/shard_map/kqn,knd->kqd/dot_general | solution.py:107
  260.5 1.6 fusion.32
  262.5 4.5 %multiply_reduce_fusion.1 = (f32[128]{0:T(128)S(1)}, f32[128,1024]{1,0:T(8,128)S(1)}) fusion(bf16[128,16,32]{0,2,1:T(8,128)(2,1)S(1)} %bitcast.128, bf16[16,1024,96]{2,1,0:T(8,128)(2,1)} %bitcast.143, bf16[1,128,1024]{2,1,0:T(8,128)(2,1)S(1)} %copy-done.4), kind=kOutput, calls=%fused_computation.43 | convolution fusion | flops 134741888 | bytes 4063744 | tf_op jit(solution)/shard_map/ngr,gcr->nc/dot_general | solution.py:182
  267.1 13.8 %scatter_custom_fusion = bf16[1280,1024]{1,0:T(8,128)(2,1)S(1)} fusion(s32[1024]{0:T(1024)S(1)} %bitcast.132, bf16[128,1024]{1,0:T(8,128)(2,1)S(1)} %multiply_convert_fusion, s32[1024]{0:T(1024)S(1)} %broadcast_clamp_fusion.1, bf16[]{:T(256)} %constant.67.clone.1), kind=kCustom, calls=%fused_computation.18 | custom fusion | bytes 2621442 | tf_op jit(solution)/shard_map/scatter | solution.py:201
  280.9 43.9 %all_to_all.10 = bf16[16,80,1024]{2,1,0:T(8,128)(2,1)S(1)} all-to-all(bf16[16,80,1024]{2,1,0:T(8,128)(2,1)S(1)} %bitcast.106), channel_id=1, replica_groups=mesh['grp'=16,'tok'=32] {'grp'}, dimensions={0} | all-to-all | bytes 5242880 | tf_op jit(solution)/shard_map/all_to_all | solution.py:207
  324.8 0.3 copy.128
  325.1 1.8 slice.114
  326.9 2.6 slice.111
  329.5 0.3 copy.141
  329.8 0.7 copy.140
  330.5 2.9 fusion.52
  333.4 1.6 convolution_convert_fusion
  335.0 1.7 copy.131
  336.7 3.9 all-to-all-start.1
  340.7 36.3 %all-to-all-done.1 = bf16[16,80,1024]{2,1,0:T(8,128)(2,1)S(1)} async-done(((bf16[16,80,1024]{2,1,0:T(8,128)(2,1)}), bf16[16,80,1024]{2,1,0:T(8,128)(2,1)S(1)}, u32[]{:S(2)}, u32[]{:S(2)}) %all-to-all-start.1) | async-done | bytes 2621472 | tf_op jit(solution)/shard_map/all_to_all | solution.py:224
  377.0 5.4 %gather_fusion = bf16[1024,1024]{1,0:T(8,128)(2,1)} fusion(bf16[1280,1024]{1,0:T(8,128)(2,1)S(1)} %bitcast.103, s32[1024]{0:T(1024)S(1)} %broadcast_clamp_fusion), kind=kCustom, calls=%fused_computation.1 | custom fusion | bytes 4198400 | tf_op jit(solution)/shard_map/gather | solution.py:231
  382.4 2.9 fusion.10
  385.3 0.8 fusion.37
  (94 shorter events, 3.8 us)
Async XLA Ops:
  7.2 43.7 %copy-start.3 = (bf16[1,128,1024]{2,1,0:T(8,128)(2,1)S(1)}, bf16[1,128,1024]{2,1,0:T(8,128)(2,1)}, u32[]{:S(2)}) copy-start(bf16[1,128,1024]{2,1,0:T(8,128)(2,1)} %param.11) | copy-start | bytes 786436
  7.2 106.2 %all-gather.10.cloned.1.call-start = ((), (), s32[]{:S(2)}) async-start(), calls=%async_computation.4 | async-start | bytes 4456448 | tf_op jit(solution)/shard_map/all_gather | solution.py:61
  8.0 43.1 %copy-start.12 = (f32[1024]{0:T(1024)S(1)}, f32[1024]{0:T(1024)}, u32[]{:S(2)}) copy-start(f32[1024]{0:T(1024)} %param.16) | copy-start | bytes 12292
  8.0 43.1 %copy-start.14 = (s32[1,3]{1,0:T(1,128)S(1)}, s32[1,3]{1,0:T(1,128)}, u32[]{:S(2)}) copy-start(s32[1,3]{1,0:T(1,128)} %param.12) | copy-start | bytes 40
  50.8 157.3 %all-gather.6.cloned.1.call-start = ((), (), s32[]{:S(2)}) async-start(), calls=%async_computation.2 | async-start | bytes 4325376 | tf_op jit(solution)/shard_map/all_gather | solution.py:173
  113.4 6.0 %copy-start.8 = (bf16[1,64,1024]{2,1,0:T(8,128)(2,1)S(1)}, bf16[1,64,1024]{2,1,0:T(8,128)(2,1)}, u32[]{:S(2)}) copy-start(bf16[1,64,1024]{2,1,0:T(8,128)(2,1)} %param.20) | copy-start | bytes 393220
  113.4 6.0 %copy-start.9 = (bf16[1,32,1024]{2,1,0:T(8,128)(2,1)S(1)}, bf16[1,32,1024]{2,1,0:T(8,128)(2,1)}, u32[]{:S(2)}) copy-start(bf16[1,32,1024]{2,1,0:T(8,128)(2,1)} %param.21) | copy-start | bytes 196612
  117.5 0.8 copy-start.5
  117.5 91.5 %copy-start.10 = (s32[1,128,8]{1,2,0:T(8,128)S(1)}, s32[1,128,8]{1,2,0:T(8,128)}, u32[]{:S(2)}) copy-start(s32[1,128,8]{1,2,0:T(8,128)} %param.14) | copy-start | bytes 12292
  119.3 205.8 %all-gather.8.cloned.1.call-start = ((), (), s32[]{:S(2)}) async-start(), calls=%async_computation.3 | async-start | bytes 6488064 | tf_op jit(solution)/shard_map/all_gather | solution.py:80
  119.4 0.9 collective-permute-start
  120.3 87.8 %copy-start.7 = (bf16[96,1024]{1,0:T(8,128)(2,1)}, bf16[96,1024]{1,0:T(8,128)(2,1)S(1)}, u32[]{:S(2)}) copy-start(bf16[96,1024]{1,0:T(8,128)(2,1)S(1)} %collective-permute-done) | copy-start | bytes 589828
  214.9 12.2 %slice-start = ((f32[128,1024]{1,0:T(8,128)}), f32[128,512]{1,0:T(8,128)S(1)}, s32[]{:S(2)}) async-start(f32[128,1024]{1,0:T(8,128)} %copy-done.5), calls=%async_computation.5 | async-start | bytes 524288 | tf_op jit(solution)/shard_map/slice | solution.py:150
  239.7 3.5 copy-start.1
  243.2 5.7 %copy-start = (f32[4,256,4096]{2,1,0:T(8,128)}, f32[4,256,4096]{2,1,0:T(8,128)S(1)}, u32[]{:S(2)}) copy-start(f32[4,256,4096]{2,1,0:T(8,128)S(1)} %get-tuple-element.24) | copy-start | bytes 50331652
  248.9 11.6 %copy-start.2 = (f32[4,256,512]{2,1,0:T(8,128)S(1)}, f32[4,256,512]{2,1,0:T(8,128)}, u32[]{:S(2)}) copy-start(f32[4,256,512]{2,1,0:T(8,128)} %get-tuple-element.22) | copy-start | bytes 6291460
  248.9 11.6 %copy-start.6 = (bf16[512,256]{0,1:T(8,128)(2,1)S(1)}, bf16[512,256]{0,1:T(8,128)(2,1)}, u32[]{:S(2)}) copy-start(bf16[512,256]{0,1:T(8,128)(2,1)} %copy.114) | copy-start | bytes 786436
  260.5 1.9 copy-start.4
  262.4 4.5 %copy-start.11 = (f32[1024]{0:T(1024)S(1)}, f32[1024]{0:T(1024)}, u32[]{:S(2)}) copy-start(f32[1024]{0:T(1024)} %param.19) | copy-start | bytes 12292
  336.7 3.9 copy-start.13
  336.7 40.3 %all-to-all-start.1 = ((bf16[16,80,1024]{2,1,0:T(8,128)(2,1)}), bf16[16,80,1024]{2,1,0:T(8,128)(2,1)S(1)}, u32[]{:S(2)}, u32[]{:S(2)}) async-start(bf16[16,80,1024]{2,1,0:T(8,128)(2,1)} %bitcast.105), calls=%async_computation.1 | async-start | bytes 5242880 | tf_op jit(solution)/shard_map/all_to_all | solution.py:224
Sparse Core Ops, SparseCore 0:
  51.0 62.3 all-gather.9
  119.4 88.6 all-gather.5
  210.2 77.2 all-gather.7

commit v3 on v2

--- a/solution.py
+++ b/solution.py
@@ -2,6 +2,8 @@
 import jax.numpy as jnp
 from jax import lax
 from jax.sharding import PartitionSpec as P
+from jax.experimental import pallas as pl
+from jax.experimental.pallas import tpu as pltpu
 
 HEADS = 8
 KV_HEADS = 4
@@ -46,9 +48,95 @@
     )
 
 
+def ring_gather(block, collective_id):
+    tok_count = lax.axis_size("tok")
+    rows, width = block.shape
+    chips = tok_count // 2
+    ahead = chips // 2
+    behind = chips - 1 - ahead
+    mesh_ids = pl.DeviceIdType.MESH
+
+    def kernel(x_ref, out_ref, local_sem, send_r, send_l, send_p, recv):
+        me = lax.axis_index("tok")
+        grp = lax.axis_index("grp")
+        z = me // 2
+        core = me % 2
+        right = ((z + 1) % chips) * 2 + core
+        left = ((z + chips - 1) % chips) * 2 + core
+        peer = z * 2 + (1 - core)
+        barrier = pltpu.get_barrier_semaphore()
+        for other in (right, left, peer):
+            pl.semaphore_signal(barrier, 1, device_id=(grp, other), device_id_type=mesh_ids)
+        pl.semaphore_wait(barrier, 3)
+
+        def remote(src, slot, sem, target):
+            return pltpu.make_async_remote_copy(
+                src_ref=src,
+                dst_ref=out_ref.at[slot],
+                send_sem=sem,
+                recv_sem=recv.at[slot],
+                device_id=(grp, target),
+                device_id_type=mesh_ids,
+            )
+
+        own = pltpu.make_async_copy(x_ref, out_ref.at[me], local_sem.at[0])
+        own.start()
+        sends = [
+            remote(x_ref, me, send_p.at[0], peer),
+            remote(x_ref, me, send_r.at[0], right),
+            remote(x_ref, me, send_l.at[0], left),
+        ]
+        for c in sends:
+            c.start()
+        peer_count = 1
+        for s in range(1, ahead + 1):
+            for sign, limit, sem, target in ((-1, ahead, send_r, right), (1, behind, send_l, left)):
+                if s > limit:
+                    continue
+                slot = ((z + chips + sign * s) % chips) * 2 + core
+                remote(out_ref.at[slot], slot, sem.at[0], target).wait_recv()
+                if s < limit:
+                    c = remote(out_ref.at[slot], slot, sem.at[s], target)
+                    c.start()
+                    sends.append(c)
+                c = remote(out_ref.at[slot], slot, send_p.at[peer_count], peer)
+                c.start()
+                sends.append(c)
+                peer_count += 1
+        for other_z in range(chips):
+            slot = other_z * 2 + (1 - core)
+            remote(out_ref.at[slot], slot, send_p.at[0], peer).wait_recv()
+        own.wait()
+        for c in sends:
+            c.wait_send()
+
+    block_bytes = rows * width * block.dtype.itemsize
+    return pl.pallas_call(
+        kernel,
+        out_shape=jax.ShapeDtypeStruct((tok_count, rows, width), block.dtype),
+        in_specs=[pl.BlockSpec(memory_space=pltpu.VMEM)],
+        out_specs=pl.BlockSpec(memory_space=pltpu.VMEM),
+        scratch_shapes=[
+            pltpu.SemaphoreType.DMA((1,)),
+            pltpu.SemaphoreType.DMA((ahead,)),
+            pltpu.SemaphoreType.DMA((ahead,)),
+            pltpu.SemaphoreType.DMA((chips,)),
+            pltpu.SemaphoreType.DMA((tok_count,)),
+        ],
+        compiler_params=pltpu.CompilerParams(collective_id=collective_id, has_side_effects=True),
+        cost_estimate=pl.CostEstimate(
+            flops=0, transcendentals=0, bytes_accessed=2 * tok_count * block_bytes
+        ),
+    )(block)
+
+
 def gather_small(blocks):
     flat = jnp.concatenate([b.reshape(-1) for b in blocks])
-    gathered = lax.all_gather(flat[None], "tok", axis=0, tiled=True)
+    width = 512
+    padded_rows = -(-flat.shape[0] // (16 * width)) * 16
+    flat = jnp.pad(flat, (0, padded_rows * width - flat.shape[0]))
+    gathered = ring_gather(flat.reshape(padded_rows, width), 1)
+    gathered = gathered.reshape(gathered.shape[0], -1)
     pieces, start = [], 0
     for b in blocks:
         size = b.size
@@ -135,7 +223,7 @@
     key_width = KV_HEADS * HEAD_DIM
     group_share = HEADS // KV_HEADS
     normed = rms_scale(tokens_here, attn_gain).astype(jnp.bfloat16)
-    qkv_columns, out_columns, prefix_all = gather_small([w_qkv.T, w_out.T, prefix_cache[0]])
+    qkv_columns, out_columns = gather_small([w_qkv.T, w_out.T])
     packed_rows = gather_rows(jnp.concatenate([qkv_columns, out_columns], axis=1))
     qkv_width = qkv_columns.shape[1]
     qkv_weight = packed_rows[:, :, :qkv_width]
@@ -167,10 +255,10 @@
         jnp.zeros((KV_HEADS, row_count), jnp.float32),
         jnp.zeros((KV_HEADS, row_count, HEAD_DIM), jnp.float32),
     )
-    carry = attend(
-        start_carry, grouped, prefix_all, None
-    )
-    piece = lax.all_gather(suffix_cache, "tok", axis=0, tiled=True)
+    both = ring_gather(jnp.concatenate([suffix_cache, prefix_cache[0]], axis=0), 0)
+    piece = both[:, :tok_count].reshape(-1, both.shape[2])
+    prefix_all = both[:, tok_count:].reshape(-1, both.shape[2])
+    carry = attend(start_carry, grouped, prefix_all, None)
     key_index = jnp.arange(piece.shape[0], dtype=jnp.int32)
     key_segment, key_offset = request_layout(group_lengths, key_index)
     earlier = key_index[None, :] <= token_index[:, None]

time: 394 us -> 377 us (0.957)
  Pallas kernels: 0 us -> 88.7 us
  waiting for transfers between devices: 186 us -> 117 us
  blocking collectives: 83.4 us -> 38.4 us
  local copies, waits for them, and re-layouts: 50.8 us -> 61.8 us
    pallas_call x0 -> x2, Pallas kernels: none -> 88.7 us  [ring_gather(): pl.pallas_call(kernel, out_shape=jax.ShapeDtypeStruct((tok_count, rows, w...]
    all_gather x1 -> x0, waiting for transfers between devices: 87.8 us -> none  [local(): piece = lax.all_gather(suffix_cache, 'tok', axis=0, tiled=True)]
    all_gather x1 -> x0, blocking collectives: 39.5 us -> none  [gather_small(): gathered = lax.all_gather(flat[None], 'tok', axis=0, tiled=True)]
    all_gather x1, waiting for transfers between devices: 61.5 us -> 81 us  [gather_rows(): return lax.all_gather(by_columns[None], 'grp', axis=0, tiled=True)]
    all_to_all x1, blocking collectives: 43.9 us -> 38.4 us  [local(): lax.all_to_all(outgoing.reshape(grp_count, local_experts * CAP, model_wid...]
    slice x2 -> x5, local copies, waits for them, and re-layouts: 0.22 us -> 4.87 us  [the longest x1 4.65 us: local(): piece = both[:, :tok_count].reshape(-1, both.shape[2])]
  transfers between devices with their start and end apart: 5 -> 4, of which waited for: 3 -> 2; matrix products, arithmetic and copies ran while one was open for 19% -> 23% of each run, Pallas kernels for 0% -> 14%
where the time goes in v3:
time: 377 us; the launch traced here: 376 us
  waiting for transfers between devices  117 us (31%)
  Pallas kernels  88.7 us (24%)
  local copies, waits for them, and re-layouts  61.8 us (16%)
  blocking collectives  38.4 us (10%)
  matrix products  28.4 us (8%)
  other arithmetic  22.3 us (6%)
  between operations  14.7 us (4%)
  starting transfers between devices  4.61 us (1%)
    pallas_call x2, Pallas kernels, ring_gather(): pl.pallas_call(kernel, out_shape=jax.ShapeDtypeStruct((tok_count, rows, w...  88.7 us
    all_gather x1, waiting for transfers between devices, gather_rows(): return lax.all_gather(by_columns[None], 'grp', axis=0, tiled=True)  81 us
    all_to_all x1, blocking collectives, local(): lax.all_to_all(outgoing.reshape(grp_count, local_experts * CAP, model_wid...  38.4 us
    all_to_all x1, waiting for transfers between devices, local(): lax.all_to_all(expert_result.reshape(grp_count, local_experts * CAP, mode...  36.3 us
    scatter x1, local copies, waits for them, and re-layouts, local(): outgoing = jnp.zeros((EXPERTS * CAP, model_width), jnp.bfloat16).at[slot_...  13.7 us
    dot_general x2, matrix products, attend(): jnp.einsum('kqn,knd->kqd', probs.astype(jnp.bfloat16), value_heads, prefe...  11.2 us
    another operation x6, other arithmetic  9.38 us
    slice x3, local copies, waits for them, and re-layouts, attend(): keys_values[:, :key_width].reshape(key_count, KV_HEADS, HEAD_DIM)  8.85 us
  transfers between devices with their start and end apart: 4, of which 2 were waited for; matrix products, arithmetic and copies ran while one was open for 23% of the time, Pallas kernels for 14%

profile of v3, /device:TPU:1, one launch (start us, length us, event | category | flops | bytes accessed | tf_op | source)
XLA Modules:
  0.0 376.2 jit_solution(111896795973751169)
XLA Ops:
  7.3 0.9 reshape.375
  8.2 0.8 copy.80
  9.0 0.6 reshape.377.x_ref
  9.7 37.6 %shard_map.122 = bf16[32,16,512]{2,1,0:T(8,128)(2,1)} custom-call(bf16[16,512]{1,0:T(8,128)(2,1)} %reshape.377.x_ref), custom_call_target="tpu_custom_call" | custom-call | bytes 1048576 | tf_op jit(solution)/shard_map/pallas_call | solution.py:114
  47.2 1.3 copy.116
  48.6 0.2 reshape.379
  48.9 0.2 reshape.380
  49.1 0.9 pad_maximum_fusion
  50.0 0.7 collective-permute-start
  51.6 81.0 %all-gather.6.cloned.1.call-done = bf16[16384,96]{1,0:T(8,128)(2,1)} async-done(((bf16[1024,96]{1,0:T(8,128)(2,1)}), bf16[16384,96]{1,0:T(8,128)(2,1)}) %all-gather.6.cloned.1.call-update) | async-done | bytes 3145744 | tf_op jit(solution)/shard_map/all_gather | solution.py:149
  132.6 4.1 %fusion.20 = f32[128,1024]{1,0:T(8,128)S(1)} fusion(bf16[16,1024,96]{2,1,0:T(8,128)(2,1)} %bitcast.150, f32[128,16,64]{0,2,1:T(8,128)S(1)} %bitcast.129, f32[16,64]{1,0:T(8,128)S(1)} %mul.203, f32[128]{0:T(128)S(1)} %add_rsqrt_fusion.1), kind=kOutput, calls=%fused_computation.29 | convolution fusion | flops 268828672 | bytes 4198912 | tf_op jit(solution)/shard_map/ngr,gcr->nc/dot_general | solution.py:232
  137.0 0.7 pad_maximum_fusion.3.x_ref
  137.7 51.2 %shard_map.123 = bf16[32,144,512]{2,1,0:T(8,128)(2,1)} custom-call(bf16[144,512]{1,0:T(8,128)(2,1)} %pad_maximum_fusion.3.x_ref), custom_call_target="tpu_custom_call" | custom-call | bytes 9437184 | tf_op jit(solution)/shard_map/pallas_call | solution.py:114
  188.9 4.7 %slice.83 = bf16[32,128,512]{2,1,0:T(8,128)(2,1)} slice(bf16[32,144,512]{2,1,0:T(8,128)(2,1)} %shard_map.123), slice={[0:32], [0:128], [0:512]} | slice | bytes 8388608 | tf_op jit(solution)/shard_map/slice | solution.py:259
  193.5 0.7 copy-done.4
  194.7 9.0 %reduce-window.11 = s32[32,8,128]{2,1,0:T(8,128)S(1)} reduce-window(s32[32,8,128]{2,1,0:T(8,128)S(1)} %fusion.42, s32[]{:T(128)} %constant.63.clone.1), window={size=1x1x128 pad=0_0x0_0x127_0}, to_apply=%region_9.10 | reduce-window | flops 4161536 | bytes 262148 | tf_op jit(solution)/shard_map/reduce-window.1
  204.2 0.5 fusion.14
  204.7 3.8 %broadcast_in_dim.44 = pred[128,2,4096]{2,1,0:T(4,128)(4,1)} broadcast(pred[128,4096]{1,0:T(8,128)(4,1)S(1)} %fusion.14), dimensions={0,2} | broadcast | bytes 1572864 | tf_op jit(solution)/shard_map/broadcast_in_dim | solution.py:187
  208.5 5.5 %broadcast_in_dim.49 = pred[256,4096]{1,0:T(8,128)(4,1)S(1)} reshape(pred[128,2,4096]{2,1,0:T(4,128)(4,1)} %broadcast_in_dim.44) | data formatting | bytes 2097152 | tf_op jit(solution)/shard_map/jit(_where)/broadcast_in_dim | solution.py:190
  215.1 4.6 %fusion.52 = (bf16[4096,256]{1,0:T(8,128)(2,1)}, bf16[4096,256]{1,0:T(8,128)(2,1)}) fusion(bf16[4096,512]{1,0:T(8,128)(2,1)} %bitcast.109), kind=kLoop, calls=%fused_computation.103 | loop fusion | bytes 8388608 | tf_op jit(solution)/shard_map/slice | solution.py:176
  219.7 4.1 %copy.91 = bf16[4096,256]{0,1:T(8,128)(2,1)} copy(bf16[4096,256]{1,0:T(8,128)(2,1)} %get-tuple-element.6) | data formatting | bytes 4194304 | tf_op jit(solution)/shard_map/slice | solution.py:176
  223.9 4.2 %copy.93 = bf16[4096,256]{0,1:T(8,128)(2,1)} copy(bf16[4096,256]{1,0:T(8,128)(2,1)} %get-tuple-element.7) | data formatting | bytes 4194304 | tf_op jit(solution)/shard_map/slice | solution.py:178
  228.0 0.7 pad_maximum_fusion.1
  228.8 0.5 multiply_reduce_fusion
  229.2 0.4 copy-done.1
  229.7 3.6 fusion
  233.3 0.6 fusion.15
  233.9 4.4 %fusion.1 = f32[4,256]{1,0:T(4,128)S(1)} fusion(f32[4,256,4096]{2,1,0:T(8,128)S(1)} %get-tuple-element.22, f32[4,256]{1,0:T(4,128)S(1)} %get-tuple-element.15, pred[256,4096]{1,0:T(8,128)(4,1)S(1)} %broadcast_in_dim.49), kind=kLoop, calls=%fused_computation.6 | loop fusion | flops 16776192 | bytes 17833984 | tf_op jit(solution)/shard_map/reduce_sum | solution.py:194
  238.3 0.8 copy-done
  239.1 9.0 %fusion.3 = f32[4,256,64]{1,2,0:T(8,128)S(1)} fusion(bf16[4,4096,64]{1,2,0:T(8,128)(2,1)} %bitcast.121, f32[4,256,4096]{2,1,0:T(8,128)} %copy-done, f32[4,256]{1,0:T(4,128)S(1)} %get-tuple-element.15, pred[256,4096]{1,0:T(8,128)(4,1)S(1)} %broadcast_in_dim.49), kind=kOutput, calls=%fused_computation.8 | convolution fusion | flops 553648128 | bytes 20189184 | tf_op jit(solution)/shard_map/kqn,knd->kqd/dot_general | solution.py:195
  248.1 2.2 fusion.32
  250.7 4.5 %multiply_reduce_fusion.1 = (f32[128]{0:T(128)S(1)}, f32[128,1024]{1,0:T(8,128)S(1)}) fusion(bf16[128,16,32]{0,2,1:T(8,128)(2,1)S(1)} %bitcast.137, bf16[16,1024,96]{2,1,0:T(8,128)(2,1)} %bitcast.151, bf16[1,128,1024]{2,1,0:T(8,128)(2,1)S(1)} %copy-done.3), kind=kOutput, calls=%fused_computation.43 | convolution fusion | flops 134741888 | bytes 4063744 | tf_op jit(solution)/shard_map/ngr,gcr->nc/dot_general | solution.py:270
  255.4 13.7 %scatter_custom_fusion = bf16[1280,1024]{1,0:T(8,128)(2,1)S(1)} fusion(s32[1024]{0:T(1024)S(1)} %bitcast.141, bf16[128,1024]{1,0:T(8,128)(2,1)S(1)} %multiply_convert_fusion, s32[1024]{0:T(1024)S(1)} %broadcast_clamp_fusion.1, bf16[]{:T(256)} %constant.31.clone.1), kind=kCustom, calls=%fused_computation.18 | custom fusion | bytes 2621442 | tf_op jit(solution)/shard_map/scatter | solution.py:289
  269.1 38.4 %all_to_all.10 = bf16[16,80,1024]{2,1,0:T(8,128)(2,1)S(1)} all-to-all(bf16[16,80,1024]{2,1,0:T(8,128)(2,1)S(1)} %bitcast.112), channel_id=1, replica_groups=mesh['grp'=16,'tok'=32] {'grp'}, dimensions={0} | all-to-all | bytes 5242880 | tf_op jit(solution)/shard_map/all_to_all | solution.py:295
  307.5 0.3 copy.102
  307.8 1.8 slice.117
  309.5 2.6 slice.114
  312.2 0.7 copy.114
  312.9 0.2 copy.115
  313.1 2.9 fusion.54
  316.0 1.6 convolution_convert_fusion
  317.6 1.7 copy.105
  319.4 3.9 %all-to-all-start.1 = ((bf16[16,80,1024]{2,1,0:T(8,128)(2,1)}), bf16[16,80,1024]{2,1,0:T(8,128)(2,1)S(1)}, u32[]{:S(2)}, u32[]{:S(2)}) async-start(bf16[16,80,1024]{2,1,0:T(8,128)(2,1)} %bitcast.111), calls=%async_computation.1 | async-start | bytes 5242880 | tf_op jit(solution)/shard_map/all_to_all | solution.py:312
  323.3 0.7 maximum_bitcast_fusion
  324.0 36.3 %all-to-all-done.1 = bf16[16,80,1024]{2,1,0:T(8,128)(2,1)S(1)} async-done(((bf16[16,80,1024]{2,1,0:T(8,128)(2,1)}), bf16[16,80,1024]{2,1,0:T(8,128)(2,1)S(1)}, u32[]{:S(2)}, u32[]{:S(2)}) %all-to-all-start.1) | async-done | bytes 2621472 | tf_op jit(solution)/shard_map/all_to_all | solution.py:312
  360.3 5.4 %gather_fusion = bf16[1024,1024]{1,0:T(8,128)(2,1)} fusion(bf16[1280,1024]{1,0:T(8,128)(2,1)S(1)} %bitcast.107, s32[1024]{0:T(1024)S(1)} %broadcast_clamp_fusion), kind=kCustom, calls=%fused_computation.1 | custom fusion | bytes 4198400 | tf_op jit(solution)/shard_map/gather | solution.py:319
  365.6 2.9 fusion.10
  368.6 0.8 fusion.37
  (89 shorter events, 3.9 us)
Async XLA Ops:
  7.2 42.8 %copy-start.6 = (bf16[1,32,1024]{2,1,0:T(8,128)(2,1)S(1)}, bf16[1,32,1024]{2,1,0:T(8,128)(2,1)}, u32[]{:S(2)}) copy-start(bf16[1,32,1024]{2,1,0:T(8,128)(2,1)} %param.21) | copy-start | bytes 196612
  7.2 42.8 %copy-start.5 = (bf16[1,64,1024]{2,1,0:T(8,128)(2,1)S(1)}, bf16[1,64,1024]{2,1,0:T(8,128)(2,1)}, u32[]{:S(2)}) copy-start(bf16[1,64,1024]{2,1,0:T(8,128)(2,1)} %param.20) | copy-start | bytes 393220
  7.2 43.5 %copy-start.10 = (f32[1024]{0:T(1024)S(1)}, f32[1024]{0:T(1024)}, u32[]{:S(2)}) copy-start(f32[1024]{0:T(1024)} %param.16) | copy-start | bytes 12292
  7.2 43.6 %copy-start.3 = (bf16[1,128,1024]{2,1,0:T(8,128)(2,1)S(1)}, bf16[1,128,1024]{2,1,0:T(8,128)(2,1)}, u32[]{:S(2)}) copy-start(bf16[1,128,1024]{2,1,0:T(8,128)(2,1)} %param.11) | copy-start | bytes 786436
  7.2 43.7 %copy-start.12 = (s32[1,3]{1,0:T(1,128)S(1)}, s32[1,3]{1,0:T(1,128)}, u32[]{:S(2)}) copy-start(s32[1,3]{1,0:T(1,128)} %param.12) | copy-start | bytes 40
  7.2 125.4 %all-gather.6.cloned.1.call-start = ((), (), s32[]{:S(2)}) async-start(), calls=%async_computation.3 | async-start | bytes 4456448 | tf_op jit(solution)/shard_map/all_gather | solution.py:149
  49.9 257.8 %all-gather.4.cloned.1.call-start = ((), (), s32[]{:S(2)}) async-start(), calls=%async_computation.2 | async-start | bytes 6488064 | tf_op jit(solution)/shard_map/all_gather | solution.py:168
  50.0 143.5 %collective-permute-start = (bf16[96,1024]{1,0:T(8,128)(2,1)S(1)}, bf16[96,1024]{1,0:T(8,128)(2,1)S(1)}, u32[]{:S(2)}, u32[]{:S(2)}) collective-permute-start(bf16[96,1024]{1,0:T(8,128)(2,1)S(1)} %pad_maximum_fusion.2), channel_id=1, source_target_pairs={{0,0},{1,1},{2,32},{3,33},{4,64},{5,65},{6,96},{7,97},{8,128},{9,1... | collective-permute-start | bytes 589832 | tf_op jit(solution)/shard_map/ppermute | solution.py:161
  132.6 4.4 %copy-start.7 = (bf16[1,16,512]{2,1,0:T(8,128)(2,1)S(1)}, bf16[1,16,512]{2,1,0:T(8,128)(2,1)}, u32[]{:S(2)}) copy-start(bf16[1,16,512]{2,1,0:T(8,128)(2,1)} %param.13) | copy-start | bytes 49156
  188.8 5.4 %copy-start.8 = (s32[1,128,8]{1,2,0:T(8,128)S(1)}, s32[1,128,8]{1,2,0:T(8,128)}, u32[]{:S(2)}) copy-start(s32[1,128,8]{1,2,0:T(8,128)} %param.14) | copy-start | bytes 12292
  193.5 0.7 copy-start.4
  208.5 6.3 %slice-start = ((bf16[32,144,512]{2,1,0:T(8,128)(2,1)}), bf16[32,16,512]{2,1,0:T(8,128)(2,1)S(1)}, s32[]{:S(2)}) async-start(bf16[32,144,512]{2,1,0:T(8,128)(2,1)} %shard_map.123), calls=%async_computation.4 | async-start | bytes 1048576 | tf_op jit(solution)/shard_map/slice | solution.py:260
  228.0 1.6 copy-start.1
  229.2 4.0 %copy-start.2 = (f32[4,256,512]{2,1,0:T(8,128)}, f32[4,256,512]{2,1,0:T(8,128)S(1)}, u32[]{:S(2)}) copy-start(f32[4,256,512]{2,1,0:T(8,128)S(1)} %get-tuple-element.20) | copy-start | bytes 6291460
  233.2 5.8 %copy-start = (f32[4,256,4096]{2,1,0:T(8,128)}, f32[4,256,4096]{2,1,0:T(8,128)S(1)}, u32[]{:S(2)}) copy-start(f32[4,256,4096]{2,1,0:T(8,128)S(1)} %get-tuple-element.22) | copy-start | bytes 50331652
  250.7 4.6 %copy-start.9 = (f32[1024]{0:T(1024)S(1)}, f32[1024]{0:T(1024)}, u32[]{:S(2)}) copy-start(f32[1024]{0:T(1024)} %param.19) | copy-start | bytes 12292
  319.4 3.9 %copy-start.11 = (f32[1,128,8]{1,2,0:T(8,128)S(1)}, f32[1,128,8]{1,2,0:T(8,128)}, u32[]{:S(2)}) copy-start(f32[1,128,8]{1,2,0:T(8,128)} %param.15) | copy-start | bytes 12292
  319.4 40.9 %all-to-all-start.1 = ((bf16[16,80,1024]{2,1,0:T(8,128)(2,1)}), bf16[16,80,1024]{2,1,0:T(8,128)(2,1)S(1)}, u32[]{:S(2)}, u32[]{:S(2)}) async-start(bf16[16,80,1024]{2,1,0:T(8,128)(2,1)} %bitcast.111), calls=%async_computation.1 | async-start | bytes 5242880 | tf_op jit(solution)/shard_map/all_to_all | solution.py:312
Sparse Core Ops, SparseCore 0:
  50.1 82.4 all-gather.5
  194.3 70.2 all-gather.3

commit v4 on v3

--- a/solution.py
+++ b/solution.py
@@ -130,26 +130,19 @@
     )(block)
 
 
-def gather_small(blocks):
-    flat = jnp.concatenate([b.reshape(-1) for b in blocks])
+def gather_weights(w_qkv, w_out):
+    qkv_rows, out_rows = w_qkv.shape[0], w_out.shape[0]
+    by_rows = lax.all_gather(
+        jnp.concatenate([w_qkv, w_out], axis=0)[None], "grp", axis=0, tiled=True
+    )
+    grp_count, packed_rows, columns = by_rows.shape
     width = 512
-    padded_rows = -(-flat.shape[0] // (16 * width)) * 16
-    flat = jnp.pad(flat, (0, padded_rows * width - flat.shape[0]))
-    gathered = ring_gather(flat.reshape(padded_rows, width), 1)
-    gathered = gathered.reshape(gathered.shape[0], -1)
-    pieces, start = [], 0
-    for b in blocks:
-        size = b.size
-        pieces.append(gathered[:, start : start + size].reshape((-1,) + b.shape[1:]))
-        start += size
-    return pieces
-
-
-def gather_rows(by_columns):
-    return lax.all_gather(by_columns[None], "grp", axis=0, tiled=True)
-
-
-def expert_weight_slices(gate_up, down):
+    ring = ring_gather(by_rows.reshape(-1, width), 1)
+    ring = ring.reshape(ring.shape[0], grp_count, packed_rows, columns)
+    return ring[:, :, :qkv_rows], ring[:, :, qkv_rows:]
+
+
+def expert_weight_slices(gate_up, down, after):
     grp_count = lax.axis_size("grp")
     tok_count = lax.axis_size("tok")
     per = tok_count // grp_count
@@ -158,6 +151,7 @@
         for e in range(tok_count):
             pairs.append((g * tok_count + e, (e // per) * tok_count + per * g + e % per))
     block = jnp.concatenate([gate_up[0], down[0]], axis=0)
+    block, _ = lax.optimization_barrier((block, after))
     return lax.ppermute(block, ("grp", "tok"), pairs)
 
 
@@ -223,18 +217,13 @@
     key_width = KV_HEADS * HEAD_DIM
     group_share = HEADS // KV_HEADS
     normed = rms_scale(tokens_here, attn_gain).astype(jnp.bfloat16)
-    qkv_columns, out_columns = gather_small([w_qkv.T, w_out.T])
-    packed_rows = gather_rows(jnp.concatenate([qkv_columns, out_columns], axis=1))
-    qkv_width = qkv_columns.shape[1]
-    qkv_weight = packed_rows[:, :, :qkv_width]
-    out_weight = packed_rows[:, :, qkv_width:]
-    expert_weights = expert_weight_slices(expert_gate_up, expert_down)
+    qkv_weight, out_weight = gather_weights(w_qkv, w_out)
     projected = jnp.einsum(
-        "ngr,gcr->nc",
-        normed.reshape(tok_count, qkv_weight.shape[0], qkv_weight.shape[2]),
+        "ngr,tgrc->ntc",
+        normed.reshape(tok_count, qkv_weight.shape[1], qkv_weight.shape[2]),
         qkv_weight,
         preferred_element_type=jnp.float32,
-    )
+    ).reshape(tok_count, -1)
     query = rotate(projected[:, :query_width].reshape(tok_count, HEADS, HEAD_DIM), position).astype(
         jnp.bfloat16
     )
@@ -258,6 +247,7 @@
     both = ring_gather(jnp.concatenate([suffix_cache, prefix_cache[0]], axis=0), 0)
     piece = both[:, :tok_count].reshape(-1, both.shape[2])
     prefix_all = both[:, tok_count:].reshape(-1, both.shape[2])
+    expert_weights = expert_weight_slices(expert_gate_up, expert_down, both)
     carry = attend(start_carry, grouped, prefix_all, None)
     key_index = jnp.arange(piece.shape[0], dtype=jnp.int32)
     key_segment, key_offset = request_layout(group_lengths, key_index)
@@ -268,11 +258,11 @@
     attended = (mixed / total[..., None]).reshape(KV_HEADS, tok_count, group_share, HEAD_DIM)
     attended = attended.transpose(1, 0, 2, 3).reshape(tok_count, query_width).astype(jnp.bfloat16)
     projected_out = jnp.einsum(
-        "ngr,gcr->nc",
-        attended.reshape(tok_count, out_weight.shape[0], out_weight.shape[2]),
+        "ngr,tgrc->ntc",
+        attended.reshape(tok_count, out_weight.shape[1], out_weight.shape[2]),
         out_weight,
         preferred_element_type=jnp.float32,
-    )
+    ).reshape(tok_count, -1)
     after_attention = tokens_here.astype(jnp.float32) + projected_out
     moe_in = rms_scale(after_attention, moe_gain).astype(jnp.bfloat16)
     model_width = moe_in.shape[1]

time: 377 us -> 416 us (1.10); the launches traced: 376 us -> 409 us
  waiting for transfers between devices: 117 us -> 34.9 us
  blocking collectives: 38.4 us -> 97.3 us
  local copies, waits for them, and re-layouts: 61.8 us -> 109 us
  Pallas kernels: 88.7 us -> 99 us
    all_gather x1 -> x0, waiting for transfers between devices: 81 us -> none  [gather_rows(): return lax.all_gather(by_columns[None], 'grp', axis=0, tiled=True)]
    all_to_all x1, blocking collectives: 38.4 us -> 77.7 us  [local(): lax.all_to_all(outgoing.reshape(grp_count, local_experts * CAP, model_wid...]
    dot_general x0 -> x5, local copies, waits for them, and re-layouts: none -> 32.4 us  [the longest x2 18.5 us: local(): jnp.einsum('ngr,tgrc->ntc', normed.reshape(tok_count, qkv_weight.shape[1]...]
    all_gather x0 -> x1, blocking collectives: none -> 19.6 us  [gather_weights(): lax.all_gather(jnp.concatenate([w_qkv, w_out], axis=0)[None], 'grp', axis...]
    reshape x5 -> x2, local copies, waits for them, and re-layouts: 2.04 us -> 15.7 us  [the longest x1 14.7 us: gather_weights(): ring = ring.reshape(ring.shape[0], grp_count, packed_rows, columns)]
    pallas_call x2, Pallas kernels: 88.7 us -> 99 us  [ring_gather(): pl.pallas_call(kernel, out_shape=jax.ShapeDtypeStruct((tok_count, rows, w...]
    dot_general x2, matrix products: 8.65 us -> 4.15 us  [the longest x1 3.73 us: local(): jnp.einsum('ngr,tgrc->ntc', normed.reshape(tok_count, qkv_weight.shape[1]...]
  transfers between devices with their start and end apart: 4 -> 3, of which waited for: 2 -> 1; matrix products, arithmetic and copies ran while one was open for 23% -> 22% of each run, Pallas kernels for 14% -> 0%
where the time goes in v4:
time: 416 us; the launch traced here: 409 us
  local copies, waits for them, and re-layouts  109 us (26%)
  Pallas kernels  99 us (24%)
  blocking collectives  97.3 us (23%)
  waiting for transfers between devices  34.9 us (8%)
  matrix products  24.4 us (6%)
  other arithmetic  24.3 us (6%)
  between operations  14.9 us (4%)
  starting transfers between devices  4.86 us (1%)
    pallas_call x2, Pallas kernels, ring_gather(): pl.pallas_call(kernel, out_shape=jax.ShapeDtypeStruct((tok_count, rows, w...  99 us
    all_to_all x1, blocking collectives, local(): lax.all_to_all(outgoing.reshape(grp_count, local_experts * CAP, model_wid...  77.7 us
    all_to_all x1, waiting for transfers between devices, local(): lax.all_to_all(expert_result.reshape(grp_count, local_experts * CAP, mode...  34.8 us
    all_gather x1, blocking collectives, gather_weights(): lax.all_gather(jnp.concatenate([w_qkv, w_out], axis=0)[None], 'grp', axis...  19.6 us
    dot_general x2, local copies, waits for them, and re-layouts, local(): jnp.einsum('ngr,tgrc->ntc', normed.reshape(tok_count, qkv_weight.shape[1]...  18.5 us
    reshape x1, local copies, waits for them, and re-layouts, gather_weights(): ring = ring.reshape(ring.shape[0], grp_count, packed_rows, columns)  14.7 us
    dot_general x3, local copies, waits for them, and re-layouts, local(): jnp.einsum('ngr,tgrc->ntc', attended.reshape(tok_count, out_weight.shape[...  13.9 us
    scatter x1, local copies, waits for them, and re-layouts, local(): outgoing = jnp.zeros((EXPERTS * CAP, model_width), jnp.bfloat16).at[slot_...  13.7 us
  transfers between devices with their start and end apart: 3, of which 1 were waited for; matrix products, arithmetic and copies ran while one was open for 22% of the time, Pallas kernels for 0%

profile of v4, /device:TPU:1, one launch (start us, length us, event | category | flops | bytes accessed | tf_op | source)
XLA Modules:
  0.0 408.5 jit_solution(4580629096140424447)
XLA Ops:
  7.2 1.1 fusion.25
  8.3 0.8 copy.115
  9.1 0.8 maximum_bitcast_fusion.1
  9.9 19.6 %all-gather.1 = bf16[16,96,32]{1,2,0:T(8,128)(2,1)S(1)} all-gather(bf16[1,96,32]{1,2,0:T(8,128)(2,1)S(1)} %maximum_bitcast_fusion.1), channel_id=2, replica_groups=mesh['grp'=16,'tok'=32] {'grp'}, dimensions={0}, use_global_device_ids=true | all-gather | bytes 104448 | tf_op jit(solution)/shard_map/all_gather | solution.py:135
  29.4 1.1 fusion.27
  30.9 1.0 reshape.378.x_ref
  31.9 53.0 %shard_map.122 = bf16[32,96,512]{2,1,0:T(8,128)(2,1)} custom-call(bf16[96,512]{1,0:T(8,128)(2,1)} %reshape.378.x_ref), custom_call_target="tpu_custom_call" | custom-call | bytes 6291456 | tf_op jit(solution)/shard_map/pallas_call | solution.py:114
  84.9 14.7 %reshape.379 = bf16[32,16,96,32]{3,2,1,0:T(8,128)(2,1)} reshape(bf16[32,96,512]{2,1,0:T(8,128)(2,1)} %shard_map.122) | data formatting | bytes 6291456 | tf_op jit(solution)/shard_map/reshape | solution.py:141
  99.6 9.9 %slice_bitcast_fusion = bf16[32,32,16,64]{1,3,2,0:T(8,128)(2,1)} fusion(bf16[32,16,96,32]{3,2,1,0:T(8,128)(2,1)} %reshape.379), kind=kLoop, calls=%fused_computation.8 | loop fusion | bytes 4194304 | tf_op jit(solution)/shard_map/ngr,tgrc->ntc/dot_general | solution.py:221
  109.5 8.6 %copy.147 = bf16[32,32,16,64]{3,1,0,2:T(8,128)(2,1)} copy(bf16[32,32,16,64]{1,3,2,0:T(8,128)(2,1)} %slice_bitcast_fusion) | data formatting | bytes 4194304 | tf_op jit(solution)/shard_map/ngr,tgrc->ntc/dot_general | solution.py:221
  118.1 3.7 convolution_bitcast_fusion.1
  122.8 0.7 pad_maximum_fusion.2.x_ref
  123.5 46.0 %shard_map.123 = bf16[32,144,512]{2,1,0:T(8,128)(2,1)} custom-call(bf16[144,512]{1,0:T(8,128)(2,1)} %pad_maximum_fusion.2.x_ref), custom_call_target="tpu_custom_call" | custom-call | bytes 9437184 | tf_op jit(solution)/shard_map/pallas_call | solution.py:114
  169.5 1.0 collective-permute-start
  170.7 0.7 eq.61
  171.4 4.6 %slice.75 = bf16[32,128,512]{2,1,0:T(8,128)(2,1)} slice(bf16[32,144,512]{2,1,0:T(8,128)(2,1)} %shard_map.123), slice={[0:32], [0:128], [0:512]} | slice | bytes 8388608 | tf_op jit(solution)/shard_map/slice | solution.py:248
  176.1 0.7 mul.239
  176.8 0.7 copy-done.9
  177.5 9.0 %reduce-window.11 = s32[32,8,128]{2,1,0:T(8,128)S(1)} reduce-window(s32[32,8,128]{2,1,0:T(8,128)S(1)} %fusion.31, s32[]{:T(128)} %constant.34.clone.1), window={size=1x1x128 pad=0_0x0_0x127_0}, to_apply=%region_9.10 | reduce-window | flops 4161536 | bytes 262148 | tf_op jit(solution)/shard_map/reduce-window.1
  187.5 3.8 broadcast_in_dim.44
  191.2 5.4 %broadcast_in_dim.49 = pred[256,4096]{1,0:T(8,128)(4,1)S(1)} reshape(pred[128,2,4096]{2,1,0:T(4,128)(4,1)} %broadcast_in_dim.44) | data formatting | bytes 2097152 | tf_op jit(solution)/shard_map/jit(_where)/broadcast_in_dim | solution.py:184
  196.7 3.0 slice_bitcast_fusion.1
  199.7 4.6 %copy.132 = bf16[32,32,16,32]{1,0,3,2:T(8,128)(2,1)} copy(bf16[32,32,16,32]{1,3,2,0:T(8,128)(2,1)S(1)} %slice_bitcast_fusion.1) | data formatting | bytes 2097152 | tf_op jit(solution)/shard_map/ngr,tgrc->ntc/dot_general | solution.py:260
  204.3 6.2 %dot_general.40 = bf16[1024,16,32]{0,2,1:T(8,128)(2,1)S(1)} reshape(bf16[32,32,16,32]{1,0,3,2:T(8,128)(2,1)} %copy.132) | data formatting | bytes 2097152 | tf_op jit(solution)/shard_map/ngr,tgrc->ntc/dot_general | solution.py:260
  211.1 0.7 fusion.39
  211.9 1.1 copy.126
  213.1 4.5 %fusion.38 = (bf16[4096,256]{1,0:T(8,128)(2,1)}, bf16[4096,256]{1,0:T(8,128)(2,1)}) fusion(bf16[4096,512]{1,0:T(8,128)(2,1)} %bitcast.123), kind=kLoop, calls=%fused_computation.98 | loop fusion | bytes 8388608 | tf_op jit(solution)/shard_map/slice | solution.py:170
  217.6 4.1 %copy.127 = bf16[4096,256]{0,1:T(8,128)(2,1)} copy(bf16[4096,256]{1,0:T(8,128)(2,1)} %get-tuple-element.8) | data formatting | bytes 4194304 | tf_op jit(solution)/shard_map/slice | solution.py:170
  221.7 4.1 %copy.129 = bf16[4096,256]{0,1:T(8,128)(2,1)} copy(bf16[4096,256]{1,0:T(8,128)(2,1)} %get-tuple-element.9) | data formatting | bytes 4194304 | tf_op jit(solution)/shard_map/slice | solution.py:172
  225.8 0.7 pad_maximum_fusion
  227.4 4.1 %fusion = (f32[4,256]{1,0:T(4,128)S(1)}, f32[4,256,4096]{2,1,0:T(8,128)S(1)}) fusion(pred[256,4096]{1,0:T(8,128)(4,1)S(1)} %broadcast_in_dim.49, bf16[4,256,64]{2,1,0:T(8,128)(2,1)S(1)} %bitcast.132, bf16[4,4096,64]{1,2,0:T(8,128)(2,1)S(1)} %bitcast.124), kind=kOutput, calls=%fused_computation.5 | convolution fusion | flops 549452800 | bytes 20058112 | tf_op jit(solution)/shard_map/kqd,knd->kqn/dot_general | solution.py:175
  232.1 4.4 %fusion.1 = f32[4,256]{1,0:T(4,128)S(1)} fusion(f32[4,256,4096]{2,1,0:T(8,128)S(1)} %get-tuple-element.24, f32[4,256]{1,0:T(4,128)S(1)} %get-tuple-element.17, pred[256,4096]{1,0:T(8,128)(4,1)S(1)} %broadcast_in_dim.49), kind=kLoop, calls=%fused_computation.6 | loop fusion | flops 16776192 | bytes 17833984 | tf_op jit(solution)/shard_map/reduce_sum | solution.py:188
  236.5 0.7 copy-done
  237.3 8.9 %fusion.3 = f32[4,256,64]{1,2,0:T(8,128)S(1)} fusion(bf16[4,4096,64]{1,2,0:T(8,128)(2,1)} %bitcast.135, f32[4,256,4096]{2,1,0:T(8,128)} %copy-done, f32[4,256]{1,0:T(4,128)S(1)} %get-tuple-element.17, pred[256,4096]{1,0:T(8,128)(4,1)S(1)} %broadcast_in_dim.49), kind=kOutput, calls=%fused_computation.9 | convolution fusion | flops 553648128 | bytes 20189184 | tf_op jit(solution)/shard_map/kqn,knd->kqd/dot_general | solution.py:189
  246.2 2.3 fusion.20
  249.6 13.7 %scatter_custom_fusion = bf16[1280,1024]{1,0:T(8,128)(2,1)S(1)} fusion(s32[1024]{0:T(1024)S(1)} %bitcast.152, bf16[128,1024]{1,0:T(8,128)(2,1)S(1)} %multiply_convert_fusion, s32[1024]{0:T(1024)S(1)} %broadcast_clamp_fusion.1, bf16[]{:T(256)} %constant.67.clone.1), kind=kCustom, calls=%fused_computation.16 | custom fusion | bytes 2621442 | tf_op jit(solution)/shard_map/scatter | solution.py:279
  263.3 77.7 %all_to_all.10 = bf16[16,80,1024]{2,1,0:T(8,128)(2,1)S(1)} all-to-all(bf16[16,80,1024]{2,1,0:T(8,128)(2,1)S(1)} %bitcast.126), channel_id=1, replica_groups=mesh['grp'=16,'tok'=32] {'grp'}, dimensions={0} | all-to-all | bytes 5242880 | tf_op jit(solution)/shard_map/all_to_all | solution.py:285
  341.3 1.8 slice.107
  343.1 2.6 slice.104
  345.7 0.7 copy.145
  346.7 2.9 fusion.40
  349.6 1.6 convolution_convert_fusion
  351.2 1.7 copy.141
  352.9 3.9 all-to-all-start.1
  357.6 34.8 %all-to-all-done.1 = bf16[16,80,1024]{2,1,0:T(8,128)(2,1)S(1)} async-done(((bf16[16,80,1024]{2,1,0:T(8,128)(2,1)}), bf16[16,80,1024]{2,1,0:T(8,128)(2,1)S(1)}, u32[]{:S(2)}, u32[]{:S(2)}) %all-to-all-start.1) | async-done | bytes 2621472 | tf_op jit(solution)/shard_map/all_to_all | solution.py:302
  392.4 5.4 %gather_fusion = bf16[1024,1024]{1,0:T(8,128)(2,1)} fusion(bf16[1280,1024]{1,0:T(8,128)(2,1)S(1)} %bitcast.120, s32[1024]{0:T(1024)S(1)} %broadcast_clamp_fusion), kind=kCustom, calls=%fused_computation.1 | custom fusion | bytes 4198400 | tf_op jit(solution)/shard_map/gather | solution.py:309
  397.8 2.9 fusion.6
  400.7 0.8 fusion.28
  (99 shorter events, 6.9 us)
Async XLA Ops:
  7.2 334.1 %all-gather.4.cloned.1.call-start = ((), (), s32[]{:S(2)}) async-start(), calls=%async_computation.2 | async-start | bytes 6488064 | tf_op jit(solution)/shard_map/all_gather | solution.py:162
  118.1 3.8 copy-start.18
  118.1 4.6 %copy-start.12 = (bf16[1,16,512]{2,1,0:T(8,128)(2,1)S(1)}, bf16[1,16,512]{2,1,0:T(8,128)(2,1)}, u32[]{:S(2)}) copy-start(bf16[1,16,512]{2,1,0:T(8,128)(2,1)} %param.13) | copy-start | bytes 49156
  121.9 49.5 %copy-start.4 = (f32[128,1024]{1,0:T(8,128)}, f32[128,1024]{1,0:T(8,128)S(1)}, u32[]{:S(2)}) copy-start(f32[128,1024]{1,0:T(8,128)S(1)} %convolution_bitcast_fusion.1) | copy-start | bytes 1572868
  121.9 47.6 %copy-start.5 = (bf16[128,256]{1,0:T(8,128)(2,1)}, bf16[128,256]{1,0:T(8,128)(2,1)S(1)}, u32[]{:S(2)}) copy-start(bf16[128,256]{1,0:T(8,128)(2,1)S(1)} %slice.127) | copy-start | bytes 196612
  122.6 46.8 %copy-start.10 = (bf16[1,64,1024]{2,1,0:T(8,128)(2,1)S(1)}, bf16[1,64,1024]{2,1,0:T(8,128)(2,1)}, u32[]{:S(2)}) copy-start(bf16[1,64,1024]{2,1,0:T(8,128)(2,1)} %param.20) | copy-start | bytes 393220
  122.6 46.8 %copy-start.11 = (bf16[1,32,1024]{2,1,0:T(8,128)(2,1)S(1)}, bf16[1,32,1024]{2,1,0:T(8,128)(2,1)}, u32[]{:S(2)}) copy-start(bf16[1,32,1024]{2,1,0:T(8,128)(2,1)} %param.21) | copy-start | bytes 196612
  122.8 46.8 %copy-start.7 = (bf16[128,256]{1,0:T(8,128)(2,1)}, bf16[128,256]{1,0:T(8,128)(2,1)S(1)}, u32[]{:S(2)}) copy-start(bf16[128,256]{1,0:T(8,128)(2,1)S(1)} %copy.123) | copy-start | bytes 196612
  123.5 47.0 %copy-start.15 = (s32[1,128,8]{1,2,0:T(8,128)S(1)}, s32[1,128,8]{1,2,0:T(8,128)}, u32[]{:S(2)}) copy-start(s32[1,128,8]{1,2,0:T(8,128)} %param.14) | copy-start | bytes 12292
  169.5 7.3 %collective-permute-start = (bf16[96,1024]{1,0:T(8,128)(2,1)S(1)}, bf16[96,1024]{1,0:T(8,128)(2,1)S(1)}, u32[]{:S(2)}, u32[]{:S(2)}) collective-permute-start(bf16[96,1024]{1,0:T(8,128)(2,1)S(1)} %pad_maximum_fusion.1), channel_id=1, source_target_pairs={{0,0},{1,1},{2,32},{3,33},{4,64},{5,65},{6,96},{7,97},{8,128},{9,1... | collective-permute-start | bytes 589832 | tf_op jit(solution)/shard_map/ppermute | solution.py:155
  176.8 0.7 copy-start.9
  204.3 6.3 %slice-start.1 = ((f32[128,1024]{1,0:T(8,128)}), f32[128,512]{1,0:T(8,128)S(1)}, s32[]{:S(2)}) async-start(f32[128,1024]{1,0:T(8,128)} %copy-done.4), calls=%async_computation.4 | async-start | bytes 524288 | tf_op jit(solution)/shard_map/slice | solution.py:227
  204.3 6.8 %slice-start = ((bf16[32,144,512]{2,1,0:T(8,128)(2,1)}), bf16[32,16,512]{2,1,0:T(8,128)(2,1)S(1)}, s32[]{:S(2)}) async-start(bf16[32,144,512]{2,1,0:T(8,128)(2,1)} %shard_map.123), calls=%async_computation.3 | async-start | bytes 1048576 | tf_op jit(solution)/shard_map/slice | solution.py:249
  225.8 1.6 copy-start.1
  227.0 4.5 %copy-start.2 = (f32[4,256,512]{2,1,0:T(8,128)}, f32[4,256,512]{2,1,0:T(8,128)S(1)}, u32[]{:S(2)}) copy-start(f32[4,256,512]{2,1,0:T(8,128)S(1)} %get-tuple-element.22) | copy-start | bytes 6291460
  231.5 5.7 %copy-start = (f32[4,256,4096]{2,1,0:T(8,128)}, f32[4,256,4096]{2,1,0:T(8,128)S(1)}, u32[]{:S(2)}) copy-start(f32[4,256,4096]{2,1,0:T(8,128)S(1)} %get-tuple-element.24) | copy-start | bytes 50331652
  246.2 2.8 copy-start.14
  246.2 2.8 copy-start.3
  246.2 3.3 copy-start.13
  246.2 3.3 copy-start.16
  352.9 3.9 copy-start.17
  352.9 4.0 copy-start.6
  352.9 4.0 copy-start.8
  352.9 39.5 %all-to-all-start.1 = ((bf16[16,80,1024]{2,1,0:T(8,128)(2,1)}), bf16[16,80,1024]{2,1,0:T(8,128)(2,1)S(1)}, u32[]{:S(2)}, u32[]{:S(2)}) async-start(bf16[16,80,1024]{2,1,0:T(8,128)(2,1)} %bitcast.125), calls=%async_computation.1 | async-start | bytes 5242880 | tf_op jit(solution)/shard_map/all_to_all | solution.py:302
Sparse Core Ops, SparseCore 0:
  177.6 111.4 all-gather.3

commit v5 on v3

--- a/solution.py
+++ b/solution.py
@@ -149,7 +149,7 @@
     return lax.all_gather(by_columns[None], "grp", axis=0, tiled=True)
 
 
-def expert_weight_slices(gate_up, down):
+def expert_weight_slices(gate_up, down, after):
     grp_count = lax.axis_size("grp")
     tok_count = lax.axis_size("tok")
     per = tok_count // grp_count
@@ -158,6 +158,8 @@
         for e in range(tok_count):
             pairs.append((g * tok_count + e, (e // per) * tok_count + per * g + e % per))
     block = jnp.concatenate([gate_up[0], down[0]], axis=0)
+    probe = after.reshape(-1)[0]
+    block = jnp.where(probe != probe, jnp.zeros_like(block), block)
     return lax.ppermute(block, ("grp", "tok"), pairs)
 
 
@@ -224,11 +226,10 @@
     group_share = HEADS // KV_HEADS
     normed = rms_scale(tokens_here, attn_gain).astype(jnp.bfloat16)
     qkv_columns, out_columns = gather_small([w_qkv.T, w_out.T])
-    packed_rows = gather_rows(jnp.concatenate([qkv_columns, out_columns], axis=1))
-    qkv_width = qkv_columns.shape[1]
-    qkv_weight = packed_rows[:, :, :qkv_width]
-    out_weight = packed_rows[:, :, qkv_width:]
-    expert_weights = expert_weight_slices(expert_gate_up, expert_down)
+    qkv_weight = gather_rows(qkv_columns)
+    out_columns, _ = lax.optimization_barrier((out_columns, qkv_weight))
+    out_weight = gather_rows(out_columns)
+    expert_weights = expert_weight_slices(expert_gate_up, expert_down, out_weight)
     projected = jnp.einsum(
         "ngr,gcr->nc",
         normed.reshape(tok_count, qkv_weight.shape[0], qkv_weight.shape[2]),
@@ -280,7 +281,13 @@
     onehot = (flat_routes[:, None] == jnp.arange(EXPERTS, dtype=jnp.int32)[None, :]).astype(
         jnp.int32
     )
-    slot_rank = jnp.sum(jnp.cumsum(onehot, axis=0) * onehot, axis=1) - 1
+    route_count = flat_routes.shape[0]
+    lower = (
+        jnp.arange(route_count, dtype=jnp.int32)[:, None]
+        >= jnp.arange(route_count, dtype=jnp.int32)[None, :]
+    ).astype(jnp.bfloat16)
+    running = jnp.dot(lower, onehot.astype(jnp.bfloat16), preferred_element_type=jnp.float32)
+    slot_rank = jnp.sum(running.astype(jnp.int32) * onehot, axis=1) - 1
     slot_index = flat_routes * CAP + slot_rank
     source_token = jnp.arange(flat_routes.shape[0], dtype=jnp.int32) // TOP
     outgoing = (

time: 377 us -> 448 us (1.19)
  waiting for transfers between devices: 117 us -> 158 us
  Pallas kernels: 88.7 us -> 116 us
  other arithmetic: 22.3 us -> 12.3 us
  blocking collectives: 38.4 us -> 44.6 us
  local copies, waits for them, and re-layouts: 61.8 us -> 67.6 us
    all_gather x1 -> x2, waiting for transfers between devices: 81 us -> 121 us  [gather_rows(): return lax.all_gather(by_columns[None], 'grp', axis=0, tiled=True)]
    pallas_call x2, Pallas kernels: 88.7 us -> 116 us  [ring_gather(): pl.pallas_call(kernel, out_shape=jax.ShapeDtypeStruct((tok_count, rows, w...]
    another operation x6 -> x3, other arithmetic: 9.38 us -> 0.24 us
    all_to_all x1, blocking collectives: 38.4 us -> 44.6 us  [local(): lax.all_to_all(outgoing.reshape(grp_count, local_experts * CAP, model_wid...]
    reshape x0 -> x1, local copies, waits for them, and re-layouts: none -> 5.13 us  [expert_weight_slices(): probe = after.reshape(-1)[0]]
  transfers between devices with their start and end apart: 4 -> 5, of which waited for: 2 -> 3; matrix products, arithmetic and copies ran while one was open for 23% -> 17% of each run, Pallas kernels for 14% -> 17%
where the time goes in v5:
time: 448 us; the launch traced here: 447 us
  waiting for transfers between devices  158 us (35%)
  Pallas kernels  116 us (26%)
  local copies, waits for them, and re-layouts  67.6 us (15%)
  blocking collectives  44.6 us (10%)
  matrix products  28.5 us (6%)
  between operations  15.6 us (3%)
  other arithmetic  12.3 us (3%)
  starting transfers between devices  4.83 us (1%)
    all_gather x2, waiting for transfers between devices, gather_rows(): return lax.all_gather(by_columns[None], 'grp', axis=0, tiled=True)  121 us
    pallas_call x2, Pallas kernels, ring_gather(): pl.pallas_call(kernel, out_shape=jax.ShapeDtypeStruct((tok_count, rows, w...  116 us
    all_to_all x1, blocking collectives, local(): lax.all_to_all(outgoing.reshape(grp_count, local_experts * CAP, model_wid...  44.6 us
    all_to_all x1, waiting for transfers between devices, local(): lax.all_to_all(expert_result.reshape(grp_count, local_experts * CAP, mode...  36.4 us
    scatter x1, local copies, waits for them, and re-layouts, local(): outgoing = jnp.zeros((EXPERTS * CAP, model_width), jnp.bfloat16).at[slot_...  13.5 us
    dot_general x2, matrix products, attend(): jnp.einsum('kqn,knd->kqd', probs.astype(jnp.bfloat16), value_heads, prefe...  11.3 us
  transfers between devices with their start and end apart: 5, of which 3 were waited for; matrix products, arithmetic and copies ran while one was open for 17% of the time, Pallas kernels for 17%

profile of v5, /device:TPU:1, one launch (start us, length us, event | category | flops | bytes accessed | tf_op | source)
XLA Modules:
  0.0 446.8 jit_solution(16414492464916319291)
XLA Ops:
  7.2 0.8 copy.99
  8.1 0.8 reshape.360
  8.9 0.6 reshape.362.x_ref
  9.6 37.6 %shard_map.122 = bf16[32,16,512]{2,1,0:T(8,128)(2,1)} custom-call(bf16[16,512]{1,0:T(8,128)(2,1)} %reshape.362.x_ref), custom_call_target="tpu_custom_call" | custom-call | bytes 1048576 | tf_op jit(solution)/shard_map/pallas_call | solution.py:114
  47.1 1.3 copy.129
  48.7 0.8 copy.100
  49.6 0.9 reshape.375
  50.5 54.1 %all-gather.5.cloned.1.call-done = bf16[16,1024,64]{1,2,0:T(8,128)(2,1)} async-done(((bf16[1,1024,64]{1,2,0:T(8,128)(2,1)}), bf16[16,1024,64]{1,2,0:T(8,128)(2,1)}) %all-gather.5.cloned.1.call-update) | async-done | bytes 2097168 | tf_op jit(solution)/shard_map/all_gather | solution.py:149
  105.6 2.3 convolution_bitcast_fusion.1
  108.1 67.2 %all-gather.9.cloned.1.call-done = bf16[16384,32]{1,0:T(8,128)(2,1)} async-done(((bf16[1024,32]{1,0:T(8,128)(2,1)}), bf16[16384,32]{1,0:T(8,128)(2,1)}) %all-gather.9.cloned.1.call-update) | async-done | bytes 1048592 | tf_op jit(solution)/shard_map/all_gather | solution.py:149
  175.4 5.1 %reshape.379 = bf16[524288]{0:T(1024)(128)(2,1)S(1)} reshape(bf16[16384,32]{1,0:T(8,128)(2,1)} %all-gather.9.cloned.1.call-done) | data formatting | bytes 2097152 | tf_op jit(solution)/shard_map/reshape | solution.py:161
  180.5 0.5 slice.98
  182.4 0.9 collective-permute-start
  183.4 0.7 pad_maximum_fusion.1.x_ref
  184.1 78.0 %shard_map.123 = bf16[32,144,512]{2,1,0:T(8,128)(2,1)} custom-call(bf16[144,512]{1,0:T(8,128)(2,1)} %pad_maximum_fusion.1.x_ref), custom_call_target="tpu_custom_call" | custom-call | bytes 9437184 | tf_op jit(solution)/shard_map/pallas_call | solution.py:114
  262.1 4.7 %slice.72 = bf16[32,128,512]{2,1,0:T(8,128)(2,1)} slice(bf16[32,144,512]{2,1,0:T(8,128)(2,1)} %shard_map.123), slice={[0:32], [0:128], [0:512]} | slice | bytes 8388608 | tf_op jit(solution)/shard_map/slice | solution.py:260
  266.8 0.7 copy-done.4
  267.6 0.5 fusion.11
  268.1 3.8 broadcast_in_dim.45
  271.9 5.4 %broadcast_in_dim.50 = pred[256,4096]{1,0:T(8,128)(4,1)S(1)} reshape(pred[128,2,4096]{2,1,0:T(4,128)(4,1)} %broadcast_in_dim.45) | data formatting | bytes 2097152 | tf_op jit(solution)/shard_map/jit(_where)/broadcast_in_dim | solution.py:192
  277.7 0.5 fusion.24
  278.3 4.5 %fusion.42 = (bf16[4096,256]{1,0:T(8,128)(2,1)}, bf16[4096,256]{1,0:T(8,128)(2,1)}) fusion(bf16[4096,512]{1,0:T(8,128)(2,1)} %bitcast.98), kind=kLoop, calls=%fused_computation.99 | loop fusion | bytes 8388608 | tf_op jit(solution)/shard_map/slice | solution.py:178
  282.8 4.1 copy.111
  287.5 4.1 copy.109
  292.0 0.7 pad_maximum_fusion
  292.7 0.5 multiply_reduce_fusion
  293.2 5.5 %fusion = (f32[4,256]{1,0:T(4,128)S(1)}, f32[4,256,4096]{2,1,0:T(8,128)S(1)}) fusion(pred[256,4096]{1,0:T(8,128)(4,1)S(1)} %broadcast_in_dim.50, bf16[4,256,64]{2,1,0:T(8,128)(2,1)S(1)} %bitcast.107, bf16[4,4096,64]{1,2,0:T(8,128)(2,1)} %bitcast.99), kind=kOutput, calls=%fused_computation.5 | convolution fusion | flops 549452800 | bytes 20058112 | tf_op jit(solution)/shard_map/kqd,knd->kqn/dot_general | solution.py:183
  298.7 0.6 fusion.12
  299.3 4.4 fusion.1
  303.7 0.8 copy-done
  304.5 9.1 %fusion.3 = f32[4,256,64]{1,2,0:T(8,128)S(1)} fusion(bf16[4,4096,64]{1,2,0:T(8,128)(2,1)} %bitcast.110, f32[4,256,4096]{2,1,0:T(8,128)} %copy-done, f32[4,256]{1,0:T(4,128)S(1)} %get-tuple-element.17, pred[256,4096]{1,0:T(8,128)(4,1)S(1)} %broadcast_in_dim.50), kind=kOutput, calls=%fused_computation.8 | convolution fusion | flops 553648128 | bytes 20189184 | tf_op jit(solution)/shard_map/kqn,knd->kqd/dot_general | solution.py:197
  313.6 2.2 fusion.21
  316.2 3.8 multiply_reduce_fusion.1
  320.1 13.5 %scatter_custom_fusion = bf16[1280,1024]{1,0:T(8,128)(2,1)S(1)} fusion(s32[1024]{0:T(1024)S(1)} %bitcast.128, bf16[128,1024]{1,0:T(8,128)(2,1)S(1)} %multiply_convert_fusion, s32[1024]{0:T(1024)S(1)} %broadcast_clamp_fusion.1, bf16[]{:T(256)} %constant.27.clone.1), kind=kCustom, calls=%fused_computation.16 | custom fusion | bytes 2621442 | tf_op jit(solution)/shard_map/scatter | solution.py:296
  333.6 44.6 %all_to_all.10 = bf16[16,80,1024]{2,1,0:T(8,128)(2,1)S(1)} all-to-all(bf16[16,80,1024]{2,1,0:T(8,128)(2,1)S(1)} %bitcast.101), channel_id=1, replica_groups=mesh['grp'=16,'tok'=32] {'grp'}, dimensions={0} | all-to-all | bytes 5242880 | tf_op jit(solution)/shard_map/all_to_all | solution.py:302
  378.6 1.8 slice.102
  380.4 2.6 slice.99
  383.0 0.3 copy.128
  383.3 0.7 copy.127
  384.0 2.9 fusion.44
  386.9 1.6 convolution_convert_fusion
  388.5 1.8 copy.121
  390.2 3.9 all-to-all-start.1
  394.2 0.7 maximum_bitcast_fusion
  394.9 36.4 %all-to-all-done.1 = bf16[16,80,1024]{2,1,0:T(8,128)(2,1)S(1)} async-done(((bf16[16,80,1024]{2,1,0:T(8,128)(2,1)}), bf16[16,80,1024]{2,1,0:T(8,128)(2,1)S(1)}, u32[]{:S(2)}, u32[]{:S(2)}) %all-to-all-start.1) | async-done | bytes 2621472 | tf_op jit(solution)/shard_map/all_to_all | solution.py:319
  431.2 5.3 %gather_fusion = bf16[1024,1024]{1,0:T(8,128)(2,1)} fusion(bf16[1280,1024]{1,0:T(8,128)(2,1)S(1)} %bitcast.95, s32[1024]{0:T(1024)S(1)} %broadcast_clamp_fusion), kind=kCustom, calls=%fused_computation.1 | custom fusion | bytes 4198400 | tf_op jit(solution)/shard_map/gather | solution.py:326
  436.6 2.9 fusion.6
  439.5 0.8 fusion.29
  (86 shorter events, 3.9 us)
Async XLA Ops:
  7.2 97.5 %copy-start.2 = (bf16[1,128,1024]{2,1,0:T(8,128)(2,1)S(1)}, bf16[1,128,1024]{2,1,0:T(8,128)(2,1)}, u32[]{:S(2)}) copy-start(bf16[1,128,1024]{2,1,0:T(8,128)(2,1)} %param.11) | copy-start | bytes 786436
  7.2 97.7 %copy-start.10 = (f32[1024]{0:T(1024)S(1)}, f32[1024]{0:T(1024)}, u32[]{:S(2)}) copy-start(f32[1024]{0:T(1024)} %param.16) | copy-start | bytes 12292
  7.2 97.7 %copy-start.12 = (s32[1,3]{1,0:T(1,128)S(1)}, s32[1,3]{1,0:T(1,128)}, u32[]{:S(2)}) copy-start(s32[1,3]{1,0:T(1,128)} %param.12) | copy-start | bytes 40
  7.2 97.4 %all-gather.5.cloned.1.call-start = ((), (), s32[]{:S(2)}) async-start(), calls=%async_computation.2 | async-start | bytes 2228224 | tf_op jit(solution)/shard_map/all_gather | solution.py:149
  49.6 125.8 %all-gather.9.cloned.1.call-start = ((), (), s32[]{:S(2)}) async-start(), calls=%async_computation.4 | async-start | bytes 4456448 | tf_op jit(solution)/shard_map/all_gather | solution.py:149
  104.6 273.9 %all-gather.7.cloned.1.call-start = ((), (), s32[]{:S(2)}) async-start(), calls=%async_computation.3 | async-start | bytes 6488064 | tf_op jit(solution)/shard_map/all_gather | solution.py:170
  107.9 170.4 %copy-start.3 = (f32[128,1024]{1,0:T(8,128)}, f32[128,1024]{1,0:T(8,128)S(1)}, u32[]{:S(2)}) copy-start(f32[128,1024]{1,0:T(8,128)S(1)} %convolution_bitcast_fusion.1) | copy-start | bytes 1572868
  108.1 74.2 %copy-start.5 = (bf16[1,64,1024]{2,1,0:T(8,128)(2,1)S(1)}, bf16[1,64,1024]{2,1,0:T(8,128)(2,1)}, u32[]{:S(2)}) copy-start(bf16[1,64,1024]{2,1,0:T(8,128)(2,1)} %param.20) | copy-start | bytes 393220
  108.1 74.2 %copy-start.6 = (bf16[1,32,1024]{2,1,0:T(8,128)(2,1)S(1)}, bf16[1,32,1024]{2,1,0:T(8,128)(2,1)}, u32[]{:S(2)}) copy-start(bf16[1,32,1024]{2,1,0:T(8,128)(2,1)} %param.21) | copy-start | bytes 196612
  108.1 75.3 %copy-start.7 = (bf16[1,16,512]{2,1,0:T(8,128)(2,1)S(1)}, bf16[1,16,512]{2,1,0:T(8,128)(2,1)}, u32[]{:S(2)}) copy-start(bf16[1,16,512]{2,1,0:T(8,128)(2,1)} %param.13) | copy-start | bytes 49156
  182.4 84.4 %collective-permute-start = (bf16[96,1024]{1,0:T(8,128)(2,1)S(1)}, bf16[96,1024]{1,0:T(8,128)(2,1)S(1)}, u32[]{:S(2)}, u32[]{:S(2)}) collective-permute-start(bf16[96,1024]{1,0:T(8,128)(2,1)S(1)} %maximum_select_fusion), channel_id=1, source_target_pairs={{0,0},{1,1},{2,32},{3,33},{4,64},{5,65},{6,96},{7,97},{8,128},{9,1... | collective-permute-start | bytes 589832 | tf_op jit(solution)/shard_map/ppermute | solution.py:163
  266.8 0.7 copy-start.4
  268.1 9.2 %copy-start.8 = (s32[1,128,8]{1,2,0:T(8,128)S(1)}, s32[1,128,8]{1,2,0:T(8,128)}, u32[]{:S(2)}) copy-start(s32[1,128,8]{1,2,0:T(8,128)} %param.14) | copy-start | bytes 12292
  282.8 4.2 slice-start.1
  287.1 4.5 %slice-start = ((bf16[32,144,512]{2,1,0:T(8,128)(2,1)}), bf16[32,16,512]{2,1,0:T(8,128)(2,1)S(1)}, s32[]{:S(2)}) async-start(bf16[32,144,512]{2,1,0:T(8,128)(2,1)} %shard_map.123), calls=%async_computation.5 | async-start | bytes 1048576 | tf_op jit(solution)/shard_map/slice | solution.py:261
  293.2 5.5 %copy-start.1 = (f32[4,256,512]{2,1,0:T(8,128)}, f32[4,256,512]{2,1,0:T(8,128)S(1)}, u32[]{:S(2)}) copy-start(f32[4,256,512]{2,1,0:T(8,128)S(1)} %get-tuple-element.22) | copy-start | bytes 6291460
  298.7 5.8 %copy-start = (f32[4,256,4096]{2,1,0:T(8,128)}, f32[4,256,4096]{2,1,0:T(8,128)S(1)}, u32[]{:S(2)}) copy-start(f32[4,256,4096]{2,1,0:T(8,128)S(1)} %get-tuple-element.24) | copy-start | bytes 50331652
  316.1 3.9 copy-start.9
  390.2 3.9 copy-start.11
  390.2 41.0 %all-to-all-start.1 = ((bf16[16,80,1024]{2,1,0:T(8,128)(2,1)}), bf16[16,80,1024]{2,1,0:T(8,128)(2,1)S(1)}, u32[]{:S(2)}, u32[]{:S(2)}) async-start(bf16[16,80,1024]{2,1,0:T(8,128)(2,1)} %bitcast.100), calls=%async_computation.1 | async-start | bytes 5242880 | tf_op jit(solution)/shard_map/all_to_all | solution.py:319
Sparse Core Ops, SparseCore 0:
  49.7 54.8 all-gather.4
  108.2 67.1 all-gather.8
  267.6 79.0 all-gather.6

commit v6 on v3

--- a/solution.py
+++ b/solution.py
@@ -280,7 +280,13 @@
     onehot = (flat_routes[:, None] == jnp.arange(EXPERTS, dtype=jnp.int32)[None, :]).astype(
         jnp.int32
     )
-    slot_rank = jnp.sum(jnp.cumsum(onehot, axis=0) * onehot, axis=1) - 1
+    route_count = flat_routes.shape[0]
+    lower = (
+        jnp.arange(route_count, dtype=jnp.int32)[:, None]
+        >= jnp.arange(route_count, dtype=jnp.int32)[None, :]
+    ).astype(jnp.bfloat16)
+    running = jnp.dot(lower, onehot.astype(jnp.bfloat16), preferred_element_type=jnp.float32)
+    slot_rank = jnp.sum(running.astype(jnp.int32) * onehot, axis=1) - 1
     slot_index = flat_routes * CAP + slot_rank
     source_token = jnp.arange(flat_routes.shape[0], dtype=jnp.int32) // TOP
     outgoing = (

time: 377 us -> 368 us (0.976)
  other arithmetic: 22.3 us -> 13.1 us
    another operation x6 -> x3, other arithmetic: 9.38 us -> 0.24 us
  transfers between devices with their start and end apart: 4 -> 4, of which waited for: 2 -> 2; matrix products, arithmetic and copies ran while one was open for 23% -> 21% of each run, Pallas kernels for 14% -> 14%
where the time goes in v6:
time: 368 us; the launch traced here: 367 us
  waiting for transfers between devices  117 us (32%)
  Pallas kernels  88.7 us (24%)
  local copies, waits for them, and re-layouts  61.2 us (17%)
  blocking collectives  38.3 us (10%)
  matrix products  29 us (8%)
  between operations  14.6 us (4%)
  other arithmetic  13.1 us (4%)
  starting transfers between devices  4.61 us (1%)
    pallas_call x2, Pallas kernels, ring_gather(): pl.pallas_call(kernel, out_shape=jax.ShapeDtypeStruct((tok_count, rows, w...  88.7 us
    all_gather x1, waiting for transfers between devices, gather_rows(): return lax.all_gather(by_columns[None], 'grp', axis=0, tiled=True)  81 us
    all_to_all x1, blocking collectives, local(): lax.all_to_all(outgoing.reshape(grp_count, local_experts * CAP, model_wid...  38.3 us
    all_to_all x1, waiting for transfers between devices, local(): lax.all_to_all(expert_result.reshape(grp_count, local_experts * CAP, mode...  36.4 us
    scatter x1, local copies, waits for them, and re-layouts, local(): outgoing = jnp.zeros((EXPERTS * CAP, model_width), jnp.bfloat16).at[slot_...  13.7 us
    dot_general x2, matrix products, attend(): jnp.einsum('kqn,knd->kqd', probs.astype(jnp.bfloat16), value_heads, prefe...  11.3 us
    slice x3, local copies, waits for them, and re-layouts, attend(): keys_values[:, :key_width].reshape(key_count, KV_HEADS, HEAD_DIM)  8.82 us
  transfers between devices with their start and end apart: 4, of which 2 were waited for; matrix products, arithmetic and copies ran while one was open for 21% of the time, Pallas kernels for 14%

profile of v6, /device:TPU:1, one launch (start us, length us, event | category | flops | bytes accessed | tf_op | source)
XLA Modules:
  0.0 367.1 jit_solution(4036951116094774331)
XLA Ops:
  7.3 0.9 reshape.359
  8.2 0.8 copy.74
  9.0 0.6 reshape.361.x_ref
  9.7 37.6 %shard_map.122 = bf16[32,16,512]{2,1,0:T(8,128)(2,1)} custom-call(bf16[16,512]{1,0:T(8,128)(2,1)} %reshape.361.x_ref), custom_call_target="tpu_custom_call" | custom-call | bytes 1048576 | tf_op jit(solution)/shard_map/pallas_call | solution.py:114
  47.2 1.3 copy.107
  48.6 0.2 reshape.363
  48.9 0.2 reshape.364
  49.1 0.9 pad_maximum_fusion
  50.0 0.7 collective-permute-start
  51.6 81.0 %all-gather.6.cloned.1.call-done = bf16[16384,96]{1,0:T(8,128)(2,1)} async-done(((bf16[1024,96]{1,0:T(8,128)(2,1)}), bf16[16384,96]{1,0:T(8,128)(2,1)}) %all-gather.6.cloned.1.call-update) | async-done | bytes 3145744 | tf_op jit(solution)/shard_map/all_gather | solution.py:149
  132.6 4.1 %fusion.21 = f32[128,1024]{1,0:T(8,128)S(1)} fusion(bf16[16,1024,96]{2,1,0:T(8,128)(2,1)} %bitcast.134, f32[128,16,64]{0,2,1:T(8,128)S(1)} %bitcast.115, f32[16,64]{1,0:T(8,128)S(1)} %mul.203, f32[128]{0:T(128)S(1)} %add_rsqrt_fusion.1), kind=kOutput, calls=%fused_computation.31 | convolution fusion | flops 268828672 | bytes 4198912 | tf_op jit(solution)/shard_map/ngr,gcr->nc/dot_general | solution.py:232
  137.0 0.7 pad_maximum_fusion.3.x_ref
  137.7 51.2 %shard_map.123 = bf16[32,144,512]{2,1,0:T(8,128)(2,1)} custom-call(bf16[144,512]{1,0:T(8,128)(2,1)} %pad_maximum_fusion.3.x_ref), custom_call_target="tpu_custom_call" | custom-call | bytes 9437184 | tf_op jit(solution)/shard_map/pallas_call | solution.py:114
  188.9 4.7 %slice.77 = bf16[32,128,512]{2,1,0:T(8,128)(2,1)} slice(bf16[32,144,512]{2,1,0:T(8,128)(2,1)} %shard_map.123), slice={[0:32], [0:128], [0:512]} | slice | bytes 8388608 | tf_op jit(solution)/shard_map/slice | solution.py:259
  193.5 0.7 copy-done.4
  194.7 0.5 fusion.15
  195.2 3.8 %broadcast_in_dim.44 = pred[128,2,4096]{2,1,0:T(4,128)(4,1)} broadcast(pred[128,4096]{1,0:T(8,128)(4,1)S(1)} %fusion.15), dimensions={0,2} | broadcast | bytes 1572864 | tf_op jit(solution)/shard_map/broadcast_in_dim | solution.py:187
  199.0 5.5 %broadcast_in_dim.49 = pred[256,4096]{1,0:T(8,128)(4,1)S(1)} reshape(pred[128,2,4096]{2,1,0:T(4,128)(4,1)} %broadcast_in_dim.44) | data formatting | bytes 2097152 | tf_op jit(solution)/shard_map/jit(_where)/broadcast_in_dim | solution.py:190
  204.6 0.5 fusion.36
  206.1 4.5 %fusion.54 = (bf16[4096,256]{1,0:T(8,128)(2,1)}, bf16[4096,256]{1,0:T(8,128)(2,1)}) fusion(bf16[4096,512]{1,0:T(8,128)(2,1)} %bitcast.95), kind=kLoop, calls=%fused_computation.104 | loop fusion | bytes 8388608 | tf_op jit(solution)/shard_map/slice | solution.py:176
  210.6 4.1 %copy.85 = bf16[4096,256]{0,1:T(8,128)(2,1)} copy(bf16[4096,256]{1,0:T(8,128)(2,1)} %get-tuple-element.6) | data formatting | bytes 4194304 | tf_op jit(solution)/shard_map/slice | solution.py:176
  214.8 4.2 %copy.87 = bf16[4096,256]{0,1:T(8,128)(2,1)} copy(bf16[4096,256]{1,0:T(8,128)(2,1)} %get-tuple-element.7) | data formatting | bytes 4194304 | tf_op jit(solution)/shard_map/slice | solution.py:178
  218.9 0.7 pad_maximum_fusion.1
  219.6 0.5 multiply_reduce_fusion
  220.1 0.4 copy-done.1
  220.5 3.6 fusion
  224.1 0.6 fusion.16
  224.7 4.4 %fusion.1 = f32[4,256]{1,0:T(4,128)S(1)} fusion(f32[4,256,4096]{2,1,0:T(8,128)S(1)} %get-tuple-element.22, f32[4,256]{1,0:T(4,128)S(1)} %get-tuple-element.15, pred[256,4096]{1,0:T(8,128)(4,1)S(1)} %broadcast_in_dim.49), kind=kLoop, calls=%fused_computation.6 | loop fusion | flops 16776192 | bytes 17833984 | tf_op jit(solution)/shard_map/reduce_sum | solution.py:194
  229.1 0.7 copy-done
  229.9 9.1 %fusion.3 = f32[4,256,64]{1,2,0:T(8,128)S(1)} fusion(bf16[4,4096,64]{1,2,0:T(8,128)(2,1)} %bitcast.107, f32[4,256,4096]{2,1,0:T(8,128)} %copy-done, f32[4,256]{1,0:T(4,128)S(1)} %get-tuple-element.15, pred[256,4096]{1,0:T(8,128)(4,1)S(1)} %broadcast_in_dim.49), kind=kOutput, calls=%fused_computation.8 | convolution fusion | flops 553648128 | bytes 20189184 | tf_op jit(solution)/shard_map/kqn,knd->kqd/dot_general | solution.py:195
  238.9 2.2 fusion.33
  241.5 4.5 %multiply_reduce_fusion.1 = (f32[128]{0:T(128)S(1)}, f32[128,1024]{1,0:T(8,128)S(1)}) fusion(bf16[128,16,32]{0,2,1:T(8,128)(2,1)S(1)} %bitcast.122, bf16[16,1024,96]{2,1,0:T(8,128)(2,1)} %bitcast.135, bf16[1,128,1024]{2,1,0:T(8,128)(2,1)S(1)} %copy-done.3), kind=kOutput, calls=%fused_computation.48 | convolution fusion | flops 134741888 | bytes 4063744 | tf_op jit(solution)/shard_map/ngr,gcr->nc/dot_general | solution.py:270
  246.2 13.7 %scatter_custom_fusion = bf16[1280,1024]{1,0:T(8,128)(2,1)S(1)} fusion(s32[1024]{0:T(1024)S(1)} %bitcast.125, bf16[128,1024]{1,0:T(8,128)(2,1)S(1)} %multiply_convert_fusion, s32[1024]{0:T(1024)S(1)} %broadcast_clamp_fusion.1, bf16[]{:T(256)} %constant.28.clone.1), kind=kCustom, calls=%fused_computation.20 | custom fusion | bytes 2621442 | tf_op jit(solution)/shard_map/scatter | solution.py:295
  259.9 38.3 %all_to_all.10 = bf16[16,80,1024]{2,1,0:T(8,128)(2,1)S(1)} all-to-all(bf16[16,80,1024]{2,1,0:T(8,128)(2,1)S(1)} %bitcast.98), channel_id=1, replica_groups=mesh['grp'=16,'tok'=32] {'grp'}, dimensions={0} | all-to-all | bytes 5242880 | tf_op jit(solution)/shard_map/all_to_all | solution.py:301
  298.2 0.3 copy.93
  298.5 1.8 slice.107
  300.3 2.6 slice.104
  302.9 0.7 copy.105
  303.6 0.2 copy.106
  303.8 2.9 fusion.56
  306.8 1.6 convolution_convert_fusion
  308.3 1.7 copy.96
  310.1 3.9 %all-to-all-start.1 = ((bf16[16,80,1024]{2,1,0:T(8,128)(2,1)}), bf16[16,80,1024]{2,1,0:T(8,128)(2,1)S(1)}, u32[]{:S(2)}, u32[]{:S(2)}) async-start(bf16[16,80,1024]{2,1,0:T(8,128)(2,1)} %bitcast.97), calls=%async_computation.1 | async-start | bytes 5242880 | tf_op jit(solution)/shard_map/all_to_all | solution.py:318
  314.1 0.7 maximum_bitcast_fusion
  314.7 36.4 %all-to-all-done.1 = bf16[16,80,1024]{2,1,0:T(8,128)(2,1)S(1)} async-done(((bf16[16,80,1024]{2,1,0:T(8,128)(2,1)}), bf16[16,80,1024]{2,1,0:T(8,128)(2,1)S(1)}, u32[]{:S(2)}, u32[]{:S(2)}) %all-to-all-start.1) | async-done | bytes 2621472 | tf_op jit(solution)/shard_map/all_to_all | solution.py:318
  351.2 5.4 %gather_fusion = bf16[1024,1024]{1,0:T(8,128)(2,1)} fusion(bf16[1280,1024]{1,0:T(8,128)(2,1)S(1)} %bitcast.93, s32[1024]{0:T(1024)S(1)} %broadcast_clamp_fusion), kind=kCustom, calls=%fused_computation.1 | custom fusion | bytes 4198400 | tf_op jit(solution)/shard_map/gather | solution.py:325
  356.5 2.9 fusion.10
  359.5 0.8 fusion.41
  (80 shorter events, 3.4 us)
Async XLA Ops:
  7.2 42.8 %copy-start.6 = (bf16[1,32,1024]{2,1,0:T(8,128)(2,1)S(1)}, bf16[1,32,1024]{2,1,0:T(8,128)(2,1)}, u32[]{:S(2)}) copy-start(bf16[1,32,1024]{2,1,0:T(8,128)(2,1)} %param.21) | copy-start | bytes 196612
  7.2 42.8 %copy-start.5 = (bf16[1,64,1024]{2,1,0:T(8,128)(2,1)S(1)}, bf16[1,64,1024]{2,1,0:T(8,128)(2,1)}, u32[]{:S(2)}) copy-start(bf16[1,64,1024]{2,1,0:T(8,128)(2,1)} %param.20) | copy-start | bytes 393220
  7.2 43.5 %copy-start.10 = (f32[1024]{0:T(1024)S(1)}, f32[1024]{0:T(1024)}, u32[]{:S(2)}) copy-start(f32[1024]{0:T(1024)} %param.16) | copy-start | bytes 12292
  7.2 43.6 %copy-start.3 = (bf16[1,128,1024]{2,1,0:T(8,128)(2,1)S(1)}, bf16[1,128,1024]{2,1,0:T(8,128)(2,1)}, u32[]{:S(2)}) copy-start(bf16[1,128,1024]{2,1,0:T(8,128)(2,1)} %param.11) | copy-start | bytes 786436
  7.2 43.7 %copy-start.12 = (s32[1,3]{1,0:T(1,128)S(1)}, s32[1,3]{1,0:T(1,128)}, u32[]{:S(2)}) copy-start(s32[1,3]{1,0:T(1,128)} %param.12) | copy-start | bytes 40
  7.2 125.4 %all-gather.6.cloned.1.call-start = ((), (), s32[]{:S(2)}) async-start(), calls=%async_computation.3 | async-start | bytes 4456448 | tf_op jit(solution)/shard_map/all_gather | solution.py:149
  49.9 248.5 %all-gather.4.cloned.1.call-start = ((), (), s32[]{:S(2)}) async-start(), calls=%async_computation.2 | async-start | bytes 6488064 | tf_op jit(solution)/shard_map/all_gather | solution.py:168
  50.0 143.5 %collective-permute-start = (bf16[96,1024]{1,0:T(8,128)(2,1)S(1)}, bf16[96,1024]{1,0:T(8,128)(2,1)S(1)}, u32[]{:S(2)}, u32[]{:S(2)}) collective-permute-start(bf16[96,1024]{1,0:T(8,128)(2,1)S(1)} %pad_maximum_fusion.2), channel_id=1, source_target_pairs={{0,0},{1,1},{2,32},{3,33},{4,64},{5,65},{6,96},{7,97},{8,128},{9,1... | collective-permute-start | bytes 589832 | tf_op jit(solution)/shard_map/ppermute | solution.py:161
  132.6 4.4 %copy-start.7 = (bf16[1,16,512]{2,1,0:T(8,128)(2,1)S(1)}, bf16[1,16,512]{2,1,0:T(8,128)(2,1)}, u32[]{:S(2)}) copy-start(bf16[1,16,512]{2,1,0:T(8,128)(2,1)} %param.13) | copy-start | bytes 49156
  188.8 5.4 %copy-start.8 = (s32[1,128,8]{1,2,0:T(8,128)S(1)}, s32[1,128,8]{1,2,0:T(8,128)}, u32[]{:S(2)}) copy-start(s32[1,128,8]{1,2,0:T(8,128)} %param.14) | copy-start | bytes 12292
  193.5 0.7 copy-start.4
  204.5 1.2 slice-start
  218.9 1.6 copy-start.1
  220.1 4.0 %copy-start.2 = (f32[4,256,512]{2,1,0:T(8,128)}, f32[4,256,512]{2,1,0:T(8,128)S(1)}, u32[]{:S(2)}) copy-start(f32[4,256,512]{2,1,0:T(8,128)S(1)} %get-tuple-element.20) | copy-start | bytes 6291460
  224.1 5.8 %copy-start = (f32[4,256,4096]{2,1,0:T(8,128)}, f32[4,256,4096]{2,1,0:T(8,128)S(1)}, u32[]{:S(2)}) copy-start(f32[4,256,4096]{2,1,0:T(8,128)S(1)} %get-tuple-element.22) | copy-start | bytes 50331652
  241.5 4.6 %copy-start.9 = (f32[1024]{0:T(1024)S(1)}, f32[1024]{0:T(1024)}, u32[]{:S(2)}) copy-start(f32[1024]{0:T(1024)} %param.19) | copy-start | bytes 12292
  310.1 3.9 %copy-start.11 = (f32[1,128,8]{1,2,0:T(8,128)S(1)}, f32[1,128,8]{1,2,0:T(8,128)}, u32[]{:S(2)}) copy-start(f32[1,128,8]{1,2,0:T(8,128)} %param.15) | copy-start | bytes 12292
  310.1 41.1 %all-to-all-start.1 = ((bf16[16,80,1024]{2,1,0:T(8,128)(2,1)}), bf16[16,80,1024]{2,1,0:T(8,128)(2,1)S(1)}, u32[]{:S(2)}, u32[]{:S(2)}) async-start(bf16[16,80,1024]{2,1,0:T(8,128)(2,1)} %bitcast.97), calls=%async_computation.1 | async-start | bytes 5242880 | tf_op jit(solution)/shard_map/all_to_all | solution.py:318
Sparse Core Ops, SparseCore 0:
  50.1 82.4 all-gather.5
  194.3 70.2 all-gather.3

commit v7 on v6

--- a/solution.py
+++ b/solution.py
@@ -224,11 +224,14 @@
     group_share = HEADS // KV_HEADS
     normed = rms_scale(tokens_here, attn_gain).astype(jnp.bfloat16)
     qkv_columns, out_columns = gather_small([w_qkv.T, w_out.T])
-    packed_rows = gather_rows(jnp.concatenate([qkv_columns, out_columns], axis=1))
+    expert_weights = expert_weight_slices(expert_gate_up, expert_down)
+    both_columns = jnp.concatenate([qkv_columns, out_columns], axis=1)
+    probe = expert_weights[0, 0]
+    both_columns = jnp.where(probe != probe, jnp.zeros_like(both_columns), both_columns)
+    packed_rows = gather_rows(both_columns)
     qkv_width = qkv_columns.shape[1]
     qkv_weight = packed_rows[:, :, :qkv_width]
     out_weight = packed_rows[:, :, qkv_width:]
-    expert_weights = expert_weight_slices(expert_gate_up, expert_down)
     projected = jnp.einsum(
         "ngr,gcr->nc",
         normed.reshape(tok_count, qkv_weight.shape[0], qkv_weight.shape[2]),

time: 368 us -> 378 us (1.027)
  Pallas kernels: 88.7 us -> 115 us
  waiting for transfers between devices: 117 us -> 102 us
  matrix products: 29 us -> 24.3 us
    pallas_call x2, Pallas kernels: 88.7 us -> 115 us  [ring_gather(): pl.pallas_call(kernel, out_shape=jax.ShapeDtypeStruct((tok_count, rows, w...]
    all_gather x1, waiting for transfers between devices: 81 us -> 65.3 us  [gather_rows(): return lax.all_gather(by_columns[None], 'grp', axis=0, tiled=True)]
  transfers between devices with their start and end apart: 4 -> 4, of which waited for: 2 -> 2; matrix products, arithmetic and copies ran while one was open for 21% -> 18% of each run, Pallas kernels for 14% -> 17%
where the time goes in v7:
time: 378 us; the launch traced here: 377 us
  Pallas kernels  115 us (30%)
  waiting for transfers between devices  102 us (27%)
  local copies, waits for them, and re-layouts  61.5 us (16%)
  blocking collectives  40.6 us (11%)
  matrix products  24.3 us (6%)
  between operations  15.9 us (4%)
  other arithmetic  13.4 us (4%)
  starting transfers between devices  4.61 us (1%)
    pallas_call x2, Pallas kernels, ring_gather(): pl.pallas_call(kernel, out_shape=jax.ShapeDtypeStruct((tok_count, rows, w...  115 us
    all_gather x1, waiting for transfers between devices, gather_rows(): return lax.all_gather(by_columns[None], 'grp', axis=0, tiled=True)  65.3 us
    all_to_all x1, blocking collectives, local(): lax.all_to_all(outgoing.reshape(grp_count, local_experts * CAP, model_wid...  40.6 us
    all_to_all x1, waiting for transfers between devices, local(): lax.all_to_all(expert_result.reshape(grp_count, local_experts * CAP, mode...  36.4 us
    scatter x1, local copies, waits for them, and re-layouts, local(): outgoing = jnp.zeros((EXPERTS * CAP, model_width), jnp.bfloat16).at[slot_...  13.5 us
    dot_general x2, matrix products, attend(): jnp.einsum('kqn,knd->kqd', probs.astype(jnp.bfloat16), value_heads, prefe...  11.3 us
    slice x3, local copies, waits for them, and re-layouts, attend(): keys_values[:, :key_width].reshape(key_count, KV_HEADS, HEAD_DIM)  8.78 us
  transfers between devices with their start and end apart: 4, of which 2 were waited for; matrix products, arithmetic and copies ran while one was open for 18% of the time, Pallas kernels for 17%

profile of v7, /device:TPU:1, one launch (start us, length us, event | category | flops | bytes accessed | tf_op | source)
XLA Modules:
  0.0 376.7 jit_solution(7090822398873531117)
XLA Ops:
  7.2 1.0 pad_maximum_fusion.1
  8.2 0.7 collective-permute-start
  8.9 0.8 reshape.387
  9.7 0.8 copy.95
  10.6 0.6 reshape.389.x_ref
  11.2 63.6 %shard_map.122 = bf16[32,16,512]{2,1,0:T(8,128)(2,1)} custom-call(bf16[16,512]{1,0:T(8,128)(2,1)} %reshape.389.x_ref), custom_call_target="tpu_custom_call" | custom-call | bytes 1048576 | tf_op jit(solution)/shard_map/pallas_call | solution.py:114
  74.8 1.3 copy.121
  76.2 0.2 concatenate.41
  76.7 0.6 slice.93
  78.7 0.8 copy.96
  80.5 65.3 %all-gather.3.cloned.1.call-done = bf16[16,1024,96]{1,2,0:T(8,128)(2,1)} async-done(((bf16[1,1024,96]{1,2,0:T(8,128)(2,1)}), bf16[16,1024,96]{1,2,0:T(8,128)(2,1)}) %all-gather.3.cloned.1.call-update) | async-done | bytes 3145744 | tf_op jit(solution)/shard_map/all_gather | solution.py:149
  145.8 2.3 fusion.19
  148.4 0.7 pad_maximum_fusion.2.x_ref
  149.1 51.0 %shard_map.123 = bf16[32,144,512]{2,1,0:T(8,128)(2,1)} custom-call(bf16[144,512]{1,0:T(8,128)(2,1)} %pad_maximum_fusion.2.x_ref), custom_call_target="tpu_custom_call" | custom-call | bytes 9437184 | tf_op jit(solution)/shard_map/pallas_call | solution.py:114
  200.1 4.7 %slice.81 = bf16[32,128,512]{2,1,0:T(8,128)(2,1)} slice(bf16[32,144,512]{2,1,0:T(8,128)(2,1)} %shard_map.123), slice={[0:32], [0:128], [0:512]} | slice | bytes 8388608 | tf_op jit(solution)/shard_map/slice | solution.py:262
  205.3 0.5 fusion.13
  205.8 3.8 %broadcast_in_dim.44 = pred[128,2,4096]{2,1,0:T(4,128)(4,1)} broadcast(pred[128,4096]{1,0:T(8,128)(4,1)S(1)} %fusion.13), dimensions={0,2} | broadcast | bytes 1572864 | tf_op jit(solution)/shard_map/broadcast_in_dim | solution.py:187
  209.6 5.4 %broadcast_in_dim.45 = pred[256,4096]{1,0:T(8,128)(4,1)S(1)} reshape(pred[128,2,4096]{2,1,0:T(4,128)(4,1)} %broadcast_in_dim.44) | data formatting | bytes 2097152 | tf_op jit(solution)/shard_map/jit(_where)/broadcast_in_dim | solution.py:190
  215.1 0.5 fusion.29
  216.6 4.5 %fusion.48 = (bf16[4096,256]{1,0:T(8,128)(2,1)}, bf16[4096,256]{1,0:T(8,128)(2,1)}) fusion(bf16[4096,512]{1,0:T(8,128)(2,1)} %bitcast.95), kind=kLoop, calls=%fused_computation.103 | loop fusion | bytes 8388608 | tf_op jit(solution)/shard_map/slice | solution.py:176
  221.1 4.1 %copy.105 = bf16[4096,256]{0,1:T(8,128)(2,1)} copy(bf16[4096,256]{1,0:T(8,128)(2,1)} %get-tuple-element.6) | data formatting | bytes 4194304 | tf_op jit(solution)/shard_map/slice | solution.py:176
  225.2 4.1 %copy.107 = bf16[4096,256]{0,1:T(8,128)(2,1)} copy(bf16[4096,256]{1,0:T(8,128)(2,1)} %get-tuple-element.7) | data formatting | bytes 4194304 | tf_op jit(solution)/shard_map/slice | solution.py:178
  229.3 0.7 pad_maximum_fusion
  230.0 0.5 multiply_reduce_fusion
  230.5 0.4 copy-done.1
  230.9 3.6 fusion
  234.6 0.6 fusion.14
  235.1 4.4 %fusion.1 = f32[4,256]{1,0:T(4,128)S(1)} fusion(f32[4,256,4096]{2,1,0:T(8,128)S(1)} %get-tuple-element.22, f32[4,256]{1,0:T(4,128)S(1)} %get-tuple-element.15, pred[256,4096]{1,0:T(8,128)(4,1)S(1)} %broadcast_in_dim.45), kind=kLoop, calls=%fused_computation.6 | loop fusion | flops 16776192 | bytes 17833984 | tf_op jit(solution)/shard_map/reduce_sum | solution.py:194
  239.6 0.8 copy-done
  240.3 9.1 %fusion.3 = f32[4,256,64]{1,2,0:T(8,128)S(1)} fusion(bf16[4,4096,64]{1,2,0:T(8,128)(2,1)} %bitcast.107, f32[4,256,4096]{2,1,0:T(8,128)} %copy-done, f32[4,256]{1,0:T(4,128)S(1)} %get-tuple-element.15, pred[256,4096]{1,0:T(8,128)(4,1)S(1)} %broadcast_in_dim.45), kind=kOutput, calls=%fused_computation.8 | convolution fusion | flops 553648128 | bytes 20189184 | tf_op jit(solution)/shard_map/kqn,knd->kqd/dot_general | solution.py:195
  249.4 2.2 fusion.26
  252.0 1.7 multiply_reduce_fusion.1
  253.8 13.5 %scatter_custom_fusion = bf16[1280,1024]{1,0:T(8,128)(2,1)S(1)} fusion(s32[1024]{0:T(1024)S(1)} %bitcast.125, bf16[128,1024]{1,0:T(8,128)(2,1)S(1)} %multiply_convert_fusion, s32[1024]{0:T(1024)S(1)} %broadcast_clamp_fusion.1, bf16[]{:T(256)} %constant.27.clone.1), kind=kCustom, calls=%fused_computation.18 | custom fusion | bytes 2621442 | tf_op jit(solution)/shard_map/scatter | solution.py:298
  267.3 40.6 %all_to_all.10 = bf16[16,80,1024]{2,1,0:T(8,128)(2,1)S(1)} all-to-all(bf16[16,80,1024]{2,1,0:T(8,128)(2,1)S(1)} %bitcast.98), channel_id=1, replica_groups=mesh['grp'=16,'tok'=32] {'grp'}, dimensions={0} | all-to-all | bytes 5242880 | tf_op jit(solution)/shard_map/all_to_all | solution.py:304
  307.9 0.3 copy.112
  308.2 1.8 slice.112
  309.9 2.6 slice.109
  312.6 0.7 copy.119
  313.3 0.2 copy.120
  313.5 2.9 fusion.50
  316.4 1.6 convolution_convert_fusion
  318.0 1.7 copy.115
  319.7 3.9 %all-to-all-start.1 = ((bf16[16,80,1024]{2,1,0:T(8,128)(2,1)}), bf16[16,80,1024]{2,1,0:T(8,128)(2,1)S(1)}, u32[]{:S(2)}, u32[]{:S(2)}) async-start(bf16[16,80,1024]{2,1,0:T(8,128)(2,1)} %bitcast.97), calls=%async_computation.1 | async-start | bytes 5242880 | tf_op jit(solution)/shard_map/all_to_all | solution.py:321
  323.7 0.7 maximum_bitcast_fusion
  324.4 36.4 %all-to-all-done.1 = bf16[16,80,1024]{2,1,0:T(8,128)(2,1)S(1)} async-done(((bf16[16,80,1024]{2,1,0:T(8,128)(2,1)}), bf16[16,80,1024]{2,1,0:T(8,128)(2,1)S(1)}, u32[]{:S(2)}, u32[]{:S(2)}) %all-to-all-start.1) | async-done | bytes 2621472 | tf_op jit(solution)/shard_map/all_to_all | solution.py:321
  360.8 5.4 %gather_fusion = bf16[1024,1024]{1,0:T(8,128)(2,1)} fusion(bf16[1280,1024]{1,0:T(8,128)(2,1)S(1)} %bitcast.93, s32[1024]{0:T(1024)S(1)} %broadcast_clamp_fusion), kind=kCustom, calls=%fused_computation.1 | custom fusion | bytes 4198400 | tf_op jit(solution)/shard_map/gather | solution.py:328
  366.2 2.9 fusion.6
  369.1 0.8 fusion.35
  (78 shorter events, 3.7 us)
Async XLA Ops:
  7.2 72.4 %copy-start.8 = (f32[1024]{0:T(1024)S(1)}, f32[1024]{0:T(1024)}, u32[]{:S(2)}) copy-start(f32[1024]{0:T(1024)} %param.16) | copy-start | bytes 12292
  7.2 72.5 %copy-start.3 = (bf16[1,128,1024]{2,1,0:T(8,128)(2,1)S(1)}, bf16[1,128,1024]{2,1,0:T(8,128)(2,1)}, u32[]{:S(2)}) copy-start(bf16[1,128,1024]{2,1,0:T(8,128)(2,1)} %param.11) | copy-start | bytes 786436
  7.2 138.6 %all-gather.3.cloned.1.call-start = ((), (), s32[]{:S(2)}) async-start(), calls=%async_computation.2 | async-start | bytes 3342336 | tf_op jit(solution)/shard_map/all_gather | solution.py:149
  8.2 71.6 %copy-start.10 = (s32[1,3]{1,0:T(1,128)S(1)}, s32[1,3]{1,0:T(1,128)}, u32[]{:S(2)}) copy-start(s32[1,3]{1,0:T(1,128)} %param.12) | copy-start | bytes 40
  8.2 68.4 %collective-permute-start = (bf16[96,1024]{1,0:T(8,128)(2,1)S(1)}, bf16[96,1024]{1,0:T(8,128)(2,1)S(1)}, u32[]{:S(2)}, u32[]{:S(2)}) collective-permute-start(bf16[96,1024]{1,0:T(8,128)(2,1)S(1)} %pad_maximum_fusion.1), channel_id=1, source_target_pairs={{0,0},{1,1},{2,32},{3,33},{4,64},{5,65},{6,96},{7,97},{8,128},{9,1... | collective-permute-start | bytes 589832 | tf_op jit(solution)/shard_map/ppermute | solution.py:161
  76.6 71.4 %copy-start.4 = (bf16[96,1024]{1,0:T(8,128)(2,1)}, bf16[96,1024]{1,0:T(8,128)(2,1)S(1)}, u32[]{:S(2)}) copy-start(bf16[96,1024]{1,0:T(8,128)(2,1)S(1)} %collective-permute-done) | copy-start | bytes 589828
  79.5 228.6 %all-gather.5.cloned.1.call-start = ((), (), s32[]{:S(2)}) async-start(), calls=%async_computation.3 | async-start | bytes 6488064 | tf_op jit(solution)/shard_map/all_gather | solution.py:168
  79.7 68.7 %copy-start.5 = (bf16[1,16,512]{2,1,0:T(8,128)(2,1)S(1)}, bf16[1,16,512]{2,1,0:T(8,128)(2,1)}, u32[]{:S(2)}) copy-start(bf16[1,16,512]{2,1,0:T(8,128)(2,1)} %param.13) | copy-start | bytes 49156
  200.1 4.7 %copy-start.6 = (s32[1,128,8]{1,2,0:T(8,128)S(1)}, s32[1,128,8]{1,2,0:T(8,128)}, u32[]{:S(2)}) copy-start(s32[1,128,8]{1,2,0:T(8,128)} %param.14) | copy-start | bytes 12292
  215.0 1.2 slice-start
  229.3 1.6 copy-start.1
  230.5 4.0 %copy-start.2 = (f32[4,256,512]{2,1,0:T(8,128)}, f32[4,256,512]{2,1,0:T(8,128)S(1)}, u32[]{:S(2)}) copy-start(f32[4,256,512]{2,1,0:T(8,128)S(1)} %get-tuple-element.20) | copy-start | bytes 6291460
  234.5 5.8 %copy-start = (f32[4,256,4096]{2,1,0:T(8,128)}, f32[4,256,4096]{2,1,0:T(8,128)S(1)}, u32[]{:S(2)}) copy-start(f32[4,256,4096]{2,1,0:T(8,128)S(1)} %get-tuple-element.22) | copy-start | bytes 50331652
  249.4 4.2 %copy-start.7 = (f32[1024]{0:T(1024)S(1)}, f32[1024]{0:T(1024)}, u32[]{:S(2)}) copy-start(f32[1024]{0:T(1024)} %param.19) | copy-start | bytes 12292
  319.7 3.9 %copy-start.9 = (f32[1,128,8]{1,2,0:T(8,128)S(1)}, f32[1,128,8]{1,2,0:T(8,128)}, u32[]{:S(2)}) copy-start(f32[1,128,8]{1,2,0:T(8,128)} %param.15) | copy-start | bytes 12292
  319.7 41.1 %all-to-all-start.1 = ((bf16[16,80,1024]{2,1,0:T(8,128)(2,1)}), bf16[16,80,1024]{2,1,0:T(8,128)(2,1)S(1)}, u32[]{:S(2)}, u32[]{:S(2)}) async-start(bf16[16,80,1024]{2,1,0:T(8,128)(2,1)} %bitcast.97), calls=%async_computation.1 | async-start | bytes 5242880 | tf_op jit(solution)/shard_map/all_to_all | solution.py:321
Sparse Core Ops, SparseCore 0:
  79.6 66.0 all-gather.2
  204.9 69.8 all-gather.4

commit v8 on v6

--- a/solution.py
+++ b/solution.py
@@ -182,11 +182,7 @@
         * score_scale
     )
     if allowed is not None:
-        row_count = grouped.shape[1]
-        share = row_count // allowed.shape[0]
-        mask = jnp.broadcast_to(allowed[:, None, :], (allowed.shape[0], share, key_count)).reshape(
-            row_count, key_count
-        )
+        mask = allowed
         scores = jnp.where(mask[None], scores, big_negative)
     new_best = jnp.maximum(best, jnp.max(scores, axis=-1))
     factor = jnp.exp(best - new_best)
@@ -261,8 +257,10 @@
     carry = attend(start_carry, grouped, prefix_all, None)
     key_index = jnp.arange(piece.shape[0], dtype=jnp.int32)
     key_segment, key_offset = request_layout(group_lengths, key_index)
-    earlier = key_index[None, :] <= token_index[:, None]
-    same_request = key_segment[None, :] == segment[:, None]
+    row_token = jnp.repeat(token_index, group_share)
+    row_segment = jnp.repeat(segment, group_share)
+    earlier = key_index[None, :] <= row_token[:, None]
+    same_request = key_segment[None, :] == row_segment[:, None]
     carry = attend(carry, grouped, piece, earlier & same_request & (key_index[None, :] >= 0))
     best, total, mixed = carry
     attended = (mixed / total[..., None]).reshape(KV_HEADS, tok_count, group_share, HEAD_DIM)

time: 368 us -> 359 us (0.976)
  local copies, waits for them, and re-layouts: 61.2 us -> 52.1 us
    broadcast_in_dim x2, local copies, waits for them, and re-layouts: 9.29 us -> 0.15 us  [the longest x1 0.07 us: local(): row_token = jnp.repeat(token_index, group_share)]
  transfers between devices with their start and end apart: 4 -> 4, of which waited for: 2 -> 2; matrix products, arithmetic and copies ran while one was open for 21% -> 19% of each run, Pallas kernels for 14% -> 14%
where the time goes in v8:
time: 359 us
  waiting for transfers between devices  117 us (33%)
  Pallas kernels  88.7 us (25%)
  local copies, waits for them, and re-layouts  52.1 us (15%)
  blocking collectives  38.3 us (11%)
  matrix products  29.1 us (8%)
  between operations  14.6 us (4%)
  other arithmetic  13.6 us (4%)
  starting transfers between devices  4.61 us (1%)
    pallas_call x2, Pallas kernels, ring_gather(): pl.pallas_call(kernel, out_shape=jax.ShapeDtypeStruct((tok_count, rows, w...  88.7 us
    all_gather x1, waiting for transfers between devices, gather_rows(): return lax.all_gather(by_columns[None], 'grp', axis=0, tiled=True)  81 us
    all_to_all x1, blocking collectives, local(): lax.all_to_all(outgoing.reshape(grp_count, local_experts * CAP, model_wid...  38.3 us
    all_to_all x1, waiting for transfers between devices, local(): lax.all_to_all(expert_result.reshape(grp_count, local_experts * CAP, mode...  36.4 us
    scatter x1, local copies, waits for them, and re-layouts, local(): outgoing = jnp.zeros((EXPERTS * CAP, model_width), jnp.bfloat16).at[slot_...  13.5 us
    dot_general x2, matrix products, attend(): jnp.einsum('kqn,knd->kqd', probs.astype(jnp.bfloat16), value_heads, prefe...  11.3 us
    slice x3, local copies, waits for them, and re-layouts, attend(): keys_values[:, :key_width].reshape(key_count, KV_HEADS, HEAD_DIM)  8.76 us
  transfers between devices with their start and end apart: 4, of which 2 were waited for; matrix products, arithmetic and copies ran while one was open for 19% of the time, Pallas kernels for 14%

profile of v8, /device:TPU:1, one launch (start us, length us, event | category | flops | bytes accessed | tf_op | source)
XLA Modules:
  0.0 358.5 jit_solution(10667341691237975032)
XLA Ops:
  7.3 0.9 reshape.371
  8.2 0.8 copy.74
  9.0 0.6 reshape.373.x_ref
  9.7 37.6 %shard_map.122 = bf16[32,16,512]{2,1,0:T(8,128)(2,1)} custom-call(bf16[16,512]{1,0:T(8,128)(2,1)} %reshape.373.x_ref), custom_call_target="tpu_custom_call" | custom-call | bytes 1048576 | tf_op jit(solution)/shard_map/pallas_call | solution.py:114
  47.2 1.3 copy.107
  48.6 0.2 reshape.375
  48.9 0.2 reshape.376
  49.1 0.9 pad_maximum_fusion
  50.0 0.7 collective-permute-start
  50.9 0.2 reduce-window.4
  51.6 81.0 %all-gather.6.cloned.1.call-done = bf16[16384,96]{1,0:T(8,128)(2,1)} async-done(((bf16[1024,96]{1,0:T(8,128)(2,1)}), bf16[16384,96]{1,0:T(8,128)(2,1)}) %all-gather.6.cloned.1.call-update) | async-done | bytes 3145744 | tf_op jit(solution)/shard_map/all_gather | solution.py:149
  132.6 4.1 %fusion.21 = f32[128,1024]{1,0:T(8,128)S(1)} fusion(bf16[16,1024,96]{2,1,0:T(8,128)(2,1)} %bitcast.134, f32[128,16,64]{0,2,1:T(8,128)S(1)} %bitcast.115, f32[16,64]{1,0:T(8,128)S(1)} %mul.203, f32[128]{0:T(128)S(1)} %add_rsqrt_fusion.1), kind=kOutput, calls=%fused_computation.31 | convolution fusion | flops 268828672 | bytes 4198912 | tf_op jit(solution)/shard_map/ngr,gcr->nc/dot_general | solution.py:228
  137.0 0.7 pad_maximum_fusion.3.x_ref
  137.7 51.2 %shard_map.123 = bf16[32,144,512]{2,1,0:T(8,128)(2,1)} custom-call(bf16[144,512]{1,0:T(8,128)(2,1)} %pad_maximum_fusion.3.x_ref), custom_call_target="tpu_custom_call" | custom-call | bytes 9437184 | tf_op jit(solution)/shard_map/pallas_call | solution.py:114
  188.9 4.7 %slice.77 = bf16[32,128,512]{2,1,0:T(8,128)(2,1)} slice(bf16[32,144,512]{2,1,0:T(8,128)(2,1)} %shard_map.123), slice={[0:32], [0:128], [0:512]} | slice | bytes 8388608 | tf_op jit(solution)/shard_map/slice | solution.py:255
  193.5 0.7 copy-done.4
  195.2 0.5 fusion.36
  195.8 1.0 fusion.11
  197.1 0.2 copy.79
  197.8 4.5 %fusion.54 = (bf16[4096,256]{1,0:T(8,128)(2,1)}, bf16[4096,256]{1,0:T(8,128)(2,1)}) fusion(bf16[4096,512]{1,0:T(8,128)(2,1)} %bitcast.95), kind=kLoop, calls=%fused_computation.104 | loop fusion | bytes 8388608 | tf_op jit(solution)/shard_map/slice | solution.py:176
  202.3 4.1 %copy.85 = bf16[4096,256]{0,1:T(8,128)(2,1)} copy(bf16[4096,256]{1,0:T(8,128)(2,1)} %get-tuple-element.6) | data formatting | bytes 4194304 | tf_op jit(solution)/shard_map/slice | solution.py:176
  206.4 4.1 %copy.87 = bf16[4096,256]{0,1:T(8,128)(2,1)} copy(bf16[4096,256]{1,0:T(8,128)(2,1)} %get-tuple-element.7) | data formatting | bytes 4194304 | tf_op jit(solution)/shard_map/slice | solution.py:178
  210.5 0.7 pad_maximum_fusion.1
  211.2 0.5 multiply_reduce_fusion
  211.7 0.4 copy-done.1
  212.1 3.6 fusion
  215.8 0.6 fusion.16
  216.3 4.4 %fusion.1 = f32[4,256]{1,0:T(4,128)S(1)} fusion(f32[4,256,4096]{2,1,0:T(8,128)S(1)} %get-tuple-element.22, f32[4,256]{1,0:T(4,128)S(1)} %get-tuple-element.15, pred[256,4096]{1,0:T(8,128)(4,1)S(1)} %fusion.11), kind=kLoop, calls=%fused_computation.6 | loop fusion | flops 16776192 | bytes 17833984 | tf_op jit(solution)/shard_map/reduce_sum | solution.py:190
  220.7 0.7 copy-done
  221.5 9.1 %fusion.3 = f32[4,256,64]{1,2,0:T(8,128)S(1)} fusion(bf16[4,4096,64]{1,2,0:T(8,128)(2,1)} %bitcast.107, f32[4,256,4096]{2,1,0:T(8,128)} %copy-done, f32[4,256]{1,0:T(4,128)S(1)} %get-tuple-element.15, pred[256,4096]{1,0:T(8,128)(4,1)S(1)} %fusion.11), kind=kOutput, calls=%fused_computation.8 | convolution fusion | flops 553648128 | bytes 20189184 | tf_op jit(solution)/shard_map/kqn,knd->kqd/dot_general | solution.py:191
  230.6 2.2 fusion.33
  233.2 4.5 %multiply_reduce_fusion.1 = (f32[128]{0:T(128)S(1)}, f32[128,1024]{1,0:T(8,128)S(1)}) fusion(bf16[128,16,32]{0,2,1:T(8,128)(2,1)S(1)} %bitcast.122, bf16[16,1024,96]{2,1,0:T(8,128)(2,1)} %bitcast.135, bf16[1,128,1024]{2,1,0:T(8,128)(2,1)S(1)} %copy-done.3), kind=kOutput, calls=%fused_computation.48 | convolution fusion | flops 134741888 | bytes 4063744 | tf_op jit(solution)/shard_map/ngr,gcr->nc/dot_general | solution.py:268
  237.8 13.5 %scatter_custom_fusion = bf16[1280,1024]{1,0:T(8,128)(2,1)S(1)} fusion(s32[1024]{0:T(1024)S(1)} %bitcast.125, bf16[128,1024]{1,0:T(8,128)(2,1)S(1)} %multiply_convert_fusion, s32[1024]{0:T(1024)S(1)} %broadcast_clamp_fusion.1, bf16[]{:T(256)} %constant.28.clone.1), kind=kCustom, calls=%fused_computation.22 | custom fusion | bytes 2621442 | tf_op jit(solution)/shard_map/scatter | solution.py:293
  251.4 38.3 %all_to_all.10 = bf16[16,80,1024]{2,1,0:T(8,128)(2,1)S(1)} all-to-all(bf16[16,80,1024]{2,1,0:T(8,128)(2,1)S(1)} %bitcast.98), channel_id=1, replica_groups=mesh['grp'=16,'tok'=32] {'grp'}, dimensions={0} | all-to-all | bytes 5242880 | tf_op jit(solution)/shard_map/all_to_all | solution.py:299
  289.6 0.3 copy.93
  289.9 1.8 slice.107
  291.7 2.6 slice.104
  294.3 0.7 copy.105
  295.1 0.2 copy.106
  295.3 2.9 fusion.56
  298.2 1.6 convolution_convert_fusion
  299.8 1.7 copy.96
  301.5 3.9 %all-to-all-start.1 = ((bf16[16,80,1024]{2,1,0:T(8,128)(2,1)}), bf16[16,80,1024]{2,1,0:T(8,128)(2,1)S(1)}, u32[]{:S(2)}, u32[]{:S(2)}) async-start(bf16[16,80,1024]{2,1,0:T(8,128)(2,1)} %bitcast.97), calls=%async_computation.1 | async-start | bytes 5242880 | tf_op jit(solution)/shard_map/all_to_all | solution.py:316
  305.5 0.7 maximum_bitcast_fusion
  306.2 36.4 %all-to-all-done.1 = bf16[16,80,1024]{2,1,0:T(8,128)(2,1)S(1)} async-done(((bf16[16,80,1024]{2,1,0:T(8,128)(2,1)}), bf16[16,80,1024]{2,1,0:T(8,128)(2,1)S(1)}, u32[]{:S(2)}, u32[]{:S(2)}) %all-to-all-start.1) | async-done | bytes 2621472 | tf_op jit(solution)/shard_map/all_to_all | solution.py:316
  342.6 5.4 %gather_fusion = bf16[1024,1024]{1,0:T(8,128)(2,1)} fusion(bf16[1280,1024]{1,0:T(8,128)(2,1)S(1)} %bitcast.93, s32[1024]{0:T(1024)S(1)} %broadcast_clamp_fusion), kind=kCustom, calls=%fused_computation.1 | custom fusion | bytes 4198400 | tf_op jit(solution)/shard_map/gather | solution.py:323
  348.0 2.9 fusion.10
  350.9 0.8 fusion.41
  (82 shorter events, 3.5 us)
Async XLA Ops:
  7.2 42.8 %copy-start.6 = (bf16[1,32,1024]{2,1,0:T(8,128)(2,1)S(1)}, bf16[1,32,1024]{2,1,0:T(8,128)(2,1)}, u32[]{:S(2)}) copy-start(bf16[1,32,1024]{2,1,0:T(8,128)(2,1)} %param.21) | copy-start | bytes 196612
  7.2 42.8 %copy-start.5 = (bf16[1,64,1024]{2,1,0:T(8,128)(2,1)S(1)}, bf16[1,64,1024]{2,1,0:T(8,128)(2,1)}, u32[]{:S(2)}) copy-start(bf16[1,64,1024]{2,1,0:T(8,128)(2,1)} %param.20) | copy-start | bytes 393220
  7.2 43.5 %copy-start.10 = (f32[1024]{0:T(1024)S(1)}, f32[1024]{0:T(1024)}, u32[]{:S(2)}) copy-start(f32[1024]{0:T(1024)} %param.16) | copy-start | bytes 12292
  7.2 43.6 %copy-start.3 = (bf16[1,128,1024]{2,1,0:T(8,128)(2,1)S(1)}, bf16[1,128,1024]{2,1,0:T(8,128)(2,1)}, u32[]{:S(2)}) copy-start(bf16[1,128,1024]{2,1,0:T(8,128)(2,1)} %param.11) | copy-start | bytes 786436
  7.2 43.7 %copy-start.12 = (s32[1,3]{1,0:T(1,128)S(1)}, s32[1,3]{1,0:T(1,128)}, u32[]{:S(2)}) copy-start(s32[1,3]{1,0:T(1,128)} %param.12) | copy-start | bytes 40
  7.2 125.4 %all-gather.6.cloned.1.call-start = ((), (), s32[]{:S(2)}) async-start(), calls=%async_computation.3 | async-start | bytes 4456448 | tf_op jit(solution)/shard_map/all_gather | solution.py:149
  49.9 240.0 %all-gather.4.cloned.1.call-start = ((), (), s32[]{:S(2)}) async-start(), calls=%async_computation.2 | async-start | bytes 6488064 | tf_op jit(solution)/shard_map/all_gather | solution.py:168
  50.0 143.5 %collective-permute-start = (bf16[96,1024]{1,0:T(8,128)(2,1)S(1)}, bf16[96,1024]{1,0:T(8,128)(2,1)S(1)}, u32[]{:S(2)}, u32[]{:S(2)}) collective-permute-start(bf16[96,1024]{1,0:T(8,128)(2,1)S(1)} %pad_maximum_fusion.2), channel_id=1, source_target_pairs={{0,0},{1,1},{2,32},{3,33},{4,64},{5,65},{6,96},{7,97},{8,128},{9,1... | collective-permute-start | bytes 589832 | tf_op jit(solution)/shard_map/ppermute | solution.py:161
  132.6 4.4 %copy-start.7 = (bf16[1,16,512]{2,1,0:T(8,128)(2,1)S(1)}, bf16[1,16,512]{2,1,0:T(8,128)(2,1)}, u32[]{:S(2)}) copy-start(bf16[1,16,512]{2,1,0:T(8,128)(2,1)} %param.13) | copy-start | bytes 49156
  188.9 5.4 %copy-start.8 = (s32[1,128,8]{1,2,0:T(8,128)S(1)}, s32[1,128,8]{1,2,0:T(8,128)}, u32[]{:S(2)}) copy-start(s32[1,128,8]{1,2,0:T(8,128)} %param.14) | copy-start | bytes 12292
  193.5 0.7 copy-start.4
  195.2 2.2 slice-start
  210.5 1.6 copy-start.1
  211.7 4.0 %copy-start.2 = (f32[4,256,512]{2,1,0:T(8,128)}, f32[4,256,512]{2,1,0:T(8,128)S(1)}, u32[]{:S(2)}) copy-start(f32[4,256,512]{2,1,0:T(8,128)S(1)} %get-tuple-element.20) | copy-start | bytes 6291460
  215.7 5.7 %copy-start = (f32[4,256,4096]{2,1,0:T(8,128)}, f32[4,256,4096]{2,1,0:T(8,128)S(1)}, u32[]{:S(2)}) copy-start(f32[4,256,4096]{2,1,0:T(8,128)S(1)} %get-tuple-element.22) | copy-start | bytes 50331652
  233.1 4.6 %copy-start.9 = (f32[1024]{0:T(1024)S(1)}, f32[1024]{0:T(1024)}, u32[]{:S(2)}) copy-start(f32[1024]{0:T(1024)} %param.19) | copy-start | bytes 12292
  301.5 3.9 %copy-start.11 = (f32[1,128,8]{1,2,0:T(8,128)S(1)}, f32[1,128,8]{1,2,0:T(8,128)}, u32[]{:S(2)}) copy-start(f32[1,128,8]{1,2,0:T(8,128)} %param.15) | copy-start | bytes 12292
  301.5 41.1 %all-to-all-start.1 = ((bf16[16,80,1024]{2,1,0:T(8,128)(2,1)}), bf16[16,80,1024]{2,1,0:T(8,128)(2,1)S(1)}, u32[]{:S(2)}, u32[]{:S(2)}) async-start(bf16[16,80,1024]{2,1,0:T(8,128)(2,1)} %bitcast.97), calls=%async_computation.1 | async-start | bytes 5242880 | tf_op jit(solution)/shard_map/all_to_all | solution.py:316
Sparse Core Ops, SparseCore 0:
  50.1 82.4 all-gather.5
  194.3 70.4 all-gather.3

commit v9 on v8

--- a/solution.py
+++ b/solution.py
@@ -287,11 +287,16 @@
     slot_rank = jnp.sum(running.astype(jnp.int32) * onehot, axis=1) - 1
     slot_index = flat_routes * CAP + slot_rank
     source_token = jnp.arange(flat_routes.shape[0], dtype=jnp.int32) // TOP
-    outgoing = (
-        jnp.zeros((EXPERTS * CAP, model_width), jnp.bfloat16)
-        .at[slot_index]
-        .set(moe_in[source_token])
-    )
+    slot_of_route = (
+        slot_index[None, :] == jnp.arange(EXPERTS * CAP, dtype=jnp.int32)[:, None]
+    ).astype(jnp.bfloat16)
+    token_of_route = (
+        source_token[:, None] == jnp.arange(tok_count, dtype=jnp.int32)[None, :]
+    ).astype(jnp.bfloat16)
+    slot_token = jnp.dot(slot_of_route, token_of_route, preferred_element_type=jnp.float32)
+    outgoing = jnp.dot(
+        slot_token.astype(jnp.bfloat16), moe_in, preferred_element_type=jnp.float32
+    ).astype(jnp.bfloat16)
     grp_count = lax.axis_size("grp")
     local_experts = EXPERTS // grp_count
     full = expert_weights_full(expert_weights, piece)

time: 359 us -> 348 us (0.969)
  local copies, waits for them, and re-layouts: 52.1 us -> 38.6 us
    scatter x1 -> x0, local copies, waits for them, and re-layouts: 13.5 us -> none  [local(): outgoing = jnp.zeros((EXPERTS * CAP, model_width), jnp.bfloat16).at[slot_...]
  transfers between devices with their start and end apart: 4 -> 4, of which waited for: 2 -> 2; matrix products, arithmetic and copies ran while one was open for 19% -> 16% of each run, Pallas kernels for 14% -> 15%
where the time goes in v9:
time: 348 us; the launch traced here: 347 us
  waiting for transfers between devices  117 us (34%)
  Pallas kernels  88.7 us (25%)
  local copies, waits for them, and re-layouts  38.6 us (11%)
  blocking collectives  38.1 us (11%)
  matrix products  31.8 us (9%)
  between operations  14.6 us (4%)
  other arithmetic  13.5 us (4%)
  starting transfers between devices  4.61 us (1%)
    pallas_call x2, Pallas kernels, ring_gather(): pl.pallas_call(kernel, out_shape=jax.ShapeDtypeStruct((tok_count, rows, w...  88.7 us
    all_gather x1, waiting for transfers between devices, gather_rows(): return lax.all_gather(by_columns[None], 'grp', axis=0, tiled=True)  81 us
    all_to_all x1, blocking collectives, local(): lax.all_to_all(outgoing.reshape(grp_count, local_experts * CAP, model_wid...  38.1 us
    all_to_all x1, waiting for transfers between devices, local(): lax.all_to_all(expert_result.reshape(grp_count, local_experts * CAP, mode...  36 us
    dot_general x2, matrix products, attend(): jnp.einsum('kqn,knd->kqd', probs.astype(jnp.bfloat16), value_heads, prefe...  11.4 us
    slice x3, local copies, waits for them, and re-layouts, attend(): keys_values[:, :key_width].reshape(key_count, KV_HEADS, HEAD_DIM)  8.76 us
  transfers between devices with their start and end apart: 4, of which 2 were waited for; matrix products, arithmetic and copies ran while one was open for 16% of the time, Pallas kernels for 15%

profile of v9, /device:TPU:1, one launch (start us, length us, event | category | flops | bytes accessed | tf_op | source)
XLA Modules:
  0.0 347.1 jit_solution(1032349531234571878)
XLA Ops:
  7.3 0.9 reshape.350
  8.2 0.8 copy.75
  9.0 0.6 reshape.352.x_ref
  9.7 37.6 %shard_map.122 = bf16[32,16,512]{2,1,0:T(8,128)(2,1)} custom-call(bf16[16,512]{1,0:T(8,128)(2,1)} %reshape.352.x_ref), custom_call_target="tpu_custom_call" | custom-call | bytes 1048576 | tf_op jit(solution)/shard_map/pallas_call | solution.py:114
  47.2 1.3 copy.108
  48.6 0.2 reshape.354
  48.9 0.2 reshape.355
  49.1 0.9 pad_maximum_fusion
  50.0 0.7 collective-permute-start
  50.9 0.2 reduce-window.4
  51.6 81.0 %all-gather.6.cloned.1.call-done = bf16[16384,96]{1,0:T(8,128)(2,1)} async-done(((bf16[1024,96]{1,0:T(8,128)(2,1)}), bf16[16384,96]{1,0:T(8,128)(2,1)}) %all-gather.6.cloned.1.call-update) | async-done | bytes 3145744 | tf_op jit(solution)/shard_map/all_gather | solution.py:149
  132.6 4.1 %fusion.21 = f32[128,1024]{1,0:T(8,128)S(1)} fusion(bf16[16,1024,96]{2,1,0:T(8,128)(2,1)} %bitcast.130, f32[128,16,64]{0,2,1:T(8,128)S(1)} %bitcast.113, f32[16,64]{1,0:T(8,128)S(1)} %mul.211, f32[128]{0:T(128)S(1)} %add_rsqrt_fusion.1), kind=kOutput, calls=%fused_computation.31 | convolution fusion | flops 268828672 | bytes 4198912 | tf_op jit(solution)/shard_map/ngr,gcr->nc/dot_general | solution.py:228
  137.0 0.7 pad_maximum_fusion.3.x_ref
  137.7 51.2 %shard_map.123 = bf16[32,144,512]{2,1,0:T(8,128)(2,1)} custom-call(bf16[144,512]{1,0:T(8,128)(2,1)} %pad_maximum_fusion.3.x_ref), custom_call_target="tpu_custom_call" | custom-call | bytes 9437184 | tf_op jit(solution)/shard_map/pallas_call | solution.py:114
  188.9 4.7 %slice.77 = bf16[32,128,512]{2,1,0:T(8,128)(2,1)} slice(bf16[32,144,512]{2,1,0:T(8,128)(2,1)} %shard_map.123), slice={[0:32], [0:128], [0:512]} | slice | bytes 8388608 | tf_op jit(solution)/shard_map/slice | solution.py:255
  193.5 0.7 copy-done.4
  195.0 0.5 fusion.36
  195.6 1.0 fusion.12
  196.8 0.2 copy.80
  197.5 4.5 %fusion.61 = (bf16[4096,256]{1,0:T(8,128)(2,1)}, bf16[4096,256]{1,0:T(8,128)(2,1)}) fusion(bf16[4096,512]{1,0:T(8,128)(2,1)} %bitcast.93), kind=kLoop, calls=%fused_computation.110 | loop fusion | bytes 8388608 | tf_op jit(solution)/shard_map/slice | solution.py:176
  202.0 4.1 %copy.86 = bf16[4096,256]{0,1:T(8,128)(2,1)} copy(bf16[4096,256]{1,0:T(8,128)(2,1)} %get-tuple-element.6) | data formatting | bytes 4194304 | tf_op jit(solution)/shard_map/slice | solution.py:176
  206.1 4.1 %copy.88 = bf16[4096,256]{0,1:T(8,128)(2,1)} copy(bf16[4096,256]{1,0:T(8,128)(2,1)} %get-tuple-element.7) | data formatting | bytes 4194304 | tf_op jit(solution)/shard_map/slice | solution.py:178
  210.3 0.7 pad_maximum_fusion.1
  211.0 0.5 multiply_reduce_fusion
  211.5 0.4 copy-done.1
  211.9 3.6 %fusion = (f32[4,256]{1,0:T(4,128)S(1)}, f32[4,256,4096]{2,1,0:T(8,128)S(1)}) fusion(pred[256,4096]{1,0:T(8,128)(4,1)S(1)} %fusion.12, bf16[4,256,64]{2,1,0:T(8,128)(2,1)S(1)} %bitcast.101, bf16[4,4096,64]{1,2,0:T(8,128)(2,1)S(1)} %bitcast.94), kind=kOutput, calls=%fused_computation.3 | convolution fusion | flops 549452800 | bytes 20058112 | tf_op jit(solution)/shard_map/kqd,knd->kqn/dot_general | solution.py:181
  215.5 0.6 fusion.17
  216.1 4.4 %fusion.1 = f32[4,256]{1,0:T(4,128)S(1)} fusion(f32[4,256,4096]{2,1,0:T(8,128)S(1)} %get-tuple-element.24, f32[4,256]{1,0:T(4,128)S(1)} %get-tuple-element.17, pred[256,4096]{1,0:T(8,128)(4,1)S(1)} %fusion.12), kind=kLoop, calls=%fused_computation.4 | loop fusion | flops 16776192 | bytes 17833984 | tf_op jit(solution)/shard_map/reduce_sum | solution.py:190
  220.5 0.7 copy-done
  221.3 9.1 %fusion.3 = f32[4,256,64]{1,2,0:T(8,128)S(1)} fusion(bf16[4,4096,64]{1,2,0:T(8,128)(2,1)} %bitcast.105, f32[4,256,4096]{2,1,0:T(8,128)} %copy-done, f32[4,256]{1,0:T(4,128)S(1)} %get-tuple-element.17, pred[256,4096]{1,0:T(8,128)(4,1)S(1)} %fusion.12), kind=kOutput, calls=%fused_computation.6 | convolution fusion | flops 553648128 | bytes 20189184 | tf_op jit(solution)/shard_map/kqn,knd->kqd/dot_general | solution.py:191
  230.4 2.3 fusion.33
  233.0 4.6 %multiply_reduce_fusion.1 = (f32[128]{0:T(128)S(1)}, f32[128,1024]{1,0:T(8,128)S(1)}) fusion(bf16[128,16,32]{0,2,1:T(8,128)(2,1)S(1)} %bitcast.120, bf16[16,1024,96]{2,1,0:T(8,128)(2,1)} %bitcast.131, bf16[1,128,1024]{2,1,0:T(8,128)(2,1)S(1)} %copy-done.3), kind=kOutput, calls=%fused_computation.48 | convolution fusion | flops 134741888 | bytes 4063744 | tf_op jit(solution)/shard_map/ngr,gcr->nc/dot_general | solution.py:268
  237.5 2.7 convolution_convert_fusion
  240.3 38.1 %all_to_all.10 = bf16[16,80,1024]{2,1,0:T(8,128)(2,1)S(1)} all-to-all(bf16[16,80,1024]{2,1,0:T(8,128)(2,1)S(1)} %bitcast.103), channel_id=1, replica_groups=mesh['grp'=16,'tok'=32] {'grp'}, dimensions={0} | all-to-all | bytes 5242880 | tf_op jit(solution)/shard_map/all_to_all | solution.py:304
  278.4 0.3 copy.93
  278.7 1.8 slice.105
  280.5 2.6 slice.102
  283.1 0.7 copy.106
  283.8 0.2 copy.107
  284.0 2.9 fusion.63
  287.0 1.6 convolution_convert_fusion.1
  288.5 1.7 copy.96
  290.3 3.9 %all-to-all-start.1 = ((bf16[16,80,1024]{2,1,0:T(8,128)(2,1)}), bf16[16,80,1024]{2,1,0:T(8,128)(2,1)S(1)}, u32[]{:S(2)}, u32[]{:S(2)}) async-start(bf16[16,80,1024]{2,1,0:T(8,128)(2,1)} %bitcast.95), calls=%async_computation.1 | async-start | bytes 5242880 | tf_op jit(solution)/shard_map/all_to_all | solution.py:321
  294.5 0.7 maximum_bitcast_fusion
  295.1 36.0 %all-to-all-done.1 = bf16[16,80,1024]{2,1,0:T(8,128)(2,1)S(1)} async-done(((bf16[16,80,1024]{2,1,0:T(8,128)(2,1)}), bf16[16,80,1024]{2,1,0:T(8,128)(2,1)S(1)}, u32[]{:S(2)}, u32[]{:S(2)}) %all-to-all-start.1) | async-done | bytes 2621472 | tf_op jit(solution)/shard_map/all_to_all | solution.py:321
  331.2 5.4 %gather_fusion = bf16[1024,1024]{1,0:T(8,128)(2,1)} fusion(bf16[1280,1024]{1,0:T(8,128)(2,1)S(1)} %bitcast.91, s32[1024]{0:T(1024)S(1)} %broadcast_clamp_fusion), kind=kCustom, calls=%fused_computation | custom fusion | bytes 4198400 | tf_op jit(solution)/shard_map/gather | solution.py:328
  336.5 2.9 fusion.11
  339.5 0.8 fusion.41
  (80 shorter events, 3.3 us)
Async XLA Ops:
  7.2 42.8 %copy-start.6 = (bf16[1,32,1024]{2,1,0:T(8,128)(2,1)S(1)}, bf16[1,32,1024]{2,1,0:T(8,128)(2,1)}, u32[]{:S(2)}) copy-start(bf16[1,32,1024]{2,1,0:T(8,128)(2,1)} %param.21) | copy-start | bytes 196612
  7.2 42.8 %copy-start.5 = (bf16[1,64,1024]{2,1,0:T(8,128)(2,1)S(1)}, bf16[1,64,1024]{2,1,0:T(8,128)(2,1)}, u32[]{:S(2)}) copy-start(bf16[1,64,1024]{2,1,0:T(8,128)(2,1)} %param.20) | copy-start | bytes 393220
  7.2 43.5 %copy-start.9 = (f32[1024]{0:T(1024)S(1)}, f32[1024]{0:T(1024)}, u32[]{:S(2)}) copy-start(f32[1024]{0:T(1024)} %param.16) | copy-start | bytes 12292
  7.2 43.6 %copy-start.3 = (bf16[1,128,1024]{2,1,0:T(8,128)(2,1)S(1)}, bf16[1,128,1024]{2,1,0:T(8,128)(2,1)}, u32[]{:S(2)}) copy-start(bf16[1,128,1024]{2,1,0:T(8,128)(2,1)} %param.11) | copy-start | bytes 786436
  7.2 43.7 %copy-start.12 = (s32[1,3]{1,0:T(1,128)S(1)}, s32[1,3]{1,0:T(1,128)}, u32[]{:S(2)}) copy-start(s32[1,3]{1,0:T(1,128)} %param.12) | copy-start | bytes 40
  7.2 125.4 %all-gather.6.cloned.1.call-start = ((), (), s32[]{:S(2)}) async-start(), calls=%async_computation.3 | async-start | bytes 4456448 | tf_op jit(solution)/shard_map/all_gather | solution.py:149
  49.9 228.7 %all-gather.4.cloned.1.call-start = ((), (), s32[]{:S(2)}) async-start(), calls=%async_computation.2 | async-start | bytes 6488064 | tf_op jit(solution)/shard_map/all_gather | solution.py:168
  50.0 143.5 %collective-permute-start = (bf16[96,1024]{1,0:T(8,128)(2,1)S(1)}, bf16[96,1024]{1,0:T(8,128)(2,1)S(1)}, u32[]{:S(2)}, u32[]{:S(2)}) collective-permute-start(bf16[96,1024]{1,0:T(8,128)(2,1)S(1)} %pad_maximum_fusion.2), channel_id=1, source_target_pairs={{0,0},{1,1},{2,32},{3,33},{4,64},{5,65},{6,96},{7,97},{8,128},{9,1... | collective-permute-start | bytes 589832 | tf_op jit(solution)/shard_map/ppermute | solution.py:161
  132.6 4.4 %copy-start.7 = (bf16[1,16,512]{2,1,0:T(8,128)(2,1)S(1)}, bf16[1,16,512]{2,1,0:T(8,128)(2,1)}, u32[]{:S(2)}) copy-start(bf16[1,16,512]{2,1,0:T(8,128)(2,1)} %param.13) | copy-start | bytes 49156
  188.9 5.8 %copy-start.8 = (s32[1,128,8]{1,2,0:T(8,128)S(1)}, s32[1,128,8]{1,2,0:T(8,128)}, u32[]{:S(2)}) copy-start(s32[1,128,8]{1,2,0:T(8,128)} %param.14) | copy-start | bytes 12292
  193.5 0.7 copy-start.4
  195.0 2.2 slice-start
  210.3 1.6 copy-start.1
  211.5 4.0 %copy-start.2 = (f32[4,256,512]{2,1,0:T(8,128)}, f32[4,256,512]{2,1,0:T(8,128)S(1)}, u32[]{:S(2)}) copy-start(f32[4,256,512]{2,1,0:T(8,128)S(1)} %get-tuple-element.22) | copy-start | bytes 6291460
  215.5 5.7 %copy-start = (f32[4,256,4096]{2,1,0:T(8,128)}, f32[4,256,4096]{2,1,0:T(8,128)S(1)}, u32[]{:S(2)}) copy-start(f32[4,256,4096]{2,1,0:T(8,128)S(1)} %get-tuple-element.24) | copy-start | bytes 50331652
  232.9 4.6 %copy-start.11 = (f32[1024]{0:T(1024)S(1)}, f32[1024]{0:T(1024)}, u32[]{:S(2)}) copy-start(f32[1024]{0:T(1024)} %param.19) | copy-start | bytes 12292
  290.3 4.1 %copy-start.10 = (f32[1,128,8]{1,2,0:T(8,128)S(1)}, f32[1,128,8]{1,2,0:T(8,128)}, u32[]{:S(2)}) copy-start(f32[1,128,8]{1,2,0:T(8,128)} %param.15) | copy-start | bytes 12292
  290.3 40.9 %all-to-all-start.1 = ((bf16[16,80,1024]{2,1,0:T(8,128)(2,1)}), bf16[16,80,1024]{2,1,0:T(8,128)(2,1)S(1)}, u32[]{:S(2)}, u32[]{:S(2)}) async-start(bf16[16,80,1024]{2,1,0:T(8,128)(2,1)} %bitcast.95), calls=%async_computation.1 | async-start | bytes 5242880 | tf_op jit(solution)/shard_map/all_to_all | solution.py:321
Sparse Core Ops, SparseCore 0:
  50.1 82.4 all-gather.5
  194.3 70.3 all-gather.3

commit v10 on v9

--- a/solution.py
+++ b/solution.py
@@ -325,8 +325,19 @@
         concat_axis=0,
         tiled=True,
     ).reshape(EXPERTS * CAP, -1)
-    weighted = returned[slot_index].astype(jnp.float32) * gates[0].reshape(-1)[:, None]
-    moe_out = jnp.sum(weighted.reshape(tok_count, TOP, -1), axis=1)
+    gate_of_route = token_of_route.astype(jnp.float32).T * gates[0].reshape(-1)[None, :]
+    combine = jnp.dot(
+        gate_of_route,
+        slot_of_route.astype(jnp.float32).T,
+        precision=lax.Precision.HIGHEST,
+        preferred_element_type=jnp.float32,
+    )
+    moe_out = jnp.dot(
+        combine,
+        returned.astype(jnp.float32),
+        precision=lax.Precision.HIGHEST,
+        preferred_element_type=jnp.float32,
+    )
     hidden_out = (after_attention + moe_out).astype(jnp.bfloat16)
     return (hidden_out[None], suffix_cache[None])
 

time: 348 us -> 344 us (0.989)
  matrix products: 31.8 us -> 39.7 us
  local copies, waits for them, and re-layouts: 38.6 us -> 32.8 us
  other arithmetic: 13.5 us -> 9.81 us
    dot_general x0 -> x2, matrix products: none -> 6 us  [the longest x1 3.01 us: local(): jnp.dot(gate_of_route, slot_of_route.astype(jnp.float32).T, precision=lax...]
    gather x1 -> x0, local copies, waits for them, and re-layouts: 5.35 us -> none  [local(): returned[slot_index].astype(jnp.float32) * gates[0].reshape(-1)[:, None]]
  transfers between devices with their start and end apart: 4 -> 4, of which waited for: 2 -> 2; matrix products, arithmetic and copies ran while one was open for 16% -> 18% of each run, Pallas kernels for 15% -> 15%
where the time goes in v10:
time: 344 us; the launch traced here: 343 us
  waiting for transfers between devices  114 us (33%)
  Pallas kernels  88.8 us (26%)
  matrix products  39.7 us (12%)
  blocking collectives  38.5 us (11%)
  local copies, waits for them, and re-layouts  32.8 us (10%)
  between operations  14.6 us (4%)
  other arithmetic  9.81 us (3%)
  starting transfers between devices  4.87 us (1%)
    pallas_call x2, Pallas kernels, ring_gather(): pl.pallas_call(kernel, out_shape=jax.ShapeDtypeStruct((tok_count, rows, w...  88.8 us
    all_gather x1, waiting for transfers between devices, gather_rows(): return lax.all_gather(by_columns[None], 'grp', axis=0, tiled=True)  81 us
    all_to_all x1, blocking collectives, local(): lax.all_to_all(outgoing.reshape(grp_count, local_experts * CAP, model_wid...  38.5 us
    all_to_all x1, waiting for transfers between devices, local(): lax.all_to_all(expert_result.reshape(grp_count, local_experts * CAP, mode...  32.9 us
    dot_general x2, matrix products, attend(): jnp.einsum('kqn,knd->kqd', probs.astype(jnp.bfloat16), value_heads, prefe...  11.3 us
    slice x3, local copies, waits for them, and re-layouts, attend(): keys_values[:, :key_width].reshape(key_count, KV_HEADS, HEAD_DIM)  8.73 us
  transfers between devices with their start and end apart: 4, of which 2 were waited for; matrix products, arithmetic and copies ran while one was open for 18% of the time, Pallas kernels for 15%

profile of v10, /device:TPU:1, one launch (start us, length us, event | category | flops | bytes accessed | tf_op | source)
XLA Modules:
  0.0 343.0 jit_solution(4008120454306279467)
XLA Ops:
  7.3 0.9 copy.72
  8.2 0.8 reshape.308
  9.0 0.6 reshape.310.x_ref
  9.7 37.6 %shard_map.122 = bf16[32,16,512]{2,1,0:T(8,128)(2,1)} custom-call(bf16[16,512]{1,0:T(8,128)(2,1)} %reshape.310.x_ref), custom_call_target="tpu_custom_call" | custom-call | bytes 1048576 | tf_op jit(solution)/shard_map/pallas_call | solution.py:114
  47.2 1.3 copy.104
  48.6 0.2 reshape.313
  48.8 0.2 reshape.312
  49.1 0.9 pad_maximum_fusion
  50.0 0.7 collective-permute-start
  50.9 0.2 reduce-window.4
  51.6 81.0 %all-gather.6.cloned.1.call-done = bf16[16384,96]{1,0:T(8,128)(2,1)} async-done(((bf16[1024,96]{1,0:T(8,128)(2,1)}), bf16[16384,96]{1,0:T(8,128)(2,1)}) %all-gather.6.cloned.1.call-update) | async-done | bytes 3145744 | tf_op jit(solution)/shard_map/all_gather | solution.py:149
  132.6 4.1 %fusion.22 = f32[128,1024]{1,0:T(8,128)S(1)} fusion(bf16[16,1024,96]{2,1,0:T(8,128)(2,1)} %bitcast.123, f32[128,16,64]{0,2,1:T(8,128)S(1)} %bitcast.109, f32[16,64]{1,0:T(8,128)S(1)} %mul.196, f32[128]{0:T(128)S(1)} %add_rsqrt_fusion.1), kind=kOutput, calls=%fused_computation.30 | convolution fusion | flops 268828672 | bytes 4198912 | tf_op jit(solution)/shard_map/ngr,gcr->nc/dot_general | solution.py:228
  137.0 0.7 pad_maximum_fusion.3.x_ref
  137.7 51.2 %shard_map.123 = bf16[32,144,512]{2,1,0:T(8,128)(2,1)} custom-call(bf16[144,512]{1,0:T(8,128)(2,1)} %pad_maximum_fusion.3.x_ref), custom_call_target="tpu_custom_call" | custom-call | bytes 9437184 | tf_op jit(solution)/shard_map/pallas_call | solution.py:114
  188.9 4.7 %slice.77 = bf16[32,128,512]{2,1,0:T(8,128)(2,1)} slice(bf16[32,144,512]{2,1,0:T(8,128)(2,1)} %shard_map.123), slice={[0:32], [0:128], [0:512]} | slice | bytes 8388608 | tf_op jit(solution)/shard_map/slice | solution.py:255
  193.6 0.7 copy-done.5
  195.1 0.5 fusion.39
  195.6 1.0 fusion.12
  196.7 4.5 %fusion.69 = (bf16[4096,256]{1,0:T(8,128)(2,1)}, bf16[4096,256]{1,0:T(8,128)(2,1)}) fusion(bf16[4096,512]{1,0:T(8,128)(2,1)} %bitcast.88), kind=kLoop, calls=%fused_computation.112 | loop fusion | bytes 8388608 | tf_op jit(solution)/shard_map/slice | solution.py:176
  201.1 4.2 %copy.85 = bf16[4096,256]{0,1:T(8,128)(2,1)} copy(bf16[4096,256]{1,0:T(8,128)(2,1)} %get-tuple-element.7) | data formatting | bytes 4194304 | tf_op jit(solution)/shard_map/slice | solution.py:178
  205.5 0.2 copy.77
  205.7 0.2 copy.76
  205.8 4.1 %copy.83 = bf16[4096,256]{0,1:T(8,128)(2,1)} copy(bf16[4096,256]{1,0:T(8,128)(2,1)} %get-tuple-element.6) | data formatting | bytes 4194304 | tf_op jit(solution)/shard_map/slice | solution.py:176
  210.3 0.7 pad_maximum_fusion.1
  211.0 0.5 multiply_reduce_fusion
  211.5 5.5 %fusion = (f32[4,256]{1,0:T(4,128)S(1)}, f32[4,256,4096]{2,1,0:T(8,128)S(1)}) fusion(pred[256,4096]{1,0:T(8,128)(4,1)S(1)} %fusion.12, bf16[4,256,64]{2,1,0:T(8,128)(2,1)S(1)} %bitcast.97, bf16[4,4096,64]{1,2,0:T(8,128)(2,1)} %bitcast.89), kind=kOutput, calls=%fused_computation.2 | convolution fusion | flops 549452800 | bytes 20058112 | tf_op jit(solution)/shard_map/kqd,knd->kqn/dot_general | solution.py:181
  217.0 0.6 fusion.18
  217.6 4.4 %fusion.1 = f32[4,256]{1,0:T(4,128)S(1)} fusion(f32[4,256,4096]{2,1,0:T(8,128)S(1)} %get-tuple-element.22, f32[4,256]{1,0:T(4,128)S(1)} %get-tuple-element.15, pred[256,4096]{1,0:T(8,128)(4,1)S(1)} %fusion.12), kind=kLoop, calls=%fused_computation.3 | loop fusion | flops 16776192 | bytes 17833984 | tf_op jit(solution)/shard_map/reduce_sum | solution.py:190
  222.0 0.8 copy-done
  222.8 9.1 %fusion.3 = f32[4,256,64]{1,2,0:T(8,128)S(1)} fusion(bf16[4,4096,64]{1,2,0:T(8,128)(2,1)} %bitcast.101, f32[4,256,4096]{2,1,0:T(8,128)} %copy-done, f32[4,256]{1,0:T(4,128)S(1)} %get-tuple-element.15, pred[256,4096]{1,0:T(8,128)(4,1)S(1)} %fusion.12), kind=kOutput, calls=%fused_computation.5 | convolution fusion | flops 553648128 | bytes 20189184 | tf_op jit(solution)/shard_map/kqn,knd->kqd/dot_general | solution.py:191
  231.9 2.2 fusion.36
  234.1 0.2 copy.86
  234.4 4.5 %multiply_reduce_fusion.1 = (f32[128]{0:T(128)S(1)}, f32[128,1024]{1,0:T(8,128)S(1)}) fusion(bf16[128,16,32]{0,2,1:T(8,128)(2,1)S(1)} %bitcast.116, bf16[16,1024,96]{2,1,0:T(8,128)(2,1)} %bitcast.124, bf16[1,128,1024]{2,1,0:T(8,128)(2,1)S(1)} %copy-done.2), kind=kOutput, calls=%fused_computation.49 | convolution fusion | flops 134741888 | bytes 4063744 | tf_op jit(solution)/shard_map/ngr,gcr->nc/dot_general | solution.py:268
  239.0 2.7 convolution_convert_fusion
  241.7 38.5 %all_to_all.10 = bf16[16,80,1024]{2,1,0:T(8,128)(2,1)S(1)} all-to-all(bf16[16,80,1024]{2,1,0:T(8,128)(2,1)S(1)} %bitcast.100), channel_id=1, replica_groups=mesh['grp'=16,'tok'=32] {'grp'}, dimensions={0} | all-to-all | bytes 5242880 | tf_op jit(solution)/shard_map/all_to_all | solution.py:304
  280.2 0.3 copy.91
  280.5 1.8 slice.103
  282.3 2.6 slice.100
  285.0 0.3 copy.103
  285.2 0.7 copy.102
  285.9 2.9 fusion.71
  288.9 1.6 convolution_convert_fusion.1
  290.4 1.7 copy.94
  292.2 4.1 %all-to-all-start.1 = ((bf16[16,80,1024]{2,1,0:T(8,128)(2,1)}), bf16[16,80,1024]{2,1,0:T(8,128)(2,1)S(1)}, u32[]{:S(2)}, u32[]{:S(2)}) async-start(bf16[16,80,1024]{2,1,0:T(8,128)(2,1)} %bitcast.91), calls=%async_computation.1 | async-start | bytes 5242880 | tf_op jit(solution)/shard_map/all_to_all | solution.py:321
  296.5 3.0 fusion.7
  299.5 0.7 maximum_bitcast_fusion
  300.2 32.9 %all-to-all-done.1 = bf16[16,80,1024]{2,1,0:T(8,128)(2,1)S(1)} async-done(((bf16[16,80,1024]{2,1,0:T(8,128)(2,1)}), bf16[16,80,1024]{2,1,0:T(8,128)(2,1)S(1)}, u32[]{:S(2)}, u32[]{:S(2)}) %all-to-all-start.1) | async-done | bytes 2621472 | tf_op jit(solution)/shard_map/all_to_all | solution.py:321
  333.2 3.0 fusion.32
  (77 shorter events, 2.9 us)
Async XLA Ops:
  7.2 42.8 %copy-start.7 = (bf16[1,32,1024]{2,1,0:T(8,128)(2,1)S(1)}, bf16[1,32,1024]{2,1,0:T(8,128)(2,1)}, u32[]{:S(2)}) copy-start(bf16[1,32,1024]{2,1,0:T(8,128)(2,1)} %param.21) | copy-start | bytes 196612
  7.2 42.8 %copy-start.6 = (bf16[1,64,1024]{2,1,0:T(8,128)(2,1)S(1)}, bf16[1,64,1024]{2,1,0:T(8,128)(2,1)}, u32[]{:S(2)}) copy-start(bf16[1,64,1024]{2,1,0:T(8,128)(2,1)} %param.20) | copy-start | bytes 393220
  7.2 43.5 %copy-start.2 = (bf16[1,128,1024]{2,1,0:T(8,128)(2,1)S(1)}, bf16[1,128,1024]{2,1,0:T(8,128)(2,1)}, u32[]{:S(2)}) copy-start(bf16[1,128,1024]{2,1,0:T(8,128)(2,1)} %param.11) | copy-start | bytes 786436
  7.2 43.7 %copy-start.9 = (f32[1024]{0:T(1024)S(1)}, f32[1024]{0:T(1024)}, u32[]{:S(2)}) copy-start(f32[1024]{0:T(1024)} %param.16) | copy-start | bytes 12292
  7.2 43.7 %copy-start.13 = (s32[1,3]{1,0:T(1,128)S(1)}, s32[1,3]{1,0:T(1,128)}, u32[]{:S(2)}) copy-start(s32[1,3]{1,0:T(1,128)} %param.12) | copy-start | bytes 40
  7.2 125.4 %all-gather.6.cloned.1.call-start = ((), (), s32[]{:S(2)}) async-start(), calls=%async_computation.3 | async-start | bytes 4456448 | tf_op jit(solution)/shard_map/all_gather | solution.py:149
  49.9 230.6 %all-gather.4.cloned.1.call-start = ((), (), s32[]{:S(2)}) async-start(), calls=%async_computation.2 | async-start | bytes 6488064 | tf_op jit(solution)/shard_map/all_gather | solution.py:168
  50.0 143.6 %collective-permute-start = (bf16[96,1024]{1,0:T(8,128)(2,1)S(1)}, bf16[96,1024]{1,0:T(8,128)(2,1)S(1)}, u32[]{:S(2)}, u32[]{:S(2)}) collective-permute-start(bf16[96,1024]{1,0:T(8,128)(2,1)S(1)} %pad_maximum_fusion.2), channel_id=1, source_target_pairs={{0,0},{1,1},{2,32},{3,33},{4,64},{5,65},{6,96},{7,97},{8,128},{9,1... | collective-permute-start | bytes 589832 | tf_op jit(solution)/shard_map/ppermute | solution.py:161
  132.6 4.4 %copy-start.8 = (bf16[1,16,512]{2,1,0:T(8,128)(2,1)S(1)}, bf16[1,16,512]{2,1,0:T(8,128)(2,1)}, u32[]{:S(2)}) copy-start(bf16[1,16,512]{2,1,0:T(8,128)(2,1)} %param.13) | copy-start | bytes 49156
  136.7 59.9 %copy-start.3 = (f32[128,1024]{1,0:T(8,128)}, f32[128,1024]{1,0:T(8,128)S(1)}, u32[]{:S(2)}) copy-start(f32[128,1024]{1,0:T(8,128)S(1)} %fusion.22) | copy-start | bytes 1572868
  188.9 5.8 %copy-start.10 = (s32[1,128,8]{1,2,0:T(8,128)S(1)}, s32[1,128,8]{1,2,0:T(8,128)}, u32[]{:S(2)}) copy-start(s32[1,128,8]{1,2,0:T(8,128)} %param.14) | copy-start | bytes 12292
  193.6 0.7 copy-start.5
  201.1 4.2 %slice-start.1 = ((f32[128,1024]{1,0:T(8,128)}), f32[128,512]{1,0:T(8,128)S(1)}, s32[]{:S(2)}) async-start(f32[128,1024]{1,0:T(8,128)} %copy-done.3), calls=%async_computation.5 | async-start | bytes 524288 | tf_op jit(solution)/shard_map/slice | solution.py:234
  205.4 4.5 %slice-start = ((bf16[32,144,512]{2,1,0:T(8,128)(2,1)}), bf16[32,16,512]{2,1,0:T(8,128)(2,1)S(1)}, s32[]{:S(2)}) async-start(bf16[32,144,512]{2,1,0:T(8,128)(2,1)} %shard_map.123), calls=%async_computation.4 | async-start | bytes 1048576 | tf_op jit(solution)/shard_map/slice | solution.py:256
  211.5 5.5 %copy-start.1 = (f32[4,256,512]{2,1,0:T(8,128)}, f32[4,256,512]{2,1,0:T(8,128)S(1)}, u32[]{:S(2)}) copy-start(f32[4,256,512]{2,1,0:T(8,128)S(1)} %get-tuple-element.20) | copy-start | bytes 6291460
  217.0 5.8 %copy-start = (f32[4,256,4096]{2,1,0:T(8,128)}, f32[4,256,4096]{2,1,0:T(8,128)S(1)}, u32[]{:S(2)}) copy-start(f32[4,256,4096]{2,1,0:T(8,128)S(1)} %get-tuple-element.22) | copy-start | bytes 50331652
  234.4 4.6 %copy-start.12 = (f32[1024]{0:T(1024)S(1)}, f32[1024]{0:T(1024)}, u32[]{:S(2)}) copy-start(f32[1024]{0:T(1024)} %param.19) | copy-start | bytes 12292
  239.0 41.3 %copy-start.4 = (f32[128,1024]{1,0:T(8,128)}, f32[128,1024]{1,0:T(8,128)S(1)}, u32[]{:S(2)}) copy-start(f32[128,1024]{1,0:T(8,128)S(1)} %get-tuple-element.24) | copy-start | bytes 1572868
  292.2 4.1 %copy-start.11 = (f32[1,128,8]{1,2,0:T(8,128)S(1)}, f32[1,128,8]{1,2,0:T(8,128)}, u32[]{:S(2)}) copy-start(f32[1,128,8]{1,2,0:T(8,128)} %param.15) | copy-start | bytes 12292
  292.2 41.0 %all-to-all-start.1 = ((bf16[16,80,1024]{2,1,0:T(8,128)(2,1)}), bf16[16,80,1024]{2,1,0:T(8,128)(2,1)S(1)}, u32[]{:S(2)}, u32[]{:S(2)}) async-start(bf16[16,80,1024]{2,1,0:T(8,128)(2,1)} %bitcast.91), calls=%async_computation.1 | async-start | bytes 5242880 | tf_op jit(solution)/shard_map/all_to_all | solution.py:321
Sparse Core Ops, SparseCore 0:
  50.1 82.4 all-gather.5
  194.4 70.7 all-gather.3

commit v11 on v10

--- a/solution.py
+++ b/solution.py
@@ -130,12 +130,82 @@
     )(block)
 
 
+def direct_gather(block, collective_id):
+    tok_count = lax.axis_size("tok")
+    rows, width = block.shape
+    mesh_ids = pl.DeviceIdType.MESH
+
+    def kernel(x_ref, out_ref, local_sem, send_sems, recv):
+        me = lax.axis_index("tok")
+        grp = lax.axis_index("grp")
+        barrier = pltpu.get_barrier_semaphore()
+
+        def other_of(i):
+            return (me + 1 + i) % tok_count
+
+        def remote(src, slot, sem, target):
+            return pltpu.make_async_remote_copy(
+                src_ref=src,
+                dst_ref=out_ref.at[slot],
+                send_sem=sem,
+                recv_sem=recv.at[slot],
+                device_id=(grp, target),
+                device_id_type=mesh_ids,
+            )
+
+        def greet(i, c):
+            pl.semaphore_signal(barrier, 1, device_id=(grp, other_of(i)), device_id_type=mesh_ids)
+            return c
+
+        lax.fori_loop(0, tok_count - 1, greet, 0)
+        pl.semaphore_wait(barrier, tok_count - 1)
+        own = pltpu.make_async_copy(x_ref, out_ref.at[me], local_sem.at[0])
+        own.start()
+
+        def send(i, c):
+            remote(x_ref, me, send_sems.at[i], other_of(i)).start()
+            return c
+
+        lax.fori_loop(0, tok_count - 1, send, 0)
+
+        def arrive(i, c):
+            source = other_of(i)
+            remote(out_ref.at[source], source, send_sems.at[0], source).wait_recv()
+            return c
+
+        lax.fori_loop(0, tok_count - 1, arrive, 0)
+        own.wait()
+
+        def sent(i, c):
+            remote(x_ref, me, send_sems.at[i], other_of(i)).wait_send()
+            return c
+
+        lax.fori_loop(0, tok_count - 1, sent, 0)
+
+    block_bytes = rows * width * block.dtype.itemsize
+    return pl.pallas_call(
+        kernel,
+        out_shape=jax.ShapeDtypeStruct((tok_count, rows, width), block.dtype),
+        in_specs=[pl.BlockSpec(memory_space=pltpu.VMEM)],
+        out_specs=pl.BlockSpec(memory_space=pltpu.VMEM),
+        scratch_shapes=[
+            pltpu.SemaphoreType.DMA((1,)),
+            pltpu.SemaphoreType.DMA((tok_count,)),
+            pltpu.SemaphoreType.DMA((tok_count,)),
+        ],
+        compiler_params=pltpu.CompilerParams(collective_id=collective_id, has_side_effects=True),
+        cost_estimate=pl.CostEstimate(
+            flops=0, transcendentals=0, bytes_accessed=2 * tok_count * block_bytes
+        ),
+    )(block)
+
+
 def gather_small(blocks):
     flat = jnp.concatenate([b.reshape(-1) for b in blocks])
     width = 512
     padded_rows = -(-flat.shape[0] // (16 * width)) * 16
     flat = jnp.pad(flat, (0, padded_rows * width - flat.shape[0]))
-    gathered = ring_gather(flat.reshape(padded_rows, width), 1)
+    gathered = direct_gather(flat.reshape(padded_rows, width), 1)
     gathered = gathered.reshape(gathered.shape[0], -1)
     pieces, start = [], 0
     for b in blocks:

time: 344 us -> 351 us (1.020)
  Pallas kernels: 88.8 us -> 93.6 us
    pallas_call x0 -> x1, Pallas kernels: none -> 42.7 us  [direct_gather(): pl.pallas_call(kernel, out_shape=jax.ShapeDtypeStruct((tok_count, rows, w...]
    pallas_call x2 -> x1, Pallas kernels: 88.8 us -> 50.9 us  [ring_gather(): pl.pallas_call(kernel, out_shape=jax.ShapeDtypeStruct((tok_count, rows, w...]
  transfers between devices with their start and end apart: 4 -> 4, of which waited for: 2 -> 2; matrix products, arithmetic and copies ran while one was open for 18% -> 17% of each run, Pallas kernels for 15% -> 15%
where the time goes in v11:
time: 351 us; the launch traced here: 350 us
  waiting for transfers between devices  116 us (33%)
  Pallas kernels  93.6 us (27%)
  matrix products  39.7 us (11%)
  blocking collectives  38.8 us (11%)
  local copies, waits for them, and re-layouts  32.8 us (9%)
  between operations  14.6 us (4%)
  other arithmetic  9.81 us (3%)
  starting transfers between devices  4.87 us (1%)
    all_gather x1, waiting for transfers between devices, gather_rows(): return lax.all_gather(by_columns[None], 'grp', axis=0, tiled=True)  83.2 us
    pallas_call x1, Pallas kernels, ring_gather(): pl.pallas_call(kernel, out_shape=jax.ShapeDtypeStruct((tok_count, rows, w...  50.9 us
    pallas_call x1, Pallas kernels, direct_gather(): pl.pallas_call(kernel, out_shape=jax.ShapeDtypeStruct((tok_count, rows, w...  42.7 us
    all_to_all x1, blocking collectives, local(): lax.all_to_all(outgoing.reshape(grp_count, local_experts * CAP, model_wid...  38.8 us
    all_to_all x1, waiting for transfers between devices, local(): lax.all_to_all(expert_result.reshape(grp_count, local_experts * CAP, mode...  32.8 us
    dot_general x2, matrix products, attend(): jnp.einsum('kqn,knd->kqd', probs.astype(jnp.bfloat16), value_heads, prefe...  11.3 us
    slice x3, local copies, waits for them, and re-layouts, attend(): keys_values[:, :key_width].reshape(key_count, KV_HEADS, HEAD_DIM)  8.73 us
  transfers between devices with their start and end apart: 4, of which 2 were waited for; matrix products, arithmetic and copies ran while one was open for 17% of the time, Pallas kernels for 15%

profile of v11, /device:TPU:1, one launch (start us, length us, event | category | flops | bytes accessed | tf_op | source)
XLA Modules:
  0.0 350.3 jit_solution(15701464440740018380)
XLA Ops:
  7.3 0.9 copy.72
  8.2 0.8 reshape.308
  9.0 0.6 reshape.310.x_ref
  9.7 42.7 %shard_map.122 = bf16[32,16,512]{2,1,0:T(8,128)(2,1)} custom-call(bf16[16,512]{1,0:T(8,128)(2,1)} %reshape.310.x_ref), custom_call_target="tpu_custom_call" | custom-call | bytes 1048576 | tf_op jit(solution)/shard_map/pallas_call | solution.py:186
  52.4 1.3 copy.104
  53.8 0.2 reshape.313
  53.9 0.2 reshape.312
  54.2 0.9 pad_maximum_fusion
  55.2 0.7 collective-permute-start
  56.1 0.2 reduce-window.4
  56.8 83.2 %all-gather.6.cloned.1.call-done = bf16[16384,96]{1,0:T(8,128)(2,1)} async-done(((bf16[1024,96]{1,0:T(8,128)(2,1)}), bf16[16384,96]{1,0:T(8,128)(2,1)}) %all-gather.6.cloned.1.call-update) | async-done | bytes 3145744 | tf_op jit(solution)/shard_map/all_gather | solution.py:219
  140.0 4.1 %fusion.22 = f32[128,1024]{1,0:T(8,128)S(1)} fusion(bf16[16,1024,96]{2,1,0:T(8,128)(2,1)} %bitcast.123, f32[128,16,64]{0,2,1:T(8,128)S(1)} %bitcast.109, f32[16,64]{1,0:T(8,128)S(1)} %mul.196, f32[128]{0:T(128)S(1)} %add_rsqrt_fusion.1), kind=kOutput, calls=%fused_computation.30 | convolution fusion | flops 268828672 | bytes 4198912 | tf_op jit(solution)/shard_map/ngr,gcr->nc/dot_general | solution.py:298
  144.4 0.7 pad_maximum_fusion.3.x_ref
  145.1 50.9 %shard_map.123 = bf16[32,144,512]{2,1,0:T(8,128)(2,1)} custom-call(bf16[144,512]{1,0:T(8,128)(2,1)} %pad_maximum_fusion.3.x_ref), custom_call_target="tpu_custom_call" | custom-call | bytes 9437184 | tf_op jit(solution)/shard_map/pallas_call | solution.py:114
  196.0 4.7 %slice.77 = bf16[32,128,512]{2,1,0:T(8,128)(2,1)} slice(bf16[32,144,512]{2,1,0:T(8,128)(2,1)} %shard_map.123), slice={[0:32], [0:128], [0:512]} | slice | bytes 8388608 | tf_op jit(solution)/shard_map/slice | solution.py:325
  200.7 0.7 copy-done.5
  202.2 0.5 fusion.39
  202.7 1.0 fusion.12
  203.8 4.5 %fusion.69 = (bf16[4096,256]{1,0:T(8,128)(2,1)}, bf16[4096,256]{1,0:T(8,128)(2,1)}) fusion(bf16[4096,512]{1,0:T(8,128)(2,1)} %bitcast.88), kind=kLoop, calls=%fused_computation.112 | loop fusion | bytes 8388608 | tf_op jit(solution)/shard_map/slice | solution.py:246
  208.3 4.2 %copy.85 = bf16[4096,256]{0,1:T(8,128)(2,1)} copy(bf16[4096,256]{1,0:T(8,128)(2,1)} %get-tuple-element.7) | data formatting | bytes 4194304 | tf_op jit(solution)/shard_map/slice | solution.py:248
  212.6 0.2 copy.77
  212.8 0.2 copy.76
  213.0 4.1 %copy.83 = bf16[4096,256]{0,1:T(8,128)(2,1)} copy(bf16[4096,256]{1,0:T(8,128)(2,1)} %get-tuple-element.6) | data formatting | bytes 4194304 | tf_op jit(solution)/shard_map/slice | solution.py:246
  217.4 0.7 pad_maximum_fusion.1
  218.1 0.5 multiply_reduce_fusion
  218.6 5.5 %fusion = (f32[4,256]{1,0:T(4,128)S(1)}, f32[4,256,4096]{2,1,0:T(8,128)S(1)}) fusion(pred[256,4096]{1,0:T(8,128)(4,1)S(1)} %fusion.12, bf16[4,256,64]{2,1,0:T(8,128)(2,1)S(1)} %bitcast.97, bf16[4,4096,64]{1,2,0:T(8,128)(2,1)} %bitcast.89), kind=kOutput, calls=%fused_computation.2 | convolution fusion | flops 549452800 | bytes 20058112 | tf_op jit(solution)/shard_map/kqd,knd->kqn/dot_general | solution.py:251
  224.2 0.6 fusion.18
  224.7 4.4 %fusion.1 = f32[4,256]{1,0:T(4,128)S(1)} fusion(f32[4,256,4096]{2,1,0:T(8,128)S(1)} %get-tuple-element.22, f32[4,256]{1,0:T(4,128)S(1)} %get-tuple-element.15, pred[256,4096]{1,0:T(8,128)(4,1)S(1)} %fusion.12), kind=kLoop, calls=%fused_computation.3 | loop fusion | flops 16776192 | bytes 17833984 | tf_op jit(solution)/shard_map/reduce_sum | solution.py:260
  229.1 0.8 copy-done
  229.9 9.1 %fusion.3 = f32[4,256,64]{1,2,0:T(8,128)S(1)} fusion(bf16[4,4096,64]{1,2,0:T(8,128)(2,1)} %bitcast.101, f32[4,256,4096]{2,1,0:T(8,128)} %copy-done, f32[4,256]{1,0:T(4,128)S(1)} %get-tuple-element.15, pred[256,4096]{1,0:T(8,128)(4,1)S(1)} %fusion.12), kind=kOutput, calls=%fused_computation.5 | convolution fusion | flops 553648128 | bytes 20189184 | tf_op jit(solution)/shard_map/kqn,knd->kqd/dot_general | solution.py:261
  239.0 2.2 fusion.36
  241.2 0.2 copy.86
  241.5 4.5 %multiply_reduce_fusion.1 = (f32[128]{0:T(128)S(1)}, f32[128,1024]{1,0:T(8,128)S(1)}) fusion(bf16[128,16,32]{0,2,1:T(8,128)(2,1)S(1)} %bitcast.116, bf16[16,1024,96]{2,1,0:T(8,128)(2,1)} %bitcast.124, bf16[1,128,1024]{2,1,0:T(8,128)(2,1)S(1)} %copy-done.2), kind=kOutput, calls=%fused_computation.49 | convolution fusion | flops 134741888 | bytes 4063744 | tf_op jit(solution)/shard_map/ngr,gcr->nc/dot_general | solution.py:338
  246.1 2.7 convolution_convert_fusion
  248.8 38.8 %all_to_all.10 = bf16[16,80,1024]{2,1,0:T(8,128)(2,1)S(1)} all-to-all(bf16[16,80,1024]{2,1,0:T(8,128)(2,1)S(1)} %bitcast.100), channel_id=1, replica_groups=mesh['grp'=16,'tok'=32] {'grp'}, dimensions={0} | all-to-all | bytes 5242880 | tf_op jit(solution)/shard_map/all_to_all | solution.py:374
  287.7 0.3 copy.91
  288.0 1.8 slice.103
  289.7 2.6 slice.100
  292.4 0.3 copy.103
  292.6 0.7 copy.102
  293.4 2.9 fusion.71
  296.3 1.6 convolution_convert_fusion.1
  297.9 1.7 copy.94
  299.6 4.1 %all-to-all-start.1 = ((bf16[16,80,1024]{2,1,0:T(8,128)(2,1)}), bf16[16,80,1024]{2,1,0:T(8,128)(2,1)S(1)}, u32[]{:S(2)}, u32[]{:S(2)}) async-start(bf16[16,80,1024]{2,1,0:T(8,128)(2,1)} %bitcast.91), calls=%async_computation.1 | async-start | bytes 5242880 | tf_op jit(solution)/shard_map/all_to_all | solution.py:391
  303.9 3.0 fusion.7
  307.0 0.7 maximum_bitcast_fusion
  307.6 32.8 %all-to-all-done.1 = bf16[16,80,1024]{2,1,0:T(8,128)(2,1)S(1)} async-done(((bf16[16,80,1024]{2,1,0:T(8,128)(2,1)}), bf16[16,80,1024]{2,1,0:T(8,128)(2,1)S(1)}, u32[]{:S(2)}, u32[]{:S(2)}) %all-to-all-start.1) | async-done | bytes 2621472 | tf_op jit(solution)/shard_map/all_to_all | solution.py:391
  340.4 3.0 fusion.32
  (77 shorter events, 2.9 us)
Async XLA Ops:
  7.2 48.0 %copy-start.7 = (bf16[1,32,1024]{2,1,0:T(8,128)(2,1)S(1)}, bf16[1,32,1024]{2,1,0:T(8,128)(2,1)}, u32[]{:S(2)}) copy-start(bf16[1,32,1024]{2,1,0:T(8,128)(2,1)} %param.21) | copy-start | bytes 196612
  7.2 48.0 %copy-start.6 = (bf16[1,64,1024]{2,1,0:T(8,128)(2,1)S(1)}, bf16[1,64,1024]{2,1,0:T(8,128)(2,1)}, u32[]{:S(2)}) copy-start(bf16[1,64,1024]{2,1,0:T(8,128)(2,1)} %param.20) | copy-start | bytes 393220
  7.2 48.7 %copy-start.2 = (bf16[1,128,1024]{2,1,0:T(8,128)(2,1)S(1)}, bf16[1,128,1024]{2,1,0:T(8,128)(2,1)}, u32[]{:S(2)}) copy-start(bf16[1,128,1024]{2,1,0:T(8,128)(2,1)} %param.11) | copy-start | bytes 786436
  7.2 48.8 %copy-start.9 = (f32[1024]{0:T(1024)S(1)}, f32[1024]{0:T(1024)}, u32[]{:S(2)}) copy-start(f32[1024]{0:T(1024)} %param.16) | copy-start | bytes 12292
  7.2 48.9 %copy-start.13 = (s32[1,3]{1,0:T(1,128)S(1)}, s32[1,3]{1,0:T(1,128)}, u32[]{:S(2)}) copy-start(s32[1,3]{1,0:T(1,128)} %param.12) | copy-start | bytes 40
  7.2 132.8 %all-gather.6.cloned.1.call-start = ((), (), s32[]{:S(2)}) async-start(), calls=%async_computation.3 | async-start | bytes 4456448 | tf_op jit(solution)/shard_map/all_gather | solution.py:219
  55.1 232.9 %all-gather.4.cloned.1.call-start = ((), (), s32[]{:S(2)}) async-start(), calls=%async_computation.2 | async-start | bytes 6488064 | tf_op jit(solution)/shard_map/all_gather | solution.py:238
  55.2 145.5 %collective-permute-start = (bf16[96,1024]{1,0:T(8,128)(2,1)S(1)}, bf16[96,1024]{1,0:T(8,128)(2,1)S(1)}, u32[]{:S(2)}, u32[]{:S(2)}) collective-permute-start(bf16[96,1024]{1,0:T(8,128)(2,1)S(1)} %pad_maximum_fusion.2), channel_id=1, source_target_pairs={{0,0},{1,1},{2,32},{3,33},{4,64},{5,65},{6,96},{7,97},{8,128},{9,1... | collective-permute-start | bytes 589832 | tf_op jit(solution)/shard_map/ppermute | solution.py:231
  140.0 4.4 %copy-start.8 = (bf16[1,16,512]{2,1,0:T(8,128)(2,1)S(1)}, bf16[1,16,512]{2,1,0:T(8,128)(2,1)}, u32[]{:S(2)}) copy-start(bf16[1,16,512]{2,1,0:T(8,128)(2,1)} %param.13) | copy-start | bytes 49156
  144.1 59.6 %copy-start.3 = (f32[128,1024]{1,0:T(8,128)}, f32[128,1024]{1,0:T(8,128)S(1)}, u32[]{:S(2)}) copy-start(f32[128,1024]{1,0:T(8,128)S(1)} %fusion.22) | copy-start | bytes 1572868
  196.0 5.8 %copy-start.10 = (s32[1,128,8]{1,2,0:T(8,128)S(1)}, s32[1,128,8]{1,2,0:T(8,128)}, u32[]{:S(2)}) copy-start(s32[1,128,8]{1,2,0:T(8,128)} %param.14) | copy-start | bytes 12292
  200.7 0.7 copy-start.5
  208.3 4.2 %slice-start.1 = ((f32[128,1024]{1,0:T(8,128)}), f32[128,512]{1,0:T(8,128)S(1)}, s32[]{:S(2)}) async-start(f32[128,1024]{1,0:T(8,128)} %copy-done.3), calls=%async_computation.5 | async-start | bytes 524288 | tf_op jit(solution)/shard_map/slice | solution.py:304
  212.5 4.5 %slice-start = ((bf16[32,144,512]{2,1,0:T(8,128)(2,1)}), bf16[32,16,512]{2,1,0:T(8,128)(2,1)S(1)}, s32[]{:S(2)}) async-start(bf16[32,144,512]{2,1,0:T(8,128)(2,1)} %shard_map.123), calls=%async_computation.4 | async-start | bytes 1048576 | tf_op jit(solution)/shard_map/slice | solution.py:326
  218.6 5.5 %copy-start.1 = (f32[4,256,512]{2,1,0:T(8,128)}, f32[4,256,512]{2,1,0:T(8,128)S(1)}, u32[]{:S(2)}) copy-start(f32[4,256,512]{2,1,0:T(8,128)S(1)} %get-tuple-element.20) | copy-start | bytes 6291460
  224.1 5.8 %copy-start = (f32[4,256,4096]{2,1,0:T(8,128)}, f32[4,256,4096]{2,1,0:T(8,128)S(1)}, u32[]{:S(2)}) copy-start(f32[4,256,4096]{2,1,0:T(8,128)S(1)} %get-tuple-element.22) | copy-start | bytes 50331652
  241.5 4.6 %copy-start.12 = (f32[1024]{0:T(1024)S(1)}, f32[1024]{0:T(1024)}, u32[]{:S(2)}) copy-start(f32[1024]{0:T(1024)} %param.19) | copy-start | bytes 12292
  246.1 41.6 %copy-start.4 = (f32[128,1024]{1,0:T(8,128)}, f32[128,1024]{1,0:T(8,128)S(1)}, u32[]{:S(2)}) copy-start(f32[128,1024]{1,0:T(8,128)S(1)} %get-tuple-element.24) | copy-start | bytes 1572868
  299.6 4.1 %copy-start.11 = (f32[1,128,8]{1,2,0:T(8,128)S(1)}, f32[1,128,8]{1,2,0:T(8,128)}, u32[]{:S(2)}) copy-start(f32[1,128,8]{1,2,0:T(8,128)} %param.15) | copy-start | bytes 12292
  299.6 40.8 %all-to-all-start.1 = ((bf16[16,80,1024]{2,1,0:T(8,128)(2,1)}), bf16[16,80,1024]{2,1,0:T(8,128)(2,1)S(1)}, u32[]{:S(2)}, u32[]{:S(2)}) async-start(bf16[16,80,1024]{2,1,0:T(8,128)(2,1)} %bitcast.91), calls=%async_computation.1 | async-start | bytes 5242880 | tf_op jit(solution)/shard_map/all_to_all | solution.py:391
Sparse Core Ops, SparseCore 0:
  55.2 84.7 all-gather.5
  201.5 70.8 all-gather.3

commit v12 on v10

--- a/solution.py
+++ b/solution.py
@@ -149,7 +149,7 @@
     return lax.all_gather(by_columns[None], "grp", axis=0, tiled=True)
 
 
-def expert_weight_slices(gate_up, down):
+def expert_weight_slices(gate_up, down, after):
     grp_count = lax.axis_size("grp")
     tok_count = lax.axis_size("tok")
     per = tok_count // grp_count
@@ -158,6 +158,8 @@
         for e in range(tok_count):
             pairs.append((g * tok_count + e, (e // per) * tok_count + per * g + e % per))
     block = jnp.concatenate([gate_up[0], down[0]], axis=0)
+    probe = after.reshape(-1)[0]
+    block = jnp.where(probe != probe, jnp.zeros_like(block), block)
     return lax.ppermute(block, ("grp", "tok"), pairs)
 
 
@@ -224,7 +226,6 @@
     qkv_width = qkv_columns.shape[1]
     qkv_weight = packed_rows[:, :, :qkv_width]
     out_weight = packed_rows[:, :, qkv_width:]
-    expert_weights = expert_weight_slices(expert_gate_up, expert_down)
     projected = jnp.einsum(
         "ngr,gcr->nc",
         normed.reshape(tok_count, qkv_weight.shape[0], qkv_weight.shape[2]),
@@ -254,6 +255,7 @@
     both = ring_gather(jnp.concatenate([suffix_cache, prefix_cache[0]], axis=0), 0)
     piece = both[:, :tok_count].reshape(-1, both.shape[2])
     prefix_all = both[:, tok_count:].reshape(-1, both.shape[2])
+    expert_weights = expert_weight_slices(expert_gate_up, expert_down, both)
     carry = attend(start_carry, grouped, prefix_all, None)
     key_index = jnp.arange(piece.shape[0], dtype=jnp.int32)
     key_segment, key_offset = request_layout(group_lengths, key_index)

time: 344 us -> 376 us (1.093)
  blocking collectives: 38.5 us -> 82.2 us
  waiting for transfers between devices: 114 us -> 91.3 us
  local copies, waits for them, and re-layouts: 32.8 us -> 39.2 us
    all_to_all x1, blocking collectives: 38.5 us -> 82.2 us  [local(): lax.all_to_all(outgoing.reshape(grp_count, local_experts * CAP, model_wid...]
    all_gather x1, waiting for transfers between devices: 81 us -> 59.9 us  [gather_rows(): return lax.all_gather(by_columns[None], 'grp', axis=0, tiled=True)]
    unnamed x33 -> x38, local copies, waits for them, and re-layouts: 4 us -> 8.61 us
  transfers between devices with their start and end apart: 4 -> 4, of which waited for: 2 -> 2; matrix products, arithmetic and copies ran while one was open for 18% -> 16% of each run, Pallas kernels for 15% -> 0%
where the time goes in v12:
time: 376 us; the launch traced here: 374 us
  waiting for transfers between devices  91.3 us (24%)
  Pallas kernels  88.8 us (24%)
  blocking collectives  82.2 us (22%)
  matrix products  40.2 us (11%)
  local copies, waits for them, and re-layouts  39.2 us (10%)
  between operations  15.9 us (4%)
  other arithmetic  12.2 us (3%)
  starting transfers between devices  4.66 us (1%)
    pallas_call x2, Pallas kernels, ring_gather(): pl.pallas_call(kernel, out_shape=jax.ShapeDtypeStruct((tok_count, rows, w...  88.8 us
    all_to_all x1, blocking collectives, local(): lax.all_to_all(outgoing.reshape(grp_count, local_experts * CAP, model_wid...  82.2 us
    all_gather x1, waiting for transfers between devices, gather_rows(): return lax.all_gather(by_columns[None], 'grp', axis=0, tiled=True)  59.9 us
    all_to_all x1, waiting for transfers between devices, local(): lax.all_to_all(expert_result.reshape(grp_count, local_experts * CAP, mode...  31.4 us
    dot_general x2, matrix products, attend(): jnp.einsum('kqn,knd->kqd', probs.astype(jnp.bfloat16), value_heads, prefe...  12.9 us
    unnamed x38, local copies, waits for them, and re-layouts  8.61 us
    slice x3, local copies, waits for them, and re-layouts, attend(): keys_values[:, :key_width].reshape(key_count, KV_HEADS, HEAD_DIM)  8.2 us
  transfers between devices with their start and end apart: 4, of which 2 were waited for; matrix products, arithmetic and copies ran while one was open for 16% of the time, Pallas kernels for 0%

profile of v12, /device:TPU:1, one launch (start us, length us, event | category | flops | bytes accessed | tf_op | source)
XLA Modules:
  0.0 374.4 jit_solution(5215525037522667576)
XLA Ops:
  7.2 0.8 reshape.312
  8.0 0.8 copy.72
  8.9 0.6 reshape.314.x_ref
  9.6 37.6 %shard_map.122 = bf16[32,16,512]{2,1,0:T(8,128)(2,1)} custom-call(bf16[16,512]{1,0:T(8,128)(2,1)} %reshape.314.x_ref), custom_call_target="tpu_custom_call" | custom-call | bytes 1048576 | tf_op jit(solution)/shard_map/pallas_call | solution.py:114
  47.1 1.3 copy.104
  49.0 0.9 pad_maximum_fusion
  49.9 0.8 mul.196
  50.6 1.1 copy.71
  52.4 59.9 %all-gather.6.cloned.1.call-done = bf16[16384,96]{1,0:T(8,128)(2,1)} async-done(((bf16[1024,96]{1,0:T(8,128)(2,1)}), bf16[16384,96]{1,0:T(8,128)(2,1)}) %all-gather.6.cloned.1.call-update) | async-done | bytes 3145744 | tf_op jit(solution)/shard_map/all_gather | solution.py:149
  112.3 4.1 %fusion.22 = f32[128,1024]{1,0:T(8,128)S(1)} fusion(bf16[16,1024,96]{2,1,0:T(8,128)(2,1)} %bitcast.128, f32[128,16,64]{0,2,1:T(8,128)S(1)} %bitcast.114, f32[16,64]{1,0:T(8,128)S(1)} %mul.196, f32[128]{0:T(128)S(1)} %add_rsqrt_fusion.1), kind=kOutput, calls=%fused_computation.30 | convolution fusion | flops 268828672 | bytes 4198912 | tf_op jit(solution)/shard_map/ngr,gcr->nc/dot_general | solution.py:229
  116.7 0.7 pad_maximum_fusion.2.x_ref
  117.4 51.2 %shard_map.123 = bf16[32,144,512]{2,1,0:T(8,128)(2,1)} custom-call(bf16[144,512]{1,0:T(8,128)(2,1)} %pad_maximum_fusion.2.x_ref), custom_call_target="tpu_custom_call" | custom-call | bytes 9437184 | tf_op jit(solution)/shard_map/pallas_call | solution.py:114
  168.6 4.9 %copy.105 = bf16[576,4,8,128]{3,1,2,0:T(4,128)(2,1)S(1)} copy(bf16[576,4,8,128]{3,2,1,0:T(8,128)(2,1)} %bitcast.90) | data formatting | bytes 9437184
  175.4 0.9 collective-permute-start
  176.3 2.4 slice.80
  178.7 0.7 copy-done.7
  180.2 0.5 fusion.39
  180.7 0.6 add_select_fusion
  181.3 1.0 fusion.12
  182.4 1.1 slice.77
  183.8 0.9 copy.76
  184.7 0.9 copy.82
  185.6 0.8 copy.80
  186.4 4.4 %fusion.69 = (bf16[4096,256]{1,0:T(8,128)(2,1)}, bf16[4096,256]{1,0:T(8,128)(2,1)}) fusion(bf16[4096,512]{1,0:T(8,128)(2,1)} %bitcast.91), kind=kLoop, calls=%fused_computation.112 | loop fusion | bytes 8388608 | tf_op jit(solution)/shard_map/slice | solution.py:178
  190.9 2.9 copy.83
  193.8 4.1 %copy.85 = bf16[4096,256]{0,1:T(8,128)(2,1)} copy(bf16[4096,256]{1,0:T(8,128)(2,1)} %get-tuple-element.7) | data formatting | bytes 4194304 | tf_op jit(solution)/shard_map/slice | solution.py:180
  197.9 1.7 pad_maximum_fusion.1
  199.6 1.4 multiply_reduce_fusion
  201.1 3.5 fusion
  204.6 0.6 fusion.18
  205.2 4.6 %fusion.1 = f32[4,256]{1,0:T(4,128)S(1)} fusion(f32[4,256,4096]{2,1,0:T(8,128)S(1)} %get-tuple-element.22, f32[4,256]{1,0:T(4,128)S(1)} %get-tuple-element.15, pred[256,4096]{1,0:T(8,128)(4,1)S(1)} %fusion.12), kind=kLoop, calls=%fused_computation.3 | loop fusion | flops 16776192 | bytes 17833984 | tf_op jit(solution)/shard_map/reduce_sum | solution.py:192
  210.3 0.6 multiply_add_fusion
  210.9 11.3 %fusion.3 = f32[4,256,64]{1,2,0:T(8,128)} fusion(bf16[4,4096,64]{1,2,0:T(8,128)(2,1)} %bitcast.105, f32[4,256,4096]{2,1,0:T(8,128)} %copy-done, f32[4,256]{1,0:T(4,128)S(1)} %get-tuple-element.15, pred[256,4096]{1,0:T(8,128)(4,1)S(1)} %fusion.12), kind=kOutput, calls=%fused_computation.5 | convolution fusion | flops 553648128 | bytes 20189184 | tf_op jit(solution)/shard_map/kqn,knd->kqd/dot_general | solution.py:193
  222.3 1.6 fusion.36
  224.2 4.5 %multiply_reduce_fusion.1 = (f32[128]{0:T(128)S(1)}, f32[128,1024]{1,0:T(8,128)S(1)}) fusion(bf16[128,16,32]{0,2,1:T(8,128)(2,1)S(1)} %bitcast.120, bf16[16,1024,96]{2,1,0:T(8,128)(2,1)} %bitcast.129, bf16[1,128,1024]{2,1,0:T(8,128)(2,1)S(1)} %copy-done.5), kind=kOutput, calls=%fused_computation.49 | convolution fusion | flops 134741888 | bytes 4063744 | tf_op jit(solution)/shard_map/ngr,gcr->nc/dot_general | solution.py:270
  228.8 2.7 convolution_convert_fusion
  231.5 82.2 %all_to_all.10 = bf16[16,80,1024]{2,1,0:T(8,128)(2,1)S(1)} all-to-all(bf16[16,80,1024]{2,1,0:T(8,128)(2,1)S(1)} %bitcast.104), channel_id=1, replica_groups=mesh['grp'=16,'tok'=32] {'grp'}, dimensions={0} | all-to-all | bytes 5242880 | tf_op jit(solution)/shard_map/all_to_all | solution.py:306
  314.0 1.8 slice.108
  315.8 2.6 slice.105
  318.4 0.7 copy.102
  319.4 2.9 fusion.71
  322.3 1.6 convolution_convert_fusion.1
  323.9 1.7 copy.94
  325.6 3.7 all-to-all-start.1
  329.5 3.0 fusion.7
  332.6 0.7 maximum_bitcast_fusion
  333.2 31.4 %all-to-all-done.1 = bf16[16,80,1024]{2,1,0:T(8,128)(2,1)S(1)} async-done(((bf16[16,80,1024]{2,1,0:T(8,128)(2,1)}), bf16[16,80,1024]{2,1,0:T(8,128)(2,1)S(1)}, u32[]{:S(2)}, u32[]{:S(2)}) %all-to-all-start.1) | async-done | bytes 2621472 | tf_op jit(solution)/shard_map/all_to_all | solution.py:323
  364.6 3.0 fusion.32
  (81 shorter events, 4.8 us)
Async XLA Ops:
  7.2 45.0 %copy-start.4 = (bf16[1,128,1024]{2,1,0:T(8,128)(2,1)S(1)}, bf16[1,128,1024]{2,1,0:T(8,128)(2,1)}, u32[]{:S(2)}) copy-start(bf16[1,128,1024]{2,1,0:T(8,128)(2,1)} %param.11) | copy-start | bytes 786436
  7.2 44.6 %copy-start.15 = (s32[1,3]{1,0:T(1,128)S(1)}, s32[1,3]{1,0:T(1,128)}, u32[]{:S(2)}) copy-start(s32[1,3]{1,0:T(1,128)} %param.12) | copy-start | bytes 40
  7.2 105.1 %all-gather.6.cloned.1.call-start = ((), (), s32[]{:S(2)}) async-start(), calls=%async_computation.3 | async-start | bytes 4456448 | tf_op jit(solution)/shard_map/all_gather | solution.py:149
  49.8 264.2 %all-gather.4.cloned.1.call-start = ((), (), s32[]{:S(2)}) async-start(), calls=%async_computation.2 | async-start | bytes 6488064 | tf_op jit(solution)/shard_map/all_gather | solution.py:170
  50.6 66.1 %copy-start.10 = (bf16[1,16,512]{2,1,0:T(8,128)(2,1)S(1)}, bf16[1,16,512]{2,1,0:T(8,128)(2,1)}, u32[]{:S(2)}) copy-start(bf16[1,16,512]{2,1,0:T(8,128)(2,1)} %param.13) | copy-start | bytes 49156
  168.6 6.8 %copy-start.8 = (bf16[1,64,1024]{2,1,0:T(8,128)(2,1)S(1)}, bf16[1,64,1024]{2,1,0:T(8,128)(2,1)}, u32[]{:S(2)}) copy-start(bf16[1,64,1024]{2,1,0:T(8,128)(2,1)} %param.20) | copy-start | bytes 393220
  168.6 6.8 %copy-start.9 = (bf16[1,32,1024]{2,1,0:T(8,128)(2,1)S(1)}, bf16[1,32,1024]{2,1,0:T(8,128)(2,1)}, u32[]{:S(2)}) copy-start(bf16[1,32,1024]{2,1,0:T(8,128)(2,1)} %param.21) | copy-start | bytes 196612
  168.6 7.7 %copy-start.1 = (bf16[32,144,512]{2,1,0:T(8,128)(2,1)S(1)}, bf16[32,144,512]{2,1,0:T(8,128)(2,1)}, u32[]{:S(2)}) copy-start(bf16[32,144,512]{2,1,0:T(8,128)(2,1)} %shard_map.123) | copy-start | bytes 14155780
  175.4 4.5 %copy-start.11 = (s32[1,128,8]{1,2,0:T(8,128)S(1)}, s32[1,128,8]{1,2,0:T(8,128)}, u32[]{:S(2)}) copy-start(s32[1,128,8]{1,2,0:T(8,128)} %param.14) | copy-start | bytes 12292
  175.4 3.3 collective-permute-start
  178.7 0.7 copy-start.7
  201.1 3.6 copy-start.2
  204.6 5.7 %copy-start = (f32[4,256,4096]{2,1,0:T(8,128)}, f32[4,256,4096]{2,1,0:T(8,128)S(1)}, u32[]{:S(2)}) copy-start(f32[4,256,4096]{2,1,0:T(8,128)S(1)} %get-tuple-element.22) | copy-start | bytes 50331652
  210.9 11.3 %copy-start.3 = (f32[4,256,512]{2,1,0:T(8,128)S(1)}, f32[4,256,512]{2,1,0:T(8,128)}, u32[]{:S(2)}) copy-start(f32[4,256,512]{2,1,0:T(8,128)} %copy-done.2) | copy-start | bytes 6291460
  210.9 13.3 %copy-start.5 = (bf16[1,128,1024]{2,1,0:T(8,128)(2,1)S(1)}, bf16[1,128,1024]{2,1,0:T(8,128)(2,1)}, u32[]{:S(2)}) copy-start(bf16[1,128,1024]{2,1,0:T(8,128)(2,1)} %param.11) | copy-start | bytes 786436
  223.9 4.8 %copy-start.13 = (s32[1024]{0:T(1024)S(1)}, s32[1024]{0:T(1024)}, u32[]{:S(2)}) copy-start(s32[1024]{0:T(1024)} %get-tuple-element.26) | copy-start | bytes 12292
  223.9 4.8 %copy-start.14 = (f32[1024]{0:T(1024)S(1)}, f32[1024]{0:T(1024)}, u32[]{:S(2)}) copy-start(f32[1024]{0:T(1024)} %param.19) | copy-start | bytes 12292
  228.7 85.0 %copy-start.6 = (f32[128,1024]{1,0:T(8,128)}, f32[128,1024]{1,0:T(8,128)S(1)}, u32[]{:S(2)}) copy-start(f32[128,1024]{1,0:T(8,128)S(1)} %get-tuple-element.24) | copy-start | bytes 1572868
  323.8 5.5 %copy-start.12 = (f32[1,128,8]{1,2,0:T(8,128)S(1)}, f32[1,128,8]{1,2,0:T(8,128)}, u32[]{:S(2)}) copy-start(f32[1,128,8]{1,2,0:T(8,128)} %param.15) | copy-start | bytes 12292
  325.6 39.0 %all-to-all-start.1 = ((bf16[16,80,1024]{2,1,0:T(8,128)(2,1)}), bf16[16,80,1024]{2,1,0:T(8,128)(2,1)S(1)}, u32[]{:S(2)}, u32[]{:S(2)}) async-start(bf16[16,80,1024]{2,1,0:T(8,128)(2,1)} %bitcast.94), calls=%async_computation.1 | async-start | bytes 5242880 | tf_op jit(solution)/shard_map/all_to_all | solution.py:323
Sparse Core Ops, SparseCore 0:
  50.0 62.3 all-gather.5
  179.5 114.3 all-gather.3

commit v13 on v10

--- a/solution.py
+++ b/solution.py
@@ -299,7 +299,7 @@
     ).astype(jnp.bfloat16)
     grp_count = lax.axis_size("grp")
     local_experts = EXPERTS // grp_count
-    full = expert_weights_full(expert_weights, piece)
+    full = expert_weights_full(expert_weights, both)
     gate_rows = expert_gate_up.shape[1]
     arrived = lax.all_to_all(
         outgoing.reshape(grp_count, local_experts * CAP, model_width),

time: 344 us -> 339 us (0.985)
  local copies, waits for them, and re-layouts: 32.8 us -> 28.2 us
  transfers between devices with their start and end apart: 4 -> 4, of which waited for: 2 -> 2; matrix products, arithmetic and copies ran while one was open for 18% -> 16% of each run, Pallas kernels for 15% -> 15%
where the time goes in v13:
time: 339 us; the launch traced here: 338 us
  waiting for transfers between devices  114 us (34%)
  Pallas kernels  88.9 us (26%)
  matrix products  39.6 us (12%)
  blocking collectives  38.4 us (11%)
  local copies, waits for them, and re-layouts  28.2 us (8%)
  between operations  14.6 us (4%)
  other arithmetic  9.81 us (3%)
  starting transfers between devices  4.83 us (1%)
    pallas_call x2, Pallas kernels, ring_gather(): pl.pallas_call(kernel, out_shape=jax.ShapeDtypeStruct((tok_count, rows, w...  88.9 us
    all_gather x1, waiting for transfers between devices, gather_rows(): return lax.all_gather(by_columns[None], 'grp', axis=0, tiled=True)  81 us
    all_to_all x1, blocking collectives, local(): lax.all_to_all(outgoing.reshape(grp_count, local_experts * CAP, model_wid...  38.4 us
    all_to_all x1, waiting for transfers between devices, local(): lax.all_to_all(expert_result.reshape(grp_count, local_experts * CAP, mode...  33 us
    dot_general x2, matrix products, attend(): jnp.einsum('kqn,knd->kqd', probs.astype(jnp.bfloat16), value_heads, prefe...  11.3 us
  transfers between devices with their start and end apart: 4, of which 2 were waited for; matrix products, arithmetic and copies ran while one was open for 16% of the time, Pallas kernels for 15%

profile of v13, /device:TPU:1, one launch (start us, length us, event | category | flops | bytes accessed | tf_op | source)
XLA Modules:
  0.0 338.4 jit_solution(6700682766606272160)
XLA Ops:
  7.3 0.9 copy.72
  8.2 0.8 reshape.308
  9.0 0.6 reshape.310.x_ref
  9.7 37.6 %shard_map.122 = bf16[32,16,512]{2,1,0:T(8,128)(2,1)} custom-call(bf16[16,512]{1,0:T(8,128)(2,1)} %reshape.310.x_ref), custom_call_target="tpu_custom_call" | custom-call | bytes 1048576 | tf_op jit(solution)/shard_map/pallas_call | solution.py:114
  47.2 1.3 copy.104
  48.6 0.2 reshape.313
  48.8 0.2 reshape.312
  49.1 0.9 pad_maximum_fusion
  50.0 0.7 collective-permute-start
  50.9 0.2 reduce-window.4
  51.6 81.0 %all-gather.6.cloned.1.call-done = bf16[16384,96]{1,0:T(8,128)(2,1)} async-done(((bf16[1024,96]{1,0:T(8,128)(2,1)}), bf16[16384,96]{1,0:T(8,128)(2,1)}) %all-gather.6.cloned.1.call-update) | async-done | bytes 3145744 | tf_op jit(solution)/shard_map/all_gather | solution.py:149
  132.6 4.1 %fusion.22 = f32[128,1024]{1,0:T(8,128)S(1)} fusion(bf16[16,1024,96]{2,1,0:T(8,128)(2,1)} %bitcast.123, f32[128,16,64]{0,2,1:T(8,128)S(1)} %bitcast.109, f32[16,64]{1,0:T(8,128)S(1)} %mul.196, f32[128]{0:T(128)S(1)} %add_rsqrt_fusion.1), kind=kOutput, calls=%fused_computation.30 | convolution fusion | flops 268828672 | bytes 4198912 | tf_op jit(solution)/shard_map/ngr,gcr->nc/dot_general | solution.py:228
  137.0 0.7 pad_maximum_fusion.3.x_ref
  137.7 51.3 %shard_map.123 = bf16[32,144,512]{2,1,0:T(8,128)(2,1)} custom-call(bf16[144,512]{1,0:T(8,128)(2,1)} %pad_maximum_fusion.3.x_ref), custom_call_target="tpu_custom_call" | custom-call | bytes 9437184 | tf_op jit(solution)/shard_map/pallas_call | solution.py:114
  189.0 0.7 copy-done.5
  190.5 0.5 fusion.39
  191.1 1.0 fusion.12
  192.1 2.2 slice-done
  194.3 2.3 fusion.69
  196.6 4.2 %copy.85 = bf16[4096,256]{0,1:T(8,128)(2,1)} copy(bf16[4096,256]{1,0:T(8,128)(2,1)} %get-tuple-element.7) | data formatting | bytes 4194304 | tf_op jit(solution)/shard_map/slice | solution.py:178
  200.9 0.2 copy.77
  201.1 0.2 copy.76
  201.3 4.2 %copy.83 = bf16[4096,256]{0,1:T(8,128)(2,1)} copy(bf16[4096,256]{1,0:T(8,128)(2,1)} %get-tuple-element.6) | data formatting | bytes 4194304 | tf_op jit(solution)/shard_map/slice | solution.py:176
  205.8 0.7 pad_maximum_fusion.1
  206.5 0.5 multiply_reduce_fusion
  207.0 5.5 %fusion = (f32[4,256]{1,0:T(4,128)S(1)}, f32[4,256,4096]{2,1,0:T(8,128)S(1)}) fusion(pred[256,4096]{1,0:T(8,128)(4,1)S(1)} %fusion.12, bf16[4,256,64]{2,1,0:T(8,128)(2,1)S(1)} %bitcast.97, bf16[4,4096,64]{1,2,0:T(8,128)(2,1)} %bitcast.89), kind=kOutput, calls=%fused_computation.2 | convolution fusion | flops 549452800 | bytes 20058112 | tf_op jit(solution)/shard_map/kqd,knd->kqn/dot_general | solution.py:181
  212.6 0.6 fusion.18
  213.1 4.4 %fusion.1 = f32[4,256]{1,0:T(4,128)S(1)} fusion(f32[4,256,4096]{2,1,0:T(8,128)S(1)} %get-tuple-element.22, f32[4,256]{1,0:T(4,128)S(1)} %get-tuple-element.15, pred[256,4096]{1,0:T(8,128)(4,1)S(1)} %fusion.12), kind=kLoop, calls=%fused_computation.3 | loop fusion | flops 16776192 | bytes 17833984 | tf_op jit(solution)/shard_map/reduce_sum | solution.py:190
  217.6 0.7 copy-done
  218.3 9.0 %fusion.3 = f32[4,256,64]{1,2,0:T(8,128)S(1)} fusion(bf16[4,4096,64]{1,2,0:T(8,128)(2,1)} %bitcast.101, f32[4,256,4096]{2,1,0:T(8,128)} %copy-done, f32[4,256]{1,0:T(4,128)S(1)} %get-tuple-element.15, pred[256,4096]{1,0:T(8,128)(4,1)S(1)} %fusion.12), kind=kOutput, calls=%fused_computation.5 | convolution fusion | flops 553648128 | bytes 20189184 | tf_op jit(solution)/shard_map/kqn,knd->kqd/dot_general | solution.py:191
  227.4 2.2 fusion.36
  229.6 0.2 copy.86
  229.9 4.5 %multiply_reduce_fusion.1 = (f32[128]{0:T(128)S(1)}, f32[128,1024]{1,0:T(8,128)S(1)}) fusion(bf16[128,16,32]{0,2,1:T(8,128)(2,1)S(1)} %bitcast.116, bf16[16,1024,96]{2,1,0:T(8,128)(2,1)} %bitcast.124, bf16[1,128,1024]{2,1,0:T(8,128)(2,1)S(1)} %copy-done.2), kind=kOutput, calls=%fused_computation.49 | convolution fusion | flops 134741888 | bytes 4063744 | tf_op jit(solution)/shard_map/ngr,gcr->nc/dot_general | solution.py:268
  234.5 2.7 convolution_convert_fusion
  237.2 38.4 %all_to_all.10 = bf16[16,80,1024]{2,1,0:T(8,128)(2,1)S(1)} all-to-all(bf16[16,80,1024]{2,1,0:T(8,128)(2,1)S(1)} %bitcast.100), channel_id=1, replica_groups=mesh['grp'=16,'tok'=32] {'grp'}, dimensions={0} | all-to-all | bytes 5242880 | tf_op jit(solution)/shard_map/all_to_all | solution.py:304
  275.6 0.3 copy.91
  275.9 1.8 slice.103
  277.7 2.6 slice.100
  280.3 0.3 copy.103
  280.6 0.7 copy.102
  281.3 2.9 fusion.71
  284.2 1.6 convolution_convert_fusion.1
  285.8 1.8 copy.94
  287.6 4.1 %all-to-all-start.1 = ((bf16[16,80,1024]{2,1,0:T(8,128)(2,1)}), bf16[16,80,1024]{2,1,0:T(8,128)(2,1)S(1)}, u32[]{:S(2)}, u32[]{:S(2)}) async-start(bf16[16,80,1024]{2,1,0:T(8,128)(2,1)} %bitcast.91), calls=%async_computation.1 | async-start | bytes 5242880 | tf_op jit(solution)/shard_map/all_to_all | solution.py:321
  291.9 3.0 fusion.7
  294.9 0.7 maximum_bitcast_fusion
  295.5 33.0 %all-to-all-done.1 = bf16[16,80,1024]{2,1,0:T(8,128)(2,1)S(1)} async-done(((bf16[16,80,1024]{2,1,0:T(8,128)(2,1)}), bf16[16,80,1024]{2,1,0:T(8,128)(2,1)S(1)}, u32[]{:S(2)}, u32[]{:S(2)}) %all-to-all-start.1) | async-done | bytes 2621472 | tf_op jit(solution)/shard_map/all_to_all | solution.py:321
  328.6 3.0 fusion.32
  (78 shorter events, 2.9 us)
Async XLA Ops:
  7.2 42.8 %copy-start.7 = (bf16[1,32,1024]{2,1,0:T(8,128)(2,1)S(1)}, bf16[1,32,1024]{2,1,0:T(8,128)(2,1)}, u32[]{:S(2)}) copy-start(bf16[1,32,1024]{2,1,0:T(8,128)(2,1)} %param.21) | copy-start | bytes 196612
  7.2 42.8 %copy-start.6 = (bf16[1,64,1024]{2,1,0:T(8,128)(2,1)S(1)}, bf16[1,64,1024]{2,1,0:T(8,128)(2,1)}, u32[]{:S(2)}) copy-start(bf16[1,64,1024]{2,1,0:T(8,128)(2,1)} %param.20) | copy-start | bytes 393220
  7.2 43.5 %copy-start.2 = (bf16[1,128,1024]{2,1,0:T(8,128)(2,1)S(1)}, bf16[1,128,1024]{2,1,0:T(8,128)(2,1)}, u32[]{:S(2)}) copy-start(bf16[1,128,1024]{2,1,0:T(8,128)(2,1)} %param.11) | copy-start | bytes 786436
  7.2 43.7 %copy-start.9 = (f32[1024]{0:T(1024)S(1)}, f32[1024]{0:T(1024)}, u32[]{:S(2)}) copy-start(f32[1024]{0:T(1024)} %param.16) | copy-start | bytes 12292
  7.2 43.7 %copy-start.13 = (s32[1,3]{1,0:T(1,128)S(1)}, s32[1,3]{1,0:T(1,128)}, u32[]{:S(2)}) copy-start(s32[1,3]{1,0:T(1,128)} %param.12) | copy-start | bytes 40
  7.2 125.4 %all-gather.6.cloned.1.call-start = ((), (), s32[]{:S(2)}) async-start(), calls=%async_computation.3 | async-start | bytes 4456448 | tf_op jit(solution)/shard_map/all_gather | solution.py:149
  49.9 226.0 %all-gather.4.cloned.1.call-start = ((), (), s32[]{:S(2)}) async-start(), calls=%async_computation.2 | async-start | bytes 6488064 | tf_op jit(solution)/shard_map/all_gather | solution.py:168
  50.0 139.0 %collective-permute-start = (bf16[96,1024]{1,0:T(8,128)(2,1)S(1)}, bf16[96,1024]{1,0:T(8,128)(2,1)S(1)}, u32[]{:S(2)}, u32[]{:S(2)}) collective-permute-start(bf16[96,1024]{1,0:T(8,128)(2,1)S(1)} %pad_maximum_fusion.2), channel_id=1, source_target_pairs={{0,0},{1,1},{2,32},{3,33},{4,64},{5,65},{6,96},{7,97},{8,128},{9,1... | collective-permute-start | bytes 589832 | tf_op jit(solution)/shard_map/ppermute | solution.py:161
  132.6 4.4 %copy-start.8 = (bf16[1,16,512]{2,1,0:T(8,128)(2,1)S(1)}, bf16[1,16,512]{2,1,0:T(8,128)(2,1)}, u32[]{:S(2)}) copy-start(bf16[1,16,512]{2,1,0:T(8,128)(2,1)} %param.13) | copy-start | bytes 49156
  136.7 55.4 %copy-start.3 = (f32[128,1024]{1,0:T(8,128)}, f32[128,1024]{1,0:T(8,128)S(1)}, u32[]{:S(2)}) copy-start(f32[128,1024]{1,0:T(8,128)S(1)} %fusion.22) | copy-start | bytes 1572868
  137.7 52.5 %copy-start.10 = (s32[1,128,8]{1,2,0:T(8,128)S(1)}, s32[1,128,8]{1,2,0:T(8,128)}, u32[]{:S(2)}) copy-start(s32[1,128,8]{1,2,0:T(8,128)} %param.14) | copy-start | bytes 12292
  189.0 0.7 copy-start.5
  192.1 2.2 slice-start
  196.6 4.2 %slice-start.2 = ((f32[128,1024]{1,0:T(8,128)}), f32[128,512]{1,0:T(8,128)S(1)}, s32[]{:S(2)}) async-start(f32[128,1024]{1,0:T(8,128)} %copy-done.3), calls=%async_computation.6 | async-start | bytes 524288 | tf_op jit(solution)/shard_map/slice | solution.py:234
  200.9 4.6 %slice-start.1 = ((bf16[32,144,512]{2,1,0:T(8,128)(2,1)}), bf16[32,16,512]{2,1,0:T(8,128)(2,1)S(1)}, s32[]{:S(2)}) async-start(bf16[32,144,512]{2,1,0:T(8,128)(2,1)} %shard_map.123), calls=%async_computation.5 | async-start | bytes 1048576 | tf_op jit(solution)/shard_map/slice | solution.py:256
  207.0 5.5 %copy-start.1 = (f32[4,256,512]{2,1,0:T(8,128)}, f32[4,256,512]{2,1,0:T(8,128)S(1)}, u32[]{:S(2)}) copy-start(f32[4,256,512]{2,1,0:T(8,128)S(1)} %get-tuple-element.20) | copy-start | bytes 6291460
  212.5 5.8 %copy-start = (f32[4,256,4096]{2,1,0:T(8,128)}, f32[4,256,4096]{2,1,0:T(8,128)S(1)}, u32[]{:S(2)}) copy-start(f32[4,256,4096]{2,1,0:T(8,128)S(1)} %get-tuple-element.22) | copy-start | bytes 50331652
  229.9 4.6 %copy-start.12 = (f32[1024]{0:T(1024)S(1)}, f32[1024]{0:T(1024)}, u32[]{:S(2)}) copy-start(f32[1024]{0:T(1024)} %param.19) | copy-start | bytes 12292
  234.4 41.2 %copy-start.4 = (f32[128,1024]{1,0:T(8,128)}, f32[128,1024]{1,0:T(8,128)S(1)}, u32[]{:S(2)}) copy-start(f32[128,1024]{1,0:T(8,128)S(1)} %get-tuple-element.24) | copy-start | bytes 1572868
  287.6 4.1 %copy-start.11 = (f32[1,128,8]{1,2,0:T(8,128)S(1)}, f32[1,128,8]{1,2,0:T(8,128)}, u32[]{:S(2)}) copy-start(f32[1,128,8]{1,2,0:T(8,128)} %param.15) | copy-start | bytes 12292
  287.6 41.0 %all-to-all-start.1 = ((bf16[16,80,1024]{2,1,0:T(8,128)(2,1)}), bf16[16,80,1024]{2,1,0:T(8,128)(2,1)S(1)}, u32[]{:S(2)}, u32[]{:S(2)}) async-start(bf16[16,80,1024]{2,1,0:T(8,128)(2,1)} %bitcast.91), calls=%async_computation.1 | async-start | bytes 5242880 | tf_op jit(solution)/shard_map/all_to_all | solution.py:321
Sparse Core Ops, SparseCore 0:
  50.1 82.4 all-gather.5
  189.8 70.5 all-gather.3
